TPU v7x, 32 devices: a whole 2x2x4 slice. The times are simulated.
32 devices in a mesh: rows: 16 (over z, y, x), seq: 2 (over core).
Axes of the slice: x: 2, y: 2, z: 4, core: 2. Of those that a mesh axis runs over, the one named last changes fastest.
Arguments:
- tokens: bfloat16 [16, 1024, 1024], P('rows', 'seq'), may hold values from -6 to 6
- noise_levels: float32 [16, 16], P('rows', 'seq'), may hold values from 0 to 1000
- frame_clip: int32 [16, 16], P('rows'), may hold values from 0 to 3, as said below
- w_qkv: bfloat16 [1024, 3, 1024], P('rows', None, 'seq'), may hold values from -0.1875 to 0.1875
- w_out: bfloat16 [1024, 1024], P('seq', 'rows'), may hold values from -1.5 to 1.5
- w_up: bfloat16 [1024, 4096], P('rows', 'seq'), may hold values from -0.1875 to 0.1875
- w_down: bfloat16 [4096, 1024], P('seq', 'rows'), may hold values from -0.09375 to 0.09375
- w_mod: bfloat16 [1024, 6144], P(None, 'seq'), may hold values from -0.1875 to 0.1875
- b_mod: bfloat16 [6144], P('seq'), may hold values from -4 to 4
- cotangent: bfloat16 [16, 1024, 1024], P('rows', 'seq'), may hold values from -6 to 6
Outputs:
- output: bfloat16 [16, 1024, 1024], P('rows', 'seq')
- grad_tokens: bfloat16 [16, 1024, 1024], P('rows', 'seq')
- grad_qkv: float32 [1024, 3, 1024], P('rows', None, 'seq')
- grad_out: float32 [1024, 1024], P('seq', 'rows')
- grad_up: float32 [1024, 4096], P('rows', 'seq')
- grad_down: float32 [4096, 1024], P('seq', 'rows')
- grad_mod: float32 [1024, 6144], P(None, 'seq')
- grad_bias: float32 [6144], P('seq')
Inputs may be any that keep to these rules, and one draw needn't show every extreme that they name: `frame_clip`: in each row the clip numbers start at 0 and rise by one from clip to clip; a run of equal numbers is one clip of 4 to 16 frames, except that the frames after the row's last whole clip (padding, fewer than 16) carry the next number.
All inputs are finite; a program needn't handle non-finite values.
Results may differ from a plain program's by a relative error of at most 0.015.
Values may be sent and summed in bfloat16 or wider, within the bound.
No kernel may reach another device: no remote copies, remote signals or barrier semaphores. Data moves between devices by JAX's collectives and lax.ppermute only.
A program may use at most 320 MiB of HBM per device.

v0:
```python
import math

import jax
import jax.numpy as jnp
from jax import lax
from jax.experimental import pallas as pl
from jax.experimental.pallas import tpu as pltpu
from jax.sharding import PartitionSpec as P

D = 1024
HEAD = 64
FRAME = 64
PAIR = 2 * HEAD
QB = 256

norm_eps = 1e-06
hidden_score = -1e30


f32 = jnp.float32
bf16 = jnp.bfloat16


def noise_features(levels):
    half_width = D // 2
    frequency = jnp.exp(
        -math.log(10000.0) * jnp.arange(half_width).astype(jnp.float32) / half_width
    )
    angles = levels[..., None] * frequency
    return jax.nn.silu(jnp.concatenate([jnp.cos(angles), jnp.sin(angles)], axis=-1))


def normalize(values):
    centered = values - jnp.mean(values, axis=-1, keepdims=True)
    return centered * lax.rsqrt(jnp.mean(centered * centered, axis=-1, keepdims=True) + norm_eps)


def modulated(values, offsets, factors):
    return normalize(values) * (1.0 + factors) + offsets


def gelu_tanh(values):
    return jax.nn.gelu(values, approximate=True)


def grid_of(count):
    deep = 4
    side = math.isqrt(count // deep)
    return (deep, side, side)


def shift_pairs(grid, axis, amount):
    pairs = []
    for z in range(grid[0]):
        for y in range(grid[1]):
            for x in range(grid[2]):
                to = [z, y, x]
                to[axis] = (to[axis] + amount) % grid[axis]
                pairs.append(
                    (
                        (z * grid[1] + y) * grid[2] + x,
                        (to[0] * grid[1] + to[1]) * grid[2] + to[2],
                    )
                )
    return pairs


def place_on(grid):
    me = lax.axis_index("rows")
    return (me // (grid[1] * grid[2]), (me // grid[2]) % grid[1], me % grid[2])


def gather_axis(part, grid, axis, at, dim):
    count = grid[axis]
    whole = jnp.zeros(part.shape[:dim] + (count,) + part.shape[dim:], part.dtype)
    pieces = [part] + [
        lax.ppermute(part, "rows", shift_pairs(grid, axis, k)) for k in range(1, count)
    ]
    for k, piece in enumerate(pieces):
        whole = lax.dynamic_update_index_in_dim(whole, piece, (at[axis] - k) % count, dim)
    return whole


def gather_deep(shard, grid, at):
    return gather_axis(shard, grid, 0, at, 0)


def gather_rest(deep, grid, at):
    cut = deep.shape[-1] // 2
    first = gather_axis(deep[..., :cut], grid, 2, at, 1)
    first = gather_axis(first, grid, 1, at, 1)
    second = gather_axis(deep[..., cut:], grid, 1, at, 1)
    second = gather_axis(second, grid, 2, at, 2)
    whole = jnp.concatenate([first, second], axis=-1)
    return whole.reshape(-1, whole.shape[-1])


def pieces_of(whole, grid, axis, at, dim):
    return [
        lax.dynamic_index_in_dim(whole, (at[axis] + k) % grid[axis], dim, keepdims=False)
        for k in range(grid[axis])
    ]


def sum_pieces(pieces, grid, axis):
    total = pieces[0].astype(f32)
    for k in range(1, grid[axis]):
        total = total + lax.ppermute(pieces[k], "rows", shift_pairs(grid, axis, k)).astype(f32)
    return total


def scatter_axis(whole, grid, axis, at, dim):
    return sum_pieces(pieces_of(whole, grid, axis, at, dim), grid, axis)


def scatter_cut(whole, grid, at):
    cols = whole.shape[-1]
    cut = cols // 2
    view = whole.reshape(*grid, -1, cols)
    return (
        pieces_of(view[..., :cut], grid, 1, at, 1),
        pieces_of(view[..., cut:], grid, 2, at, 2),
    )


def scatter_rows(cuts, grid, at):
    first = sum_pieces(cuts[0], grid, 1).astype(bf16)
    second = sum_pieces(cuts[1], grid, 2).astype(bf16)
    first = scatter_axis(first, grid, 2, at, 1).astype(bf16)
    second = scatter_axis(second, grid, 1, at, 1).astype(bf16)
    return scatter_axis(jnp.concatenate([first, second], axis=-1), grid, 0, at, 0)


def swapped(part):
    return lax.ppermute(part, "seq", [(0, 1), (1, 0)])


def in_order(own, other, side):
    whole = jnp.zeros((2 * own.shape[0],) + own.shape[1:], own.dtype)
    half = own.shape[0]
    whole = lax.dynamic_update_slice_in_dim(whole, own, side * half, 0)
    return lax.dynamic_update_slice_in_dim(whole, other, (1 - side) * half, 0)


def half_of(whole, which):
    half = whole.shape[0] // 2
    return lax.dynamic_slice_in_dim(whole, which * half, half, 0)


def nt(a, b):
    return lax.dot_general(a, b, (((1,), (1,)), ((), ())), preferred_element_type=f32)


def nn(a, b):
    return lax.dot_general(a, b, (((1,), (0,)), ((), ())), preferred_element_type=f32)


def lane_in(shape, head):
    lanes = lax.broadcasted_iota(jnp.int32, shape, 1)
    return (lanes // HEAD) == head


def forward_kernel(qkv_ref, seen_ref, frame_ref, out_ref, log_ref):
    length = qkv_ref.shape[0]
    queries = qkv_ref[:, 0:PAIR] * jnp.asarray(HEAD**-0.5, bf16)
    keys = qkv_ref[:, PAIR : 2 * PAIR]
    values_t = qkv_ref[:, 2 * PAIR : 3 * PAIR].T
    seen = seen_ref[...]
    frames = frame_ref[...]
    own = [lane_in((length, PAIR), head) for head in range(2)]
    query_h = [jnp.where(own[head], queries, seen) for head in range(2)]
    key_h = [jnp.where(own[head], keys, frames) for head in range(2)]
    for start in range(0, length, QB):
        stop = start + QB
        parts = []
        for head in range(2):
            scores = nt(key_h[head][:stop], query_h[head][start:stop])
            largest = jnp.max(scores, axis=0, keepdims=True)
            exponent = jnp.exp(scores - largest)
            denominator = jnp.sum(exponent, axis=0, keepdims=True)
            combined = nn(values_t[head * HEAD : (head + 1) * HEAD, :stop], exponent.astype(bf16))
            parts.append(combined / denominator)
            log_ref[0, head : head + 1, start:stop] = largest + jnp.log(denominator)
        out_ref[start:stop, :] = jnp.concatenate(parts, axis=0).T.astype(bf16)


def backward_kernel(qkv_ref, seen_ref, frame_ref, log_ref, grad_ref, out_ref, key_sum, value_sum):
    length = qkv_ref.shape[0]
    queries = qkv_ref[:, 0:PAIR] * jnp.asarray(HEAD**-0.5, bf16)
    keys = qkv_ref[:, PAIR : 2 * PAIR]
    values = qkv_ref[:, 2 * PAIR : 3 * PAIR]
    grads = grad_ref[...]
    keys_t = keys.T
    seen = seen_ref[...]
    frames = frame_ref[...]
    nothing = jnp.zeros((length, PAIR), bf16)
    own = [lane_in((length, PAIR), head) for head in range(2)]
    query_h = [jnp.where(own[head], queries, seen) for head in range(2)]
    query_only = [jnp.where(own[head], queries, nothing) for head in range(2)]
    key_h = [jnp.where(own[head], keys, frames) for head in range(2)]
    grad_h = [jnp.where(own[head], grads, nothing) for head in range(2)]
    for start in reversed(range(0, length, QB)):
        stop = start + QB
        query_parts = []
        for head in range(2):
            grad_block = grad_h[head][start:stop]
            scores = nt(key_h[head][:stop], query_h[head][start:stop])
            chance = jnp.exp(scores - log_ref[0, head : head + 1, start:stop])
            grad_chance = nt(values[:stop], grad_block)
            product = chance * grad_chance
            grad_scores = product - chance * jnp.sum(product, axis=0, keepdims=True)
            grad_scores = grad_scores.astype(bf16)
            value_part = nn(chance.astype(bf16), grad_block)
            key_part = nn(grad_scores, query_only[head][start:stop])
            if stop == length and head == 0:
                value_sum[...] = value_part
                key_sum[...] = key_part
            else:
                value_sum[:stop, :] += value_part
                key_sum[:stop, :] += key_part
            query_parts.append(nn(keys_t[head * HEAD : (head + 1) * HEAD, :stop], grad_scores))
        query_grad = jnp.concatenate(query_parts, axis=0).T * HEAD**-0.5
        out_ref[start:stop, 0:PAIR] = query_grad.astype(bf16)
    out_ref[:, PAIR : 2 * PAIR] = key_sum[...].astype(bf16)
    out_ref[:, 2 * PAIR : 3 * PAIR] = value_sum[...].astype(bf16)


def attend(qkv, seen, frames):
    length, cols = qkv.shape
    pairs = cols // (3 * PAIR)
    whole = pl.BlockSpec((length, PAIR), lambda p: (0, 0))
    return pl.pallas_call(
        forward_kernel,
        grid=(pairs,),
        in_specs=[pl.BlockSpec((length, 3 * PAIR), lambda p: (0, p)), whole, whole],
        out_specs=[
            pl.BlockSpec((length, PAIR), lambda p: (0, p)),
            pl.BlockSpec((1, 2, length), lambda p: (p, 0, 0)),
        ],
        out_shape=[
            jax.ShapeDtypeStruct((length, pairs * PAIR), bf16),
            jax.ShapeDtypeStruct((pairs, 2, length), f32),
        ],
        cost_estimate=pl.CostEstimate(
            flops=8 * pairs * length * length * HEAD,
            bytes_accessed=8 * pairs * length * PAIR,
            transcendentals=2 * pairs * length * length,
        ),
        name="attend",
    )(qkv, seen, frames)


def attend_back(qkv, seen, frames, logs, grads):
    length, cols = qkv.shape
    pairs = cols // (3 * PAIR)
    whole = pl.BlockSpec((length, PAIR), lambda p: (0, 0))
    return pl.pallas_call(
        backward_kernel,
        grid=(pairs,),
        in_specs=[
            pl.BlockSpec((length, 3 * PAIR), lambda p: (0, p)),
            whole,
            whole,
            pl.BlockSpec((1, 2, length), lambda p: (p, 0, 0)),
            pl.BlockSpec((length, PAIR), lambda p: (0, p)),
        ],
        out_specs=pl.BlockSpec((length, 3 * PAIR), lambda p: (0, p)),
        out_shape=jax.ShapeDtypeStruct((length, pairs * 3 * PAIR), bf16),
        scratch_shapes=[pltpu.VMEM((length, PAIR), f32), pltpu.VMEM((length, PAIR), f32)],
        cost_estimate=pl.CostEstimate(
            flops=20 * pairs * length * length * HEAD,
            bytes_accessed=14 * pairs * length * PAIR,
            transcendentals=2 * pairs * length * length,
        ),
        name="attend_back",
    )(qkv, seen, frames, logs, grads)


def frame_lanes(per_frame):
    frames = per_frame.shape[0]
    padded = jnp.pad(per_frame.astype(bf16), ((0, 0), (0, HEAD - frames)))
    return jnp.repeat(jnp.concatenate([padded, padded], axis=1), FRAME, axis=0)


def block(tokens, noise_levels, frame_clip, w_qkv, w_out, w_up, w_down, w_mod, b_mod, cotangent):
    _, local_len, width = tokens.shape
    frames_here = noise_levels.shape[1]
    grid = grid_of(lax.axis_size("rows"))
    at = place_on(grid)
    side = lax.axis_index("seq")
    share = w_qkv.shape[0]
    head_cols = w_qkv.shape[2]
    pairs = head_cols // PAIR

    qkv_share = (
        w_qkv.reshape(share, 3, pairs, PAIR).transpose(0, 2, 1, 3).reshape(share, 3 * head_cols)
    )
    levels = in_order(noise_levels[0], swapped(noise_levels[0]), side)
    condition = noise_features(levels).astype(bf16)
    condition_cols = condition.size // share
    rest_share = jnp.concatenate(
        [w_out.T, condition.reshape(share, condition_cols), w_up], axis=1
    )
    down_share = w_down.T
    qkv_deep = gather_deep(qkv_share, grid, at)
    rest_share, down_share, qkv_deep = lax.optimization_barrier(
        (rest_share, down_share, qkv_deep)
    )
    qkv_whole = gather_rest(qkv_deep, grid, at)
    down_whole = lax.all_gather(down_share, "rows", axis=0, tiled=True)
    rest_whole = gather_rest(gather_deep(rest_share, grid, at), grid, at)
    out_whole = rest_whole[:, :head_cols]
    up_whole = rest_whole[:, head_cols + condition_cols :]
    condition_all = rest_whole[:, head_cols : head_cols + condition_cols].reshape(-1, width)

    mod_cols = jnp.dot(condition, w_mod, preferred_element_type=f32) + b_mod.astype(f32)
    own_cols = half_of(mod_cols, side)
    other_cols = swapped(half_of(mod_cols, 1 - side))
    modulation = in_order(
        own_cols.reshape(frames_here, 3, width).transpose(1, 0, 2),
        other_cols.reshape(frames_here, 3, width).transpose(1, 0, 2),
        side,
    )[:, :, None]
    shift_attn, scale_attn, gate_attn, shift_mlp, scale_mlp, gate_mlp = [
        modulation[k] for k in range(6)
    ]

    framed = tokens[0].astype(f32).reshape(frames_here, FRAME, width)
    upstream = cotangent[0].astype(f32).reshape(frames_here, FRAME, width)
    first_own = modulated(framed, shift_attn, scale_attn).astype(bf16).reshape(local_len, width)
    first_full = in_order(first_own, swapped(first_own), side)
    grad_mlp = (gate_mlp * upstream).astype(bf16).reshape(local_len, width)
    grad_mlp_full = jnp.concatenate([grad_mlp, swapped(grad_mlp)], axis=0)

    clip = frame_clip[0]
    order = jnp.arange(clip.shape[0])
    visible = (clip[:, None] == clip[None, :]) & (order[None, :] <= order[:, None])
    seen = frame_lanes(jnp.where(visible, 0.0, hidden_score))
    frames = frame_lanes(jnp.eye(clip.shape[0]))

    qkv = jnp.dot(first_full, qkv_whole, preferred_element_type=f32).astype(bf16)
    attended, logs = attend(qkv, seen, frames)
    branch_other = swapped(nt(half_of(attended, 1 - side), out_whole).astype(bf16))
    branch = nt(half_of(attended, side), out_whole) + branch_other.astype(f32)
    branch = branch.reshape(framed.shape)
    middle = framed + gate_attn * branch
    second_own = modulated(middle, shift_mlp, scale_mlp).astype(bf16).reshape(local_len, width)
    second_full = jnp.concatenate([second_own, swapped(second_own)], axis=0)
    hidden_pre = jnp.dot(second_full, up_whole, preferred_element_type=f32)
    hidden = gelu_tanh(hidden_pre).astype(bf16)
    mlp_other = swapped(nt(hidden[local_len:], down_whole).astype(bf16))
    mlp_out = (nt(hidden[:local_len], down_whole) + mlp_other.astype(f32)).reshape(framed.shape)
    output = (middle + gate_mlp * mlp_out).astype(bf16).reshape(tokens.shape)
    grad_gate_mlp = jnp.sum(upstream * mlp_out, axis=1)

    def tn(a, b):
        return lax.dot_general(a, b, (((0,), (0,)), ((), ())), preferred_element_type=f32)

    down_sum = lax.psum_scatter(
        tn(grad_mlp_full, hidden).astype(bf16), "rows", scatter_dimension=0, tiled=True
    ).astype(f32)
    grad_hidden = jnp.dot(grad_mlp_full, down_whole, preferred_element_type=f32)
    grad_pre = jax.vjp(gelu_tanh, hidden_pre)[1](grad_hidden)[0].astype(bf16)
    second_other = swapped(nt(grad_pre[local_len:], up_whole).astype(bf16))
    grad_second = nt(grad_pre[:local_len], up_whole) + second_other.astype(f32)
    up_cuts = scatter_cut(tn(second_full, grad_pre).astype(bf16), grid, at)
    second_back = jax.vjp(modulated, middle, shift_mlp, scale_mlp)[1]
    grad_middle, grad_shift_mlp, grad_scale_mlp = second_back(grad_second.reshape(framed.shape))
    grad_middle = grad_middle + upstream
    grad_gate_attn = jnp.sum(grad_middle * branch, axis=1)
    grad_branch = (gate_attn * grad_middle).astype(bf16).reshape(local_len, width)
    branch_full = in_order(grad_branch, swapped(grad_branch), side)
    grad_out = tn(branch_full, attended).astype(bf16)
    grad_attended = jnp.dot(branch_full, out_whole, preferred_element_type=f32).astype(bf16)
    grad_attended, up_cuts = lax.optimization_barrier((grad_attended, up_cuts))
    up_sum = scatter_rows(up_cuts, grid, at)
    grad_qkv = attend_back(qkv, seen, frames, logs, grad_attended)
    grad_tail = jnp.concatenate([tn(first_full, grad_qkv).astype(bf16), grad_out], axis=1)
    tail_sum = scatter_rows(scatter_cut(grad_tail, grid, at), grid, at)
    qkv_sum, out_sum = tail_sum[:, : 3 * head_cols], tail_sum[:, 3 * head_cols :]
    first_other = swapped(nt(half_of(grad_qkv, 1 - side), qkv_whole).astype(bf16))
    grad_first = nt(half_of(grad_qkv, side), qkv_whole) + first_other.astype(f32)
    first_back = jax.vjp(modulated, framed, shift_attn, scale_attn)[1]
    grad_framed, grad_shift_attn, grad_scale_attn = first_back(grad_first.reshape(framed.shape))
    grad_tokens = (grad_framed + grad_middle).astype(bf16).reshape(tokens.shape)

    low = jnp.concatenate([grad_shift_attn, grad_scale_attn, grad_gate_attn[:, None]], axis=-1)
    high = jnp.concatenate([grad_shift_mlp, grad_scale_mlp, grad_gate_mlp[:, None]], axis=-1)
    low, high = low.reshape(frames_here, -1), high.reshape(frames_here, -1)
    keep = jnp.where(side == 0, low, high).astype(bf16)
    give = jnp.where(side == 0, high, low).astype(bf16)
    mine = in_order(keep, swapped(give), side)
    grad_mods = lax.all_gather(mine, "rows", axis=0, tiled=True)
    mod_sum = tn(condition_all, grad_mods)
    bias_sum = jnp.sum(grad_mods.astype(f32), axis=0)

    qkv_sum = qkv_sum.reshape(share, pairs, 3, PAIR).transpose(0, 2, 1, 3).reshape(w_qkv.shape)
    return (output, grad_tokens, qkv_sum, out_sum.T, up_sum, down_sum.T, mod_sum, bias_sum)


def solution(mesh):
    in_specs = (
        P("rows", "seq", None),
        P("rows", "seq"),
        P("rows", None),
        P("rows", None, "seq"),
        P("seq", "rows"),
        P("rows", "seq"),
        P("seq", "rows"),
        P(None, "seq"),
        P("seq"),
        P("rows", "seq", None),
    )
    out_specs = (
        P("rows", "seq", None),
        P("rows", "seq", None),
        P("rows", None, "seq"),
        P("seq", "rows"),
        P("rows", "seq"),
        P("seq", "rows"),
        P(None, "seq"),
        P("seq"),
    )
    return jax.shard_map(block, mesh=mesh, in_specs=in_specs, out_specs=out_specs, check_vma=False)
```

profile of v0, /device:TPU:10, one launch (start us, length us, event | category | flops | bytes accessed | tf_op | source)
XLA Modules:
  0.0 441.0 jit_solution(5386651105852957218)
XLA Ops:
  15.4 3.8 convolution_add_fusion
  24.0 3.1 collective-permute-done.4
  30.7 1.9 collective-permute-start.12
  35.7 4.9 %collective-permute-done.10 = bf16[64,2816]{1,0:T(8,128)(2,1)} collective-permute-done((bf16[64,2816]{1,0:T(8,128)(2,1)}, bf16[64,2816]{1,0:T(8,128)(2,1)}, u32[]{:S(2)}, u32[]{:S(2)}) %collective-permute-start.10) | collective-permute-done | bytes 360480 | tf_op jit(solution)/shard_map/ppermute | solution.py:77
  43.1 23.1 %collective-permute-done.11 = bf16[64,2816]{1,0:T(8,128)(2,1)} collective-permute-done((bf16[64,2816]{1,0:T(8,128)(2,1)}, bf16[64,2816]{1,0:T(8,128)(2,1)}, u32[]{:S(2)}, u32[]{:S(2)}) %collective-permute-start.11) | collective-permute-done | bytes 360480 | tf_op jit(solution)/shard_map/ppermute | solution.py:77
  81.1 14.1 %collective-permute-done.13 = bf16[4,64,1408]{2,1,0:T(8,128)(2,1)S(1)} collective-permute-done((bf16[4,64,1408]{2,1,0:T(8,128)(2,1)S(1)}, bf16[4,64,1408]{2,1,0:T(8,128)(2,1)S(1)}, u32[]{:S(2)}, u32[]{:S(2)}) %collective-permute-start.13) | collective-permute-done | bytes 720928 | tf_op jit(solution)/shard_map/ppermute | solution.py:77
  97.9 2.0 bitcast_dynamic-update-slice_fusion.2
  103.9 14.5 %collective-permute-done.7 = bf16[4,2,64,768]{3,2,1,0:T(8,128)(2,1)S(1)} collective-permute-done((bf16[4,2,64,768]{3,2,1,0:T(8,128)(2,1)S(1)}, bf16[4,2,64,768]{3,2,1,0:T(8,128)(2,1)S(1)}, u32[]{:S(2)}, u32[]{:S(2)}) %collective-permute-start.7) | collective-permute-done | bytes 786464 | tf_op jit(solution)/shard_map/ppermute | solution.py:77
  118.5 6.2 %collective-permute-done.9 = bf16[4,2,64,768]{3,2,1,0:T(8,128)(2,1)S(1)} collective-permute-done((bf16[4,2,64,768]{3,2,1,0:T(8,128)(2,1)S(1)}, bf16[4,2,64,768]{3,2,1,0:T(8,128)(2,1)S(1)}, u32[]{:S(2)}, u32[]{:S(2)}) %collective-permute-start.9) | collective-permute-done | bytes 786464 | tf_op jit(solution)/shard_map/ppermute | solution.py:77
  125.0 4.8 %convolution_convert_fusion.1.qkv_ref = bf16[1024,1536]{1,0:T(8,128)(2,1)} fusion(bf16[1024,1024]{1,0:T(8,128)(2,1)S(1)} %constant_dynamic-update-slice_fusion.4, bf16[1024,1536]{1,0:T(8,128)(2,1)S(1)} %bitcast.318), kind=kOutput, calls=%fused_computation.13 | convolution fusion | flops 3222798336 | bytes 8388608 | tf_op jit(solution)/shard_map/dot_general | solution.py:341
  131.3 18.7 %attend.1 = (bf16[1024,512]{1,0:T(8,128)(2,1)}, f32[4,2,1024]{2,1,0:T(2,128)}) custom-call(bf16[1024,1536]{1,0:T(8,128)(2,1)} %convolution_convert_fusion.1.qkv_ref, bf16[1024,128]{1,0:T(8,128)(2,1)} %bitcast.329, bf16[1024,128]{1,0:T(8,128)(2,1)} %bitcast.331), custom_call_target="tpu_custom_call" | custom-call | flops 2147483648 | bytes 4194304 | tf_op jit(solution)/shard_map/attend/pallas_call | solution.py:232
  150.1 4.6 %collective-permute-done.14 = bf16[4,2,64,1408]{3,2,1,0:T(8,128)(2,1)S(1)} collective-permute-done((bf16[4,2,64,1408]{3,2,1,0:T(8,128)(2,1)}, bf16[4,2,64,1408]{3,2,1,0:T(8,128)(2,1)S(1)}, u32[]{:S(2)}, u32[]{:S(2)}) %collective-permute-start.14) | collective-permute-done | bytes 1441824 | tf_op jit(solution)/shard_map/ppermute | solution.py:77
  161.3 2.6 collective-permute-done.17
  163.9 2.3 bitcast_add_fusion.2
  169.9 2.5 fusion.26
  172.7 1.9 slice.112
  174.6 2.2 reshape.378
  176.9 11.9 %multiply_convert_fusion = (bf16[1024,2048]{1,0:T(8,128)(2,1)S(1)}, f32[1024,2048]{1,0:T(8,128)}) fusion(bf16[1024,2816]{1,0:T(8,128)(2,1)} %bitcast.310, bf16[512,1024]{1,0:T(8,128)(2,1)} %collective-permute-done.18, bf16[512,1024]{1,0:T(8,128)(2,1)} %fusion.28), kind=kOutput, calls=%fused_computation.9 | convolution fusion | flops 4318035968 | bytes 18874368 | tf_op jit(solution)/shard_map/dot_general | solution.py:349
  188.8 2.0 copy-done.49
  190.8 7.7 %convolution_convert_fusion.2 = bf16[1024,2048]{1,0:T(8,128)(2,1)} fusion(bf16[1024,2048]{1,0:T(8,128)(2,1)S(1)} %get-tuple-element.87, bf16[512,1024]{1,0:T(8,128)(2,1)} %collective-permute-done.20, bf16[512,1024]{1,0:T(8,128)(2,1)} %fusion.26), kind=kOutput, calls=%fused_computation.14 | convolution fusion | flops 4301258752 | bytes 10485760 | tf_op jit(solution)/shard_map/dot_general | solution.py:357
  198.6 12.7 %fusion.6 = bf16[1024,2048]{1,0:T(8,128)(2,1)S(1)} fusion(f32[1024,2048]{1,0:T(8,128)} %get-tuple-element.88, bf16[1024,2048]{1,0:T(8,128)(2,1)} %all-gather.3.cloned.1.call-done, bf16[512,1024]{1,0:T(8,128)(2,1)} %collective-permute-done.20, bf16[512,1024]{1,0:T(8,128)(2,1)} %fusion.26), kind=kOutput, calls=%fused_computation.8 | convolution fusion | flops 4341104640 | bytes 18874368 | tf_op jit(solution)/shard_map/dot_general | solution.py:362
  211.4 4.7 %fusion.64 = bf16[512,1024]{1,0:T(8,128)(2,1)S(1)} fusion(bf16[1024,2816]{1,0:T(8,128)(2,1)} %bitcast.311, bf16[1024,2048]{1,0:T(8,128)(2,1)S(1)} %fusion.6), kind=kOutput, calls=%fused_computation.108 | convolution fusion | flops 2148007936 | bytes 7340032 | tf_op jit(solution)/shard_map/dot_general | solution.py:151
  216.3 3.4 fusion.61
  220.1 6.6 %convolution_convert_fusion.3 = bf16[1024,2048]{1,0:T(8,128)(2,1)S(1)} fusion(bf16[1024,2048]{1,0:T(8,128)(2,1)S(1)} %fusion.6, bf16[512,1024]{1,0:T(8,128)(2,1)} %collective-permute-done.18, bf16[512,1024]{1,0:T(8,128)(2,1)} %fusion.28), kind=kOutput, calls=%fused_computation.15 | convolution fusion | flops 4301258752 | bytes 10485760 | tf_op jit(solution)/shard_map/dot_general | solution.py:357
  230.9 3.7 bitcast_multiply_fusion
  241.8 3.7 fusion.33
  247.2 2.3 constant_dynamic-update-slice_fusion.1
  249.5 4.1 convolution_convert_fusion.5.grad_ref
  253.6 20.9 %attend_back.1 = bf16[1024,1536]{1,0:T(8,128)(2,1)} custom-call(bf16[1024,1536]{1,0:T(8,128)(2,1)} %convolution_convert_fusion.1.qkv_ref, bf16[1024,128]{1,0:T(8,128)(2,1)} %bitcast.330, bf16[1024,128]{1,0:T(8,128)(2,1)} %bitcast.332, f32[4,2,1024]{2,1,0:T(2,128)} %get-tuple-element.22.log_ref, bf16[1024,512]{1,0:T(8,128)(2,1)} %convolution_convert_fusion.5.grad_ref), custom_call_target="tpu_custom_call" | custom-call | flops 5368709120 | bytes 7340032 | tf_op jit(solution)/shard_map/attend_back/pallas_call | solution.py:257
  274.5 4.4 fusion.58
  279.4 3.8 convolution_convert_fusion
  294.0 4.0 bitcast_reduce_fusion.1
  298.1 15.3 %collective-permute-done.33 = bf16[4,2,64,1024]{3,2,0,1:T(8,128)(2,1)S(1)} collective-permute-done((bf16[4,2,64,1024]{3,2,0,1:T(8,128)(2,1)S(1)}, bf16[4,2,64,1024]{3,2,0,1:T(8,128)(2,1)S(1)}, u32[]{:S(2)}, u32[]{:S(2)}) %collective-permute-start.33) | collective-permute-done | bytes 1048608 | tf_op jit(solution)/shard_map/ppermute | solution.py:108
  314.8 3.3 collective-permute-start.34
  319.4 16.5 %collective-permute-done.26 = bf16[4,2,64,1024]{3,2,0,1:T(8,128)(2,1)S(1)} collective-permute-done((bf16[4,2,64,1024]{3,2,0,1:T(8,128)(2,1)S(1)}, bf16[4,2,64,1024]{3,2,0,1:T(8,128)(2,1)S(1)}, u32[]{:S(2)}, u32[]{:S(2)}) %collective-permute-start.26) | collective-permute-done | bytes 1048608 | tf_op jit(solution)/shard_map/ppermute | solution.py:108
  337.2 3.3 collective-permute-start.27
  343.9 2.8 fusion.15
  347.3 11.3 %collective-permute-done.27 = bf16[4,64,1024]{2,1,0:T(8,128)(2,1)} collective-permute-done((bf16[4,64,1024]{2,1,0:T(8,128)(2,1)}, bf16[4,64,1024]{2,1,0:T(8,128)(2,1)}, u32[]{:S(2)}, u32[]{:S(2)}) %collective-permute-start.27) | collective-permute-done | bytes 524320 | tf_op jit(solution)/shard_map/ppermute | solution.py:108
  364.0 1.9 collective-permute-start.30
  369.4 2.9 collective-permute-start.36
  372.3 7.4 %collective-permute-done.28 = bf16[64,2048]{1,0:T(8,128)(2,1)S(1)} collective-permute-done((bf16[64,2048]{1,0:T(8,128)(2,1)S(1)}, bf16[64,2048]{1,0:T(8,128)(2,1)S(1)}, u32[]{:S(2)}, u32[]{:S(2)}) %collective-permute-start.28) | collective-permute-done | bytes 262176 | tf_op jit(solution)/shard_map/ppermute | solution.py:108
  379.7 22.0 %collective-permute-done.29 = bf16[64,2048]{1,0:T(8,128)(2,1)S(1)} collective-permute-done((bf16[64,2048]{1,0:T(8,128)(2,1)S(1)}, bf16[64,2048]{1,0:T(8,128)(2,1)S(1)}, u32[]{:S(2)}, u32[]{:S(2)}) %collective-permute-start.29) | collective-permute-done | bytes 262176 | tf_op jit(solution)/shard_map/ppermute | solution.py:108
  405.3 2.3 collective-permute-done.35
  407.6 8.3 %collective-permute-done.36 = bf16[64,2048]{1,0:T(8,128)(2,1)S(1)} collective-permute-done((bf16[64,2048]{1,0:T(8,128)(2,1)}, bf16[64,2048]{1,0:T(8,128)(2,1)S(1)}, u32[]{:S(2)}, u32[]{:S(2)}) %collective-permute-start.36) | collective-permute-done | bytes 262176 | tf_op jit(solution)/shard_map/ppermute | solution.py:108
  416.0 2.2 collective-permute-done.37
  420.9 4.4 all-gather.5.cloned.1.call-done
  425.2 2.4 convert_reduce_fusion
  427.6 6.6 %fusion.123 = f32[1024,3072]{1,0:T(8,128)} fusion(bf16[256,1024]{1,0:T(8,128)(2,1)S(1)} %copy-done.26, bf16[256,3072]{1,0:T(8,128)(2,1)S(1)} %copy-done.16), kind=kOutput, calls=%fused_computation.273 | convolution fusion | flops 1610612736 | bytes 14680064 | tf_op jit(solution)/shard_map/dot_general | solution.py:357
  (304 shorter events, 103.7 us)
Async XLA Ops:
  7.2 191.4 %all-gather.3.cloned.1.call-start = ((), (), s32[]{:S(2)}) async-start(), calls=%async_computation.1 | async-start | bytes 4456448 | tf_op jit(solution)/shard_map/all_gather | solution.py:310
  8.7 15.3 %collective-permute-start.3 = (bf16[64,1536]{1,0:T(8,128)(2,1)S(1)}, bf16[64,1536]{1,0:T(8,128)(2,1)S(1)}, u32[]{:S(2)}, u32[]{:S(2)}) collective-permute-start(bf16[64,1536]{1,0:T(8,128)(2,1)S(1)} %reshape.369), channel_id=1, source_target_pairs={{0,8},{2,10},{4,12},{6,14},{8,16},{10,18},{12,20},{14,22},{16,24},... | collective-permute-start | bytes 589832 | tf_op jit(solution)/shard_map/ppermute | solution.py:77
  10.3 16.8 %collective-permute-start.4 = (bf16[64,1536]{1,0:T(8,128)(2,1)S(1)}, bf16[64,1536]{1,0:T(8,128)(2,1)S(1)}, u32[]{:S(2)}, u32[]{:S(2)}) collective-permute-start(bf16[64,1536]{1,0:T(8,128)(2,1)S(1)} %reshape.369), channel_id=1, source_target_pairs={{0,16},{2,18},{4,20},{6,22},{8,24},{10,26},{12,28},{14,30},{16,0},... | collective-permute-start | bytes 589832 | tf_op jit(solution)/shard_map/ppermute | solution.py:77
  11.5 17.3 %collective-permute-start.5 = (bf16[64,1536]{1,0:T(8,128)(2,1)S(1)}, bf16[64,1536]{1,0:T(8,128)(2,1)S(1)}, u32[]{:S(2)}, u32[]{:S(2)}) collective-permute-start(bf16[64,1536]{1,0:T(8,128)(2,1)S(1)} %reshape.369), channel_id=1, source_target_pairs={{0,24},{2,26},{4,28},{6,30},{8,0},{10,2},{12,4},{14,6},{16,8},{18,... | collective-permute-start | bytes 589832 | tf_op jit(solution)/shard_map/ppermute | solution.py:77
  13.3 1.5 collective-permute-start
  19.2 1.5 collective-permute-start.1
  22.5 56.0 %collective-permute-start.2 = (bf16[512,1024]{1,0:T(8,128)(2,1)}, bf16[512,1024]{1,0:T(8,128)(2,1)}, u32[]{:S(2)}, u32[]{:S(2)}) collective-permute-start(bf16[512,1024]{1,0:T(8,128)(2,1)} %get-tuple-element.78), channel_id=1, source_target_pairs={{0,1},{1,0},{2,3},{3,2},{4,5},{5,4},{6,7},{7,6},{8,9},{9,8},{10,11... | collective-permute-start | bytes 3145736 | tf_op jit(solution)/shard_map/ppermute | solution.py:135
  28.9 11.7 %collective-permute-start.10 = (bf16[64,2816]{1,0:T(8,128)(2,1)}, bf16[64,2816]{1,0:T(8,128)(2,1)}, u32[]{:S(2)}, u32[]{:S(2)}) collective-permute-start(bf16[64,2816]{1,0:T(8,128)(2,1)} %pad_maximum_fusion.11), channel_id=1, source_target_pairs={{0,8},{2,10},{4,12},{6,14},{8,16},{10,18},{12,20},{14,22},{16,24},... | collective-permute-start | bytes 1081352 | tf_op jit(solution)/shard_map/ppermute | solution.py:77
  29.0 37.2 %collective-permute-start.11 = (bf16[64,2816]{1,0:T(8,128)(2,1)}, bf16[64,2816]{1,0:T(8,128)(2,1)}, u32[]{:S(2)}, u32[]{:S(2)}) collective-permute-start(bf16[64,2816]{1,0:T(8,128)(2,1)} %pad_maximum_fusion.11), channel_id=1, source_target_pairs={{0,16},{2,18},{4,20},{6,22},{8,24},{10,26},{12,28},{14,30},{16,0},... | collective-permute-start | bytes 1081352 | tf_op jit(solution)/shard_map/ppermute | solution.py:77
  30.7 36.6 %collective-permute-start.12 = (bf16[64,2816]{1,0:T(8,128)(2,1)}, bf16[64,2816]{1,0:T(8,128)(2,1)}, u32[]{:S(2)}, u32[]{:S(2)}) collective-permute-start(bf16[64,2816]{1,0:T(8,128)(2,1)} %pad_maximum_fusion.11), channel_id=1, source_target_pairs={{0,24},{2,26},{4,28},{6,30},{8,0},{10,2},{12,4},{14,6},{16,8},{18,... | collective-permute-start | bytes 1081352 | tf_op jit(solution)/shard_map/ppermute | solution.py:77
  34.7 40.1 %collective-permute-start.6 = (bf16[4,64,768]{2,1,0:T(8,128)(2,1)}, bf16[4,64,768]{2,1,0:T(8,128)(2,1)}, u32[]{:S(2)}, u32[]{:S(2)}) collective-permute-start(bf16[4,64,768]{2,1,0:T(8,128)(2,1)} %get-tuple-element.61), channel_id=1, source_target_pairs={{0,2},{2,0},{4,6},{6,4},{8,10},{10,8},{12,14},{14,12},{16,18},{18,... | collective-permute-start | bytes 1179656 | tf_op jit(solution)/shard_map/ppermute | solution.py:77
  35.2 383.8 %reduce-scatter.2.cloned.1.call-start = ((), (), s32[]{:S(2)}) async-start(), calls=%async_computation.2 | async-start | bytes 4456448 | tf_op jit(solution)/shard_map/reduce_scatter | solution.py:359
  40.5 35.9 %collective-permute-start.8 = (bf16[4,64,768]{2,1,0:T(8,128)(2,1)S(1)}, bf16[4,64,768]{2,1,0:T(8,128)(2,1)S(1)}, u32[]{:S(2)}, u32[]{:S(2)}) collective-permute-start(bf16[4,64,768]{2,1,0:T(8,128)(2,1)S(1)} %copy-done.38), channel_id=1, source_target_pairs={{0,4},{2,6},{4,0},{6,2},{8,12},{10,14},{12,8},{14,10},{16,20},{18,... | collective-permute-start | bytes 1179656 | tf_op jit(solution)/shard_map/ppermute | solution.py:77
  70.6 24.6 %collective-permute-start.13 = (bf16[4,64,1408]{2,1,0:T(8,128)(2,1)S(1)}, bf16[4,64,1408]{2,1,0:T(8,128)(2,1)S(1)}, u32[]{:S(2)}, u32[]{:S(2)}) collective-permute-start(bf16[4,64,1408]{2,1,0:T(8,128)(2,1)S(1)} %get-tuple-element.53), channel_id=1, source_target_pairs={{0,2},{2,0},{4,6},{6,4},{8,10},{10,8},{12,14},{14,12},{16,18},{18,... | collective-permute-start | bytes 2162696 | tf_op jit(solution)/shard_map/ppermute | solution.py:77
  71.1 28.8 %collective-permute-start.15 = (bf16[4,64,1408]{2,1,0:T(8,128)(2,1)S(1)}, bf16[4,64,1408]{2,1,0:T(8,128)(2,1)S(1)}, u32[]{:S(2)}, u32[]{:S(2)}) collective-permute-start(bf16[4,64,1408]{2,1,0:T(8,128)(2,1)S(1)} %get-tuple-element.54), channel_id=1, source_target_pairs={{0,4},{2,6},{4,0},{6,2},{8,12},{10,14},{12,8},{14,10},{16,20},{18,... | collective-permute-start | bytes 2162696 | tf_op jit(solution)/shard_map/ppermute | solution.py:77
  75.8 42.6 %collective-permute-start.7 = (bf16[4,2,64,768]{3,2,1,0:T(8,128)(2,1)S(1)}, bf16[4,2,64,768]{3,2,1,0:T(8,128)(2,1)S(1)}, u32[]{:S(2)}, u32[]{:S(2)}) collective-permute-start(bf16[4,2,64,768]{3,2,1,0:T(8,128)(2,1)S(1)} %bitcast_dynamic-update-slice_fusion.13), channel_id=1, source_target_pairs={{0,4},{2,6},{4,0},{6,2},{8,12},{10,14},{12,8},{14,10},{16,20},{18,... | collective-permute-start | bytes 2359304 | tf_op jit(solution)/shard_map/ppermute | solution.py:77
  76.4 48.2 %collective-permute-start.9 = (bf16[4,2,64,768]{3,2,1,0:T(8,128)(2,1)S(1)}, bf16[4,2,64,768]{3,2,1,0:T(8,128)(2,1)S(1)}, u32[]{:S(2)}, u32[]{:S(2)}) collective-permute-start(bf16[4,2,64,768]{3,2,1,0:T(8,128)(2,1)S(1)} %bitcast_dynamic-update-slice_fusion.15), channel_id=1, source_target_pairs={{0,2},{2,0},{4,6},{6,4},{8,10},{10,8},{12,14},{14,12},{16,18},{18,... | collective-permute-start | bytes 2359304 | tf_op jit(solution)/shard_map/ppermute | solution.py:77
  81.1 43.9 %copy-start.29 = (bf16[1024,1024]{1,0:T(8,128)(2,1)}, bf16[1024,1024]{1,0:T(8,128)(2,1)S(1)}, u32[]{:S(2)}) copy-start(bf16[1024,1024]{1,0:T(8,128)(2,1)S(1)} %constant_dynamic-update-slice_fusion.4) | copy-start | bytes 6291460
  96.1 58.6 %collective-permute-start.14 = (bf16[4,2,64,1408]{3,2,1,0:T(8,128)(2,1)}, bf16[4,2,64,1408]{3,2,1,0:T(8,128)(2,1)S(1)}, u32[]{:S(2)}, u32[]{:S(2)}) collective-permute-start(bf16[4,2,64,1408]{3,2,1,0:T(8,128)(2,1)} %bitcast_dynamic-update-slice_fusion.9), channel_id=1, source_target_pairs={{0,4},{2,6},{4,0},{6,2},{8,12},{10,14},{12,8},{14,10},{16,20},{18,... | collective-permute-start | bytes 4325384 | tf_op jit(solution)/shard_map/ppermute | solution.py:77
  101.0 56.7 %collective-permute-start.16 = (bf16[4,2,64,1408]{3,2,1,0:T(8,128)(2,1)}, bf16[4,2,64,1408]{3,2,1,0:T(8,128)(2,1)}, u32[]{:S(2)}, u32[]{:S(2)}) collective-permute-start(bf16[4,2,64,1408]{3,2,1,0:T(8,128)(2,1)} %bitcast_dynamic-update-slice_fusion.11), channel_id=1, source_target_pairs={{0,2},{2,0},{4,6},{6,4},{8,10},{10,8},{12,14},{14,12},{16,18},{18,... | collective-permute-start | bytes 4325384 | tf_op jit(solution)/shard_map/ppermute | solution.py:77
  103.9 20.7 %copy-start.13 = (bf16[4,2,2,64,1408]{4,3,2,1,0:T(8,128)(2,1)}, bf16[4,2,2,64,1408]{4,3,2,1,0:T(8,128)(2,1)S(1)}, u32[]{:S(2)}) copy-start(bf16[4,2,2,64,1408]{4,3,2,1,0:T(8,128)(2,1)S(1)} %bitcast_dynamic-update-slice_fusion) | copy-start | bytes 8650756
  161.2 2.7 collective-permute-start.17
  169.6 7.3 %collective-permute-start.18 = (bf16[512,1024]{1,0:T(8,128)(2,1)}, bf16[512,1024]{1,0:T(8,128)(2,1)}, u32[]{:S(2)}, u32[]{:S(2)}) collective-permute-start(bf16[512,1024]{1,0:T(8,128)(2,1)} %fusion.28), channel_id=1, source_target_pairs={{0,1},{1,0},{2,3},{3,2},{4,5},{5,4},{6,7},{7,6},{8,9},{9,8},{10,11... | collective-permute-start | bytes 3145736 | tf_op jit(solution)/shard_map/ppermute | solution.py:135
  172.4 16.5 %collective-permute-start.20 = (bf16[512,1024]{1,0:T(8,128)(2,1)}, bf16[512,1024]{1,0:T(8,128)(2,1)}, u32[]{:S(2)}, u32[]{:S(2)}) collective-permute-start(bf16[512,1024]{1,0:T(8,128)(2,1)} %fusion.26), channel_id=1, source_target_pairs={{0,1},{1,0},{2,3},{3,2},{4,5},{5,4},{6,7},{7,6},{8,9},{9,8},{10,11... | collective-permute-start | bytes 3145736 | tf_op jit(solution)/shard_map/ppermute | solution.py:135
  198.5 226.7 %all-gather.5.cloned.1.call-start = ((), (), s32[]{:S(2)}) async-start(), calls=%async_computation.3 | async-start | bytes 1671168 | tf_op jit(solution)/shard_map/all_gather | solution.py:393
  216.1 13.2 %collective-permute-start.21 = (bf16[512,1024]{1,0:T(8,128)(2,1)S(1)}, bf16[512,1024]{1,0:T(8,128)(2,1)S(1)}, u32[]{:S(2)}, u32[]{:S(2)}) collective-permute-start(bf16[512,1024]{1,0:T(8,128)(2,1)S(1)} %fusion.64), channel_id=1, source_target_pairs={{0,1},{1,0},{2,3},{3,2},{4,5},{5,4},{6,7},{7,6},{8,9},{9,8},{10,11... | collective-permute-start | bytes 3145736 | tf_op jit(solution)/shard_map/ppermute | solution.py:135
  219.7 73.8 %collective-permute-start.19 = (bf16[512,1024]{1,0:T(8,128)(2,1)}, bf16[512,1024]{1,0:T(8,128)(2,1)}, u32[]{:S(2)}, u32[]{:S(2)}) collective-permute-start(bf16[512,1024]{1,0:T(8,128)(2,1)} %fusion.61), channel_id=1, source_target_pairs={{0,1},{1,0},{2,3},{3,2},{4,5},{5,4},{6,7},{7,6},{8,9},{9,8},{10,11... | collective-permute-start | bytes 3145736 | tf_op jit(solution)/shard_map/ppermute | solution.py:135
  241.7 5.5 %collective-permute-start.22 = (bf16[512,1024]{1,0:T(8,128)(2,1)}, bf16[512,1024]{1,0:T(8,128)(2,1)}, u32[]{:S(2)}, u32[]{:S(2)}) collective-permute-start(bf16[512,1024]{1,0:T(8,128)(2,1)} %get-tuple-element.84), channel_id=1, source_target_pairs={{0,1},{1,0},{2,3},{3,2},{4,5},{5,4},{6,7},{7,6},{8,9},{9,8},{10,11... | collective-permute-start | bytes 3145736 | tf_op jit(solution)/shard_map/ppermute | solution.py:135
  278.9 11.2 %collective-permute-start.23 = (bf16[512,1024]{1,0:T(8,128)(2,1)S(1)}, bf16[512,1024]{1,0:T(8,128)(2,1)S(1)}, u32[]{:S(2)}, u32[]{:S(2)}) collective-permute-start(bf16[512,1024]{1,0:T(8,128)(2,1)S(1)} %fusion.58), channel_id=1, source_target_pairs={{0,1},{1,0},{2,3},{3,2},{4,5},{5,4},{6,7},{7,6},{8,9},{9,8},{10,11... | collective-permute-start | bytes 3145736 | tf_op jit(solution)/shard_map/ppermute | solution.py:135
  284.5 28.9 %collective-permute-start.33 = (bf16[4,2,64,1024]{3,2,0,1:T(8,128)(2,1)S(1)}, bf16[4,2,64,1024]{3,2,0,1:T(8,128)(2,1)S(1)}, u32[]{:S(2)}, u32[]{:S(2)}) collective-permute-start(bf16[4,2,64,1024]{3,2,0,1:T(8,128)(2,1)S(1)} %copy-done.34), channel_id=1, source_target_pairs={{0,2},{2,0},{4,6},{6,4},{8,10},{10,8},{12,14},{14,12},{16,18},{18,... | collective-permute-start | bytes 3145736 | tf_op jit(solution)/shard_map/ppermute | solution.py:108
  286.1 31.9 %collective-permute-start.31 = (bf16[4,2,64,1024]{3,2,0,1:T(8,128)(2,1)S(1)}, bf16[4,2,64,1024]{3,2,0,1:T(8,128)(2,1)S(1)}, u32[]{:S(2)}, u32[]{:S(2)}) collective-permute-start(bf16[4,2,64,1024]{3,2,0,1:T(8,128)(2,1)S(1)} %copy-done.35), channel_id=1, source_target_pairs={{0,4},{2,6},{4,0},{6,2},{8,12},{10,14},{12,8},{14,10},{16,20},{18,... | collective-permute-start | bytes 3145736 | tf_op jit(solution)/shard_map/ppermute | solution.py:108
  289.1 46.7 %collective-permute-start.26 = (bf16[4,2,64,1024]{3,2,0,1:T(8,128)(2,1)S(1)}, bf16[4,2,64,1024]{3,2,0,1:T(8,128)(2,1)S(1)}, u32[]{:S(2)}, u32[]{:S(2)}) collective-permute-start(bf16[4,2,64,1024]{3,2,0,1:T(8,128)(2,1)S(1)} %bitcast.326), channel_id=1, source_target_pairs={{0,2},{2,0},{4,6},{6,4},{8,10},{10,8},{12,14},{14,12},{16,18},{18,... | collective-permute-start | bytes 3145736 | tf_op jit(solution)/shard_map/ppermute | solution.py:108
  290.1 50.4 %collective-permute-start.24 = (bf16[4,2,64,1024]{3,2,0,1:T(8,128)(2,1)S(1)}, bf16[4,2,64,1024]{3,2,0,1:T(8,128)(2,1)S(1)}, u32[]{:S(2)}, u32[]{:S(2)}) collective-permute-start(bf16[4,2,64,1024]{3,2,0,1:T(8,128)(2,1)S(1)} %bitcast.325), channel_id=1, source_target_pairs={{0,4},{2,6},{4,0},{6,2},{8,12},{10,14},{12,8},{14,10},{16,20},{18,... | collective-permute-start | bytes 3145736 | tf_op jit(solution)/shard_map/ppermute | solution.py:108
  294.0 19.4 %copy-start.24 = (bf16[4,2,64,1024]{3,2,0,1:T(8,128)(2,1)S(1)}, bf16[4,2,64,1024]{3,2,0,1:T(8,128)(2,1)}, u32[]{:S(2)}) copy-start(bf16[4,2,64,1024]{3,2,0,1:T(8,128)(2,1)} %get-tuple-element.26) | copy-start | bytes 3145732
  298.1 20.0 %copy-start.25 = (bf16[4,2,64,1024]{3,2,0,1:T(8,128)(2,1)S(1)}, bf16[4,2,64,1024]{3,2,0,1:T(8,128)(2,1)}, u32[]{:S(2)}) copy-start(bf16[4,2,64,1024]{3,2,0,1:T(8,128)(2,1)} %get-tuple-element.24) | copy-start | bytes 3145732
  298.1 48.6 %collective-permute-start.38 = (bf16[8,3072]{1,0:T(8,128)(2,1)S(1)}, bf16[8,3072]{1,0:T(8,128)(2,1)S(1)}, u32[]{:S(2)}, u32[]{:S(2)}) collective-permute-start(bf16[8,3072]{1,0:T(8,128)(2,1)S(1)} %fusion.102), channel_id=1, source_target_pairs={{0,1},{1,0},{2,3},{3,2},{4,5},{5,4},{6,7},{7,6},{8,9},{9,8},{10,11... | collective-permute-start | bytes 147464 | tf_op jit(solution)/shard_map/ppermute | solution.py:135
  314.8 51.2 %collective-permute-start.34 = (bf16[4,64,1024]{2,1,0:T(8,128)(2,1)}, bf16[4,64,1024]{2,1,0:T(8,128)(2,1)}, u32[]{:S(2)}, u32[]{:S(2)}) collective-permute-start(bf16[4,64,1024]{2,1,0:T(8,128)(2,1)} %dynamic-slice_bitcast_fusion), channel_id=1, source_target_pairs={{0,4},{2,6},{4,0},{6,2},{8,12},{10,14},{12,8},{14,10},{16,20},{18,... | collective-permute-start | bytes 1572872 | tf_op jit(solution)/shard_map/ppermute | solution.py:108
  318.4 17.9 %copy-start.19 = (bf16[4,2,64,1024]{3,2,0,1:T(8,128)(2,1)}, bf16[4,2,64,1024]{3,2,0,1:T(8,128)(2,1)S(1)}, u32[]{:S(2)}) copy-start(bf16[4,2,64,1024]{3,2,0,1:T(8,128)(2,1)S(1)} %add_convert_fusion.1) | copy-start | bytes 3145732
  319.4 47.8 %collective-permute-start.32 = (bf16[4,64,1024]{2,1,0:T(8,128)(2,1)}, bf16[4,64,1024]{2,1,0:T(8,128)(2,1)}, u32[]{:S(2)}, u32[]{:S(2)}) collective-permute-start(bf16[4,64,1024]{2,1,0:T(8,128)(2,1)} %dynamic-slice_bitcast_fusion.1), channel_id=1, source_target_pairs={{0,2},{2,0},{4,6},{6,4},{8,10},{10,8},{12,14},{14,12},{16,18},{18,... | collective-permute-start | bytes 1572872 | tf_op jit(solution)/shard_map/ppermute | solution.py:108
  337.2 21.4 %collective-permute-start.27 = (bf16[4,64,1024]{2,1,0:T(8,128)(2,1)}, bf16[4,64,1024]{2,1,0:T(8,128)(2,1)}, u32[]{:S(2)}, u32[]{:S(2)}) collective-permute-start(bf16[4,64,1024]{2,1,0:T(8,128)(2,1)} %dynamic-slice_bitcast_fusion.2), channel_id=1, source_target_pairs={{0,4},{2,6},{4,0},{6,2},{8,12},{10,14},{12,8},{14,10},{16,20},{18,... | collective-permute-start | bytes 1572872 | tf_op jit(solution)/shard_map/ppermute | solution.py:108
  341.9 18.2 %collective-permute-start.25 = (bf16[4,64,1024]{2,1,0:T(8,128)(2,1)}, bf16[4,64,1024]{2,1,0:T(8,128)(2,1)}, u32[]{:S(2)}, u32[]{:S(2)}) collective-permute-start(bf16[4,64,1024]{2,1,0:T(8,128)(2,1)} %dynamic-slice_bitcast_fusion.3), channel_id=1, source_target_pairs={{0,2},{2,0},{4,6},{6,4},{8,10},{10,8},{12,14},{14,12},{16,18},{18,... | collective-permute-start | bytes 1572872 | tf_op jit(solution)/shard_map/ppermute | solution.py:108
  361.5 18.2 %collective-permute-start.28 = (bf16[64,2048]{1,0:T(8,128)(2,1)S(1)}, bf16[64,2048]{1,0:T(8,128)(2,1)S(1)}, u32[]{:S(2)}, u32[]{:S(2)}) collective-permute-start(bf16[64,2048]{1,0:T(8,128)(2,1)S(1)} %get-tuple-element.58), channel_id=1, source_target_pairs={{0,8},{2,10},{4,12},{6,14},{8,16},{10,18},{12,20},{14,22},{16,24},... | collective-permute-start | bytes 786440 | tf_op jit(solution)/shard_map/ppermute | solution.py:108
  362.2 39.6 %collective-permute-start.29 = (bf16[64,2048]{1,0:T(8,128)(2,1)S(1)}, bf16[64,2048]{1,0:T(8,128)(2,1)S(1)}, u32[]{:S(2)}, u32[]{:S(2)}) collective-permute-start(bf16[64,2048]{1,0:T(8,128)(2,1)S(1)} %get-tuple-element.59), channel_id=1, source_target_pairs={{0,16},{2,18},{4,20},{6,22},{8,24},{10,26},{12,28},{14,30},{16,0},... | collective-permute-start | bytes 786440 | tf_op jit(solution)/shard_map/ppermute | solution.py:108
  364.0 39.2 %collective-permute-start.30 = (bf16[64,2048]{1,0:T(8,128)(2,1)S(1)}, bf16[64,2048]{1,0:T(8,128)(2,1)S(1)}, u32[]{:S(2)}, u32[]{:S(2)}) collective-permute-start(bf16[64,2048]{1,0:T(8,128)(2,1)S(1)} %get-tuple-element.60), channel_id=1, source_target_pairs={{0,24},{2,26},{4,28},{6,30},{8,0},{10,2},{12,4},{14,6},{16,8},{18,... | collective-permute-start | bytes 786440 | tf_op jit(solution)/shard_map/ppermute | solution.py:108
  369.3 38.3 %collective-permute-start.35 = (bf16[64,2048]{1,0:T(8,128)(2,1)}, bf16[64,2048]{1,0:T(8,128)(2,1)S(1)}, u32[]{:S(2)}, u32[]{:S(2)}) collective-permute-start(bf16[64,2048]{1,0:T(8,128)(2,1)} %get-tuple-element.55), channel_id=1, source_target_pairs={{0,8},{2,10},{4,12},{6,14},{8,16},{10,18},{12,20},{14,22},{16,24},... | collective-permute-start | bytes 786440 | tf_op jit(solution)/shard_map/ppermute | solution.py:108
  369.4 46.6 %collective-permute-start.36 = (bf16[64,2048]{1,0:T(8,128)(2,1)}, bf16[64,2048]{1,0:T(8,128)(2,1)S(1)}, u32[]{:S(2)}, u32[]{:S(2)}) collective-permute-start(bf16[64,2048]{1,0:T(8,128)(2,1)} %get-tuple-element.56), channel_id=1, source_target_pairs={{0,16},{2,18},{4,20},{6,22},{8,24},{10,26},{12,28},{14,30},{16,0},... | collective-permute-start | bytes 786440 | tf_op jit(solution)/shard_map/ppermute | solution.py:108
  379.7 38.5 %collective-permute-start.37 = (bf16[64,2048]{1,0:T(8,128)(2,1)S(1)}, bf16[64,2048]{1,0:T(8,128)(2,1)S(1)}, u32[]{:S(2)}, u32[]{:S(2)}) collective-permute-start(bf16[64,2048]{1,0:T(8,128)(2,1)S(1)} %get-tuple-element.57), channel_id=1, source_target_pairs={{0,24},{2,26},{4,28},{6,30},{8,0},{10,2},{12,4},{14,6},{16,8},{18,... | collective-permute-start | bytes 786440 | tf_op jit(solution)/shard_map/ppermute | solution.py:108
  405.3 22.3 %copy-start.26 = (bf16[256,1024]{1,0:T(8,128)(2,1)S(1)}, bf16[256,1024]{1,0:T(8,128)(2,1)}, u32[]{:S(2)}) copy-start(bf16[256,1024]{1,0:T(8,128)(2,1)} %reshape.378) | copy-start | bytes 1572868
  (47 other events, 182.5 us)
Sparse Core Ops, SparseCore 0:
  35.4 106.2 all-gather.2
  198.7 101.0 reduce-scatter.1
  347.5 77.7 all-gather.4
where the time goes:
time: 449 us; the launch traced here: 441 us
  waiting for transfers between devices  169 us (38%)
  matrix products  88 us (20%)
  local copies, waits for them, and re-layouts  57.5 us (13%)
  Pallas kernels  39.7 us (9%)
  starting transfers between devices  38.4 us (9%)
  other arithmetic  33 us (7%)
  between operations  15.5 us (3%)
    ppermute x14, waiting for transfers between devices, sum_pieces(): lax.ppermute(pieces[k], 'rows', shift_pairs(grid, axis, k)).astype(f32)  86.8 us
    ppermute x14, waiting for transfers between devices, gather_axis(): lax.ppermute(part, 'rows', shift_pairs(grid, axis, k))  75 us
    dot_general x5, matrix products, tn(): lax.dot_general(a, b, (((0,), (0,)), ((), ())), preferred_element_type=f32)  26 us
    dot_general x8, matrix products, nt(): lax.dot_general(a, b, (((1,), (1,)), ((), ())), preferred_element_type=f32)  24.7 us
    pallas_call x1, Pallas kernels, attend_back(): pl.pallas_call(backward_kernel, grid=(pairs,), in_specs=[pl.BlockSpec((le...  20.9 us
    pallas_call x1, Pallas kernels, attend(): pl.pallas_call(forward_kernel, grid=(pairs,), in_specs=[pl.BlockSpec((len...  18.7 us
    ppermute x14, starting transfers between devices, sum_pieces(): lax.ppermute(pieces[k], 'rows', shift_pairs(grid, axis, k)).astype(f32)  18.2 us
    ppermute x14, starting transfers between devices, gather_axis(): lax.ppermute(part, 'rows', shift_pairs(grid, axis, k))  17.2 us
  transfers between devices with their start and end apart: 42, of which 23 were waited for; matrix products, arithmetic and copies ran while one was open for 35% of the time, Pallas kernels for 9%

commit v1 on v0

--- a/solution.py
+++ b/solution.py
@@ -39,8 +39,14 @@
     return normalize(values) * (1.0 + factors) + offsets
 
 
-def gelu_tanh(values):
-    return jax.nn.gelu(values, approximate=True)
+def gelu_and_slope(values):
+    square = values * values
+    inner = math.sqrt(2.0 / math.pi) * (values + 0.044715 * (values * square))
+    bend = jnp.tanh(inner)
+    half = 0.5 * (1.0 + bend)
+    steep = math.sqrt(2.0 / math.pi) * (1.0 + 3.0 * 0.044715 * square)
+    slope = half + 0.5 * values * (1.0 - bend * bend) * steep
+    return (values * half).astype(bf16), slope.astype(bf16)
 
 
 def grid_of(count):
@@ -70,12 +76,14 @@
     return (me // (grid[1] * grid[2]), (me // grid[2]) % grid[1], me % grid[2])
 
 
+def moved(part, grid, axis, k):
+    return lax.ppermute(part, "rows", shift_pairs(grid, axis, k))
+
+
 def gather_axis(part, grid, axis, at, dim):
     count = grid[axis]
     whole = jnp.zeros(part.shape[:dim] + (count,) + part.shape[dim:], part.dtype)
-    pieces = [part] + [
-        lax.ppermute(part, "rows", shift_pairs(grid, axis, k)) for k in range(1, count)
-    ]
+    pieces = [part] + [moved(part, grid, axis, k) for k in range(1, count)]
     for k, piece in enumerate(pieces):
         whole = lax.dynamic_update_index_in_dim(whole, piece, (at[axis] - k) % count, dim)
     return whole
@@ -103,9 +111,10 @@
 
 
 def sum_pieces(pieces, grid, axis):
+    come = [moved(pieces[k], grid, axis, k) for k in range(1, grid[axis])]
     total = pieces[0].astype(f32)
-    for k in range(1, grid[axis]):
-        total = total + lax.ppermute(pieces[k], "rows", shift_pairs(grid, axis, k)).astype(f32)
+    for piece in come:
+        total = total + piece.astype(f32)
     return total
 
 
@@ -128,7 +137,8 @@
     second = sum_pieces(cuts[1], grid, 2).astype(bf16)
     first = scatter_axis(first, grid, 2, at, 1).astype(bf16)
     second = scatter_axis(second, grid, 1, at, 1).astype(bf16)
-    return scatter_axis(jnp.concatenate([first, second], axis=-1), grid, 0, at, 0)
+    both = jnp.concatenate([first, second], axis=-1)
+    return scatter_axis(both, grid, 0, at, 0)
 
 
 def swapped(part):
@@ -347,7 +357,7 @@
     second_own = modulated(middle, shift_mlp, scale_mlp).astype(bf16).reshape(local_len, width)
     second_full = jnp.concatenate([second_own, swapped(second_own)], axis=0)
     hidden_pre = jnp.dot(second_full, up_whole, preferred_element_type=f32)
-    hidden = gelu_tanh(hidden_pre).astype(bf16)
+    hidden, slope = lax.optimization_barrier(gelu_and_slope(hidden_pre))
     mlp_other = swapped(nt(hidden[local_len:], down_whole).astype(bf16))
     mlp_out = (nt(hidden[:local_len], down_whole) + mlp_other.astype(f32)).reshape(framed.shape)
     output = (middle + gate_mlp * mlp_out).astype(bf16).reshape(tokens.shape)
@@ -356,14 +366,18 @@
     def tn(a, b):
         return lax.dot_general(a, b, (((0,), (0,)), ((), ())), preferred_element_type=f32)
 
-    down_sum = lax.psum_scatter(
-        tn(grad_mlp_full, hidden).astype(bf16), "rows", scatter_dimension=0, tiled=True
-    ).astype(f32)
+    grad_down = tn(grad_mlp_full, hidden).astype(bf16)
+    grad_mlp_full, grad_down = lax.optimization_barrier((grad_mlp_full, grad_down))
+    down_sum = lax.psum_scatter(grad_down, "rows", scatter_dimension=0, tiled=True)
+    down_sum = down_sum.astype(f32)
     grad_hidden = jnp.dot(grad_mlp_full, down_whole, preferred_element_type=f32)
-    grad_pre = jax.vjp(gelu_tanh, hidden_pre)[1](grad_hidden)[0].astype(bf16)
-    second_other = swapped(nt(grad_pre[local_len:], up_whole).astype(bf16))
+    grad_pre = (grad_hidden * slope.astype(f32)).astype(bf16)
+    second_other = nt(grad_pre[local_len:], up_whole).astype(bf16)
+    up_cuts = scatter_cut(tn(second_full, grad_pre).astype(bf16), grid, at)
+    second_other, up_cuts = lax.optimization_barrier((second_other, up_cuts))
+    up_sum = scatter_rows(up_cuts, grid, at)
+    second_other = swapped(second_other)
     grad_second = nt(grad_pre[:local_len], up_whole) + second_other.astype(f32)
-    up_cuts = scatter_cut(tn(second_full, grad_pre).astype(bf16), grid, at)
     second_back = jax.vjp(modulated, middle, shift_mlp, scale_mlp)[1]
     grad_middle, grad_shift_mlp, grad_scale_mlp = second_back(grad_second.reshape(framed.shape))
     grad_middle = grad_middle + upstream
@@ -372,8 +386,6 @@
     branch_full = in_order(grad_branch, swapped(grad_branch), side)
     grad_out = tn(branch_full, attended).astype(bf16)
     grad_attended = jnp.dot(branch_full, out_whole, preferred_element_type=f32).astype(bf16)
-    grad_attended, up_cuts = lax.optimization_barrier((grad_attended, up_cuts))
-    up_sum = scatter_rows(up_cuts, grid, at)
     grad_qkv = attend_back(qkv, seen, frames, logs, grad_attended)
     grad_tail = jnp.concatenate([tn(first_full, grad_qkv).astype(bf16), grad_out], axis=1)
     tail_sum = scatter_rows(scatter_cut(grad_tail, grid, at), grid, at)
@@ -389,8 +401,9 @@
     low, high = low.reshape(frames_here, -1), high.reshape(frames_here, -1)
     keep = jnp.where(side == 0, low, high).astype(bf16)
     give = jnp.where(side == 0, high, low).astype(bf16)
-    mine = in_order(keep, swapped(give), side)
-    grad_mods = lax.all_gather(mine, "rows", axis=0, tiled=True)
+    give = swapped(give)
+    mine = in_order(keep, give, side)
+    grad_mods = gather_rest(gather_deep(mine, grid, at), grid, at)
     mod_sum = tn(condition_all, grad_mods)
     bias_sum = jnp.sum(grad_mods.astype(f32), axis=0)
 

time: 449 us -> 468 us (1.042)
  the two profiles are of different devices: /device:TPU:10 before, /device:TPU:0 now
where the time goes in v1:
time: 468 us; the launch traced here: 461 us
  waiting for transfers between devices  154 us (33%)
  matrix products  93.9 us (20%)
  starting transfers between devices  70.7 us (15%)
  local copies, waits for them, and re-layouts  55.3 us (12%)
  Pallas kernels  39.5 us (8%)
  other arithmetic  31.6 us (7%)
  between operations  15.9 us (3%)
    ppermute x35, waiting for transfers between devices, moved(): return lax.ppermute(part, 'rows', shift_pairs(grid, axis, k))  152 us
    ppermute x35, starting transfers between devices, moved(): return lax.ppermute(part, 'rows', shift_pairs(grid, axis, k))  68.5 us
    dot_general x8, matrix products, nt(): lax.dot_general(a, b, (((1,), (1,)), ((), ())), preferred_element_type=f32)  31.1 us
    dot_general x5, matrix products, tn(): lax.dot_general(a, b, (((0,), (0,)), ((), ())), preferred_element_type=f32)  29.8 us
    pallas_call x1, Pallas kernels, attend_back(): pl.pallas_call(backward_kernel, grid=(pairs,), in_specs=[pl.BlockSpec((le...  20.9 us
    pallas_call x1, Pallas kernels, attend(): pl.pallas_call(forward_kernel, grid=(pairs,), in_specs=[pl.BlockSpec((len...  18.5 us
    dynamic_update_slice x36, local copies, waits for them, and re-layouts, gather_axis(): lax.dynamic_update_index_in_dim(whole, piece, (at[axis] - k) % count, dim)  15.5 us
    unnamed x96, local copies, waits for them, and re-layouts  13.4 us
  transfers between devices with their start and end apart: 48, of which 21 were waited for; matrix products, arithmetic and copies ran while one was open for 30% of the time, Pallas kernels for 9%

profile of v1, /device:TPU:0, one launch (start us, length us, event | category | flops | bytes accessed | tf_op | source)
XLA Modules:
  0.0 460.7 jit_solution(13453056156353715538)
XLA Ops:
  8.7 3.1 collective-permute-start.3
  11.8 2.6 collective-permute-start.4
  17.7 3.8 convolution_add_fusion
  25.1 2.1 collective-permute-done.4
  27.3 4.7 %collective-permute-start.10 = (bf16[64,2816]{1,0:T(8,128)(2,1)}, bf16[64,2816]{1,0:T(8,128)(2,1)}, u32[]{:S(2)}, u32[]{:S(2)}) collective-permute-start(bf16[64,2816]{1,0:T(8,128)(2,1)} %pad_maximum_fusion.8), channel_id=1, source_target_pairs={{0,8},{2,10},{4,12},{6,14},{8,16},{10,18},{12,20},{14,22},{16,24},... | collective-permute-start | bytes 1081352 | tf_op jit(solution)/shard_map/ppermute | solution.py:80
  38.3 4.5 collective-permute-done.10
  45.3 15.5 %collective-permute-done.11 = bf16[64,2816]{1,0:T(8,128)(2,1)} collective-permute-done((bf16[64,2816]{1,0:T(8,128)(2,1)}, bf16[64,2816]{1,0:T(8,128)(2,1)}, u32[]{:S(2)}, u32[]{:S(2)}) %collective-permute-start.11) | collective-permute-done | bytes 360480 | tf_op jit(solution)/shard_map/ppermute | solution.py:80
  75.7 12.3 %collective-permute-done.15 = bf16[4,64,1408]{2,1,0:T(8,128)(2,1)S(1)} collective-permute-done((bf16[4,64,1408]{2,1,0:T(8,128)(2,1)S(1)}, bf16[4,64,1408]{2,1,0:T(8,128)(2,1)S(1)}, u32[]{:S(2)}, u32[]{:S(2)}) %collective-permute-start.15) | collective-permute-done | bytes 720928 | tf_op jit(solution)/shard_map/ppermute | solution.py:80
  92.3 3.1 collective-permute-done.13
  98.7 24.2 %collective-permute-done.9 = bf16[4,2,64,768]{3,2,1,0:T(8,128)(2,1)S(1)} collective-permute-done((bf16[4,2,64,768]{3,2,1,0:T(8,128)(2,1)S(1)}, bf16[4,2,64,768]{3,2,1,0:T(8,128)(2,1)S(1)}, u32[]{:S(2)}, u32[]{:S(2)}) %collective-permute-start.9) | collective-permute-done | bytes 786464 | tf_op jit(solution)/shard_map/ppermute | solution.py:80
  123.4 5.1 %convolution_convert_fusion.1.qkv_ref = bf16[1024,1536]{1,0:T(8,128)(2,1)} fusion(bf16[1024,1024]{1,0:T(8,128)(2,1)S(1)} %constant_dynamic-update-slice_fusion.4, bf16[1024,1536]{1,0:T(8,128)(2,1)S(1)} %bitcast.354), kind=kOutput, calls=%fused_computation.17 | convolution fusion | flops 3222798336 | bytes 8388608 | tf_op jit(solution)/shard_map/dot_general | solution.py:351
  129.9 18.5 %attend.1 = (bf16[1024,512]{1,0:T(8,128)(2,1)}, f32[4,2,1024]{2,1,0:T(2,128)}) custom-call(bf16[1024,1536]{1,0:T(8,128)(2,1)} %convolution_convert_fusion.1.qkv_ref, bf16[1024,128]{1,0:T(8,128)(2,1)} %bitcast.366, bf16[1024,128]{1,0:T(8,128)(2,1)} %bitcast.368), custom_call_target="tpu_custom_call" | custom-call | flops 2147483648 | bytes 4194304 | tf_op jit(solution)/shard_map/attend/pallas_call | solution.py:242
  148.4 8.2 %collective-permute-done.16 = bf16[4,2,64,1408]{3,2,1,0:T(8,128)(2,1)S(1)} collective-permute-done((bf16[4,2,64,1408]{3,2,1,0:T(8,128)(2,1)}, bf16[4,2,64,1408]{3,2,1,0:T(8,128)(2,1)S(1)}, u32[]{:S(2)}, u32[]{:S(2)}) %collective-permute-start.16) | collective-permute-done | bytes 1441824 | tf_op jit(solution)/shard_map/ppermute | solution.py:80
  164.8 2.2 bitcast_add_fusion.2
  170.5 3.2 pad_maximum_fusion.4
  173.7 12.1 %fusion.8 = (bf16[1024,2048]{1,0:T(8,128)(2,1)}, bf16[1024,2048]{1,0:T(8,128)(2,1)S(1)}) fusion(bf16[1024,2816]{1,0:T(8,128)(2,1)} %bitcast.347, bf16[512,1024]{1,0:T(8,128)(2,1)} %collective-permute-done.18, bf16[512,1024]{1,0:T(8,128)(2,1)} %fusion.30), kind=kOutput, calls=%fused_computation.10 | convolution fusion | flops 4339007488 | bytes 14680064 | tf_op jit(solution)/shard_map/dot_general | solution.py:359
  185.9 2.1 copy-done.34
  188.0 8.2 %convolution_convert_fusion.3 = bf16[1024,2048]{1,0:T(8,128)(2,1)} fusion(bf16[1024,2048]{1,0:T(8,128)(2,1)S(1)} %get-tuple-element.25, bf16[512,1024]{1,0:T(8,128)(2,1)} %collective-permute-done.20, bf16[512,1024]{1,0:T(8,128)(2,1)} %fusion.28), kind=kOutput, calls=%fused_computation.19 | convolution fusion | flops 4301258752 | bytes 10485760 | tf_op jit(solution)/shard_map/dot_general | solution.py:367
  196.2 8.6 %multiply_convert_fusion = bf16[1024,2048]{1,0:T(8,128)(2,1)S(1)} fusion(bf16[1024,2048]{1,0:T(8,128)(2,1)} %get-tuple-element.29, bf16[1024,1024]{1,0:T(8,128)(2,1)} %pad_maximum_fusion.4, bf16[1024,2048]{1,0:T(8,128)(2,1)} %all-gather.2.cloned.1.call-done), kind=kOutput, calls=%fused_computation.11 | convolution fusion | flops 4301258752 | bytes 14680064 | tf_op jit(solution)/shard_map/dot_general | solution.py:373
  204.8 7.1 %fusion.68 = bf16[512,1024]{1,0:T(8,128)(2,1)} fusion(bf16[1024,2816]{1,0:T(8,128)(2,1)} %bitcast.348, bf16[1024,2048]{1,0:T(8,128)(2,1)S(1)} %multiply_convert_fusion), kind=kOutput, calls=%fused_computation.113 | convolution fusion | flops 2148007936 | bytes 7340032 | tf_op jit(solution)/shard_map/dot_general | solution.py:161
  211.8 6.6 %convolution_convert_fusion.2 = bf16[1024,2048]{1,0:T(8,128)(2,1)S(1)} fusion(bf16[1024,2048]{1,0:T(8,128)(2,1)S(1)} %multiply_convert_fusion, bf16[512,1024]{1,0:T(8,128)(2,1)} %collective-permute-done.18, bf16[512,1024]{1,0:T(8,128)(2,1)} %fusion.30), kind=kOutput, calls=%fused_computation.18 | convolution fusion | flops 4301258752 | bytes 10485760 | tf_op jit(solution)/shard_map/dot_general | solution.py:367
  223.5 1.9 slice.118
  225.4 2.2 reshape.381
  229.3 6.9 %bitcast_multiply_fusion = (f32[512,1024]{1,0:T(8,128)S(1)}, f32[512,1024]{1,0:T(8,128)}) fusion(f32[8,1024]{1,0:T(8,128)S(1)} %get-tuple-element.76, bf16[512,1024]{1,0:T(8,128)(2,1)} %collective-permute-done.21, bf16[1024,2816]{1,0:T(8,128)(2,1)} %bitcast.350, bf16[1024,2048]{1,0:T(8,128)(2,1)} %copy-done.33), kind=kOutput, calls=%fused_computation.28 | convolution fusion | flops 2149056512 | bytes 11567104 | tf_op jit(solution)/shard_map/dot_general | solution.py:161
  242.1 11.2 %collective-permute-done.31 = bf16[4,2,64,1024]{3,2,0,1:T(8,128)(2,1)} collective-permute-done((bf16[4,2,64,1024]{3,2,0,1:T(8,128)(2,1)}, bf16[4,2,64,1024]{3,2,0,1:T(8,128)(2,1)}, u32[]{:S(2)}, u32[]{:S(2)}) %collective-permute-start.31) | collective-permute-done | bytes 1048608 | tf_op jit(solution)/shard_map/ppermute | solution.py:80
  255.9 18.6 %collective-permute-done.33 = bf16[4,2,64,1024]{3,2,0,1:T(8,128)(2,1)S(1)} collective-permute-done((bf16[4,2,64,1024]{3,2,0,1:T(8,128)(2,1)}, bf16[4,2,64,1024]{3,2,0,1:T(8,128)(2,1)S(1)}, u32[]{:S(2)}, u32[]{:S(2)}) %collective-permute-start.33) | collective-permute-done | bytes 1048608 | tf_op jit(solution)/shard_map/ppermute | solution.py:80
  276.1 2.8 collective-permute-start.34
  278.9 3.4 fusion.65
  282.4 15.4 %collective-permute-done.32 = bf16[4,64,1024]{2,1,0:T(8,128)(2,1)} collective-permute-done((bf16[4,64,1024]{2,1,0:T(8,128)(2,1)}, bf16[4,64,1024]{2,1,0:T(8,128)(2,1)}, u32[]{:S(2)}, u32[]{:S(2)}) %collective-permute-start.32) | collective-permute-done | bytes 524320 | tf_op jit(solution)/shard_map/ppermute | solution.py:80
  302.0 17.5 %collective-permute-start.37 = (bf16[64,2048]{1,0:T(8,128)(2,1)}, bf16[64,2048]{1,0:T(8,128)(2,1)}, u32[]{:S(2)}, u32[]{:S(2)}) collective-permute-start(bf16[64,2048]{1,0:T(8,128)(2,1)} %get-tuple-element.66), channel_id=1, source_target_pairs={{0,24},{2,26},{4,28},{6,30},{8,0},{10,2},{12,4},{14,6},{16,8},{18,... | collective-permute-start | bytes 786440 | tf_op jit(solution)/shard_map/ppermute | solution.py:80
  321.5 3.5 convolution_convert_fusion.5.grad_ref
  325.0 2.2 convolution_convert_fusion.4
  327.3 20.9 %attend_back.1 = bf16[1024,1536]{1,0:T(8,128)(2,1)} custom-call(bf16[1024,1536]{1,0:T(8,128)(2,1)} %convolution_convert_fusion.1.qkv_ref, bf16[1024,128]{1,0:T(8,128)(2,1)} %bitcast.367, bf16[1024,128]{1,0:T(8,128)(2,1)} %bitcast.369, f32[4,2,1024]{2,1,0:T(2,128)} %get-tuple-element.27.log_ref, bf16[1024,512]{1,0:T(8,128)(2,1)} %convolution_convert_fusion.5.grad_ref), custom_call_target="tpu_custom_call" | custom-call | flops 5368709120 | bytes 7340032 | tf_op jit(solution)/shard_map/attend_back/pallas_call | solution.py:267
  348.2 6.1 %convolution_convert_fusion = bf16[1024,1536]{1,0:T(8,128)(2,1)S(1)} fusion(bf16[1024,1024]{1,0:T(8,128)(2,1)} %copy-done.30, bf16[1024,1536]{1,0:T(8,128)(2,1)} %attend_back.1), kind=kOutput, calls=%fused_computation.16 | convolution fusion | flops 3222798336 | bytes 8388608 | tf_op jit(solution)/shard_map/dot_general | solution.py:367
  355.7 3.4 collective-permute-start.24
  364.4 2.0 fusion.84
  366.5 11.3 %collective-permute-done.24 = bf16[4,2,64,1024]{3,2,0,1:T(8,128)(2,1)S(1)} collective-permute-done((bf16[4,2,64,1024]{3,2,0,1:T(8,128)(2,1)S(1)}, bf16[4,2,64,1024]{3,2,0,1:T(8,128)(2,1)S(1)}, u32[]{:S(2)}, u32[]{:S(2)}) %collective-permute-start.24) | collective-permute-done | bytes 1048608 | tf_op jit(solution)/shard_map/ppermute | solution.py:80
  387.7 7.1 %fusion.17 = (bf16[1,512,1024]{2,1,0:T(8,128)(2,1)}, bf16[1,512,1024]{2,1,0:T(8,128)(2,1)}, f32[512,1024]{1,0:T(8,128)S(1)}) fusion(bf16[1,512,1024]{2,1,0:T(8,128)(2,1)S(1)} %copy-done, f32[512,1024]{1,0:T(8,128)S(1)} %get-tuple-element.96, f32[512,1024]{1,0:T(8,128)S(1)} %copy-done.5, f32[1,512,1024]{2,1,0:T(8,128)S(1)} %get-tuple-element.90, ...), kind=kOutput, calls=%fused_computation.44 | convolution fusion | flops 2159017984 | bytes 19972096 | tf_op jit(solution)/shard_map/dot_general | solution.py:161
  394.8 3.1 bitcast_reduce_fusion.1
  399.2 5.2 %collective-permute-start.39 = (bf16[16,3072]{1,0:T(8,128)(2,1)S(1)}, bf16[16,3072]{1,0:T(8,128)(2,1)S(1)}, u32[]{:S(2)}, u32[]{:S(2)}) collective-permute-start(bf16[16,3072]{1,0:T(8,128)(2,1)S(1)} %constant_dynamic-update-slice_fusion), channel_id=1, source_target_pairs={{0,8},{2,10},{4,12},{6,14},{8,16},{10,18},{12,20},{14,22},{16,24},... | collective-permute-start | bytes 294920 | tf_op jit(solution)/shard_map/ppermute | solution.py:80
  405.5 1.9 collective-permute-start.41
  408.4 4.0 collective-permute-done.40
  412.5 2.1 collective-permute-start.44
  414.7 4.8 %collective-permute-done.44 = bf16[4,16,1536]{2,1,0:T(8,128)(2,1)S(1)} collective-permute-done((bf16[4,16,1536]{2,1,0:T(8,128)(2,1)S(1)}, bf16[4,16,1536]{2,1,0:T(8,128)(2,1)S(1)}, u32[]{:S(2)}, u32[]{:S(2)}) %collective-permute-start.44) | collective-permute-done | bytes 196640 | tf_op jit(solution)/shard_map/ppermute | solution.py:80
  423.5 4.0 collective-permute-start.30
  428.2 1.8 collective-permute-done.45
  431.5 6.6 %fusion.125 = f32[1024,3072]{1,0:T(8,128)} fusion(bf16[256,1024]{1,0:T(8,128)(2,1)S(1)} %copy-done.27, bf16[256,3072]{1,0:T(8,128)(2,1)S(1)} %bitcast.357), kind=kOutput, calls=%fused_computation.288 | convolution fusion | flops 1610612736 | bytes 14680064 | tf_op jit(solution)/shard_map/dot_general | solution.py:367
  439.0 10.5 %collective-permute-done.29 = bf16[64,2048]{1,0:T(8,128)(2,1)S(1)} collective-permute-done((bf16[64,2048]{1,0:T(8,128)(2,1)S(1)}, bf16[64,2048]{1,0:T(8,128)(2,1)S(1)}, u32[]{:S(2)}, u32[]{:S(2)}) %collective-permute-start.29) | collective-permute-done | bytes 262176 | tf_op jit(solution)/shard_map/ppermute | solution.py:80
  (321 shorter events, 106.3 us)
Async XLA Ops:
  7.2 189.0 %all-gather.2.cloned.1.call-start = ((), (), s32[]{:S(2)}) async-start(), calls=%async_computation.1 | async-start | bytes 4456448 | tf_op jit(solution)/shard_map/all_gather | solution.py:320
  8.7 16.4 %collective-permute-start.3 = (bf16[64,1536]{1,0:T(8,128)(2,1)S(1)}, bf16[64,1536]{1,0:T(8,128)(2,1)S(1)}, u32[]{:S(2)}, u32[]{:S(2)}) collective-permute-start(bf16[64,1536]{1,0:T(8,128)(2,1)S(1)} %reshape.372), channel_id=1, source_target_pairs={{0,8},{2,10},{4,12},{6,14},{8,16},{10,18},{12,20},{14,22},{16,24},... | collective-permute-start | bytes 589832 | tf_op jit(solution)/shard_map/ppermute | solution.py:80
  11.8 15.5 %collective-permute-start.4 = (bf16[64,1536]{1,0:T(8,128)(2,1)S(1)}, bf16[64,1536]{1,0:T(8,128)(2,1)S(1)}, u32[]{:S(2)}, u32[]{:S(2)}) collective-permute-start(bf16[64,1536]{1,0:T(8,128)(2,1)S(1)} %reshape.372), channel_id=1, source_target_pairs={{0,16},{2,18},{4,20},{6,22},{8,24},{10,26},{12,28},{14,30},{16,0},... | collective-permute-start | bytes 589832 | tf_op jit(solution)/shard_map/ppermute | solution.py:80
  14.4 12.9 %collective-permute-start.5 = (bf16[64,1536]{1,0:T(8,128)(2,1)S(1)}, bf16[64,1536]{1,0:T(8,128)(2,1)S(1)}, u32[]{:S(2)}, u32[]{:S(2)}) collective-permute-start(bf16[64,1536]{1,0:T(8,128)(2,1)S(1)} %reshape.372), channel_id=1, source_target_pairs={{0,24},{2,26},{4,28},{6,30},{8,0},{10,2},{12,4},{14,6},{16,8},{18,... | collective-permute-start | bytes 589832 | tf_op jit(solution)/shard_map/ppermute | solution.py:80
  15.7 1.5 collective-permute-start
  21.5 1.5 collective-permute-start.1
  24.7 48.3 %collective-permute-start.2 = (bf16[512,1024]{1,0:T(8,128)(2,1)}, bf16[512,1024]{1,0:T(8,128)(2,1)}, u32[]{:S(2)}, u32[]{:S(2)}) collective-permute-start(bf16[512,1024]{1,0:T(8,128)(2,1)} %get-tuple-element.89), channel_id=1, source_target_pairs={{0,1},{1,0},{2,3},{3,2},{4,5},{5,4},{6,7},{7,6},{8,9},{9,8},{10,11... | collective-permute-start | bytes 3145736 | tf_op jit(solution)/shard_map/ppermute | solution.py:145
  27.3 15.5 %collective-permute-start.10 = (bf16[64,2816]{1,0:T(8,128)(2,1)}, bf16[64,2816]{1,0:T(8,128)(2,1)}, u32[]{:S(2)}, u32[]{:S(2)}) collective-permute-start(bf16[64,2816]{1,0:T(8,128)(2,1)} %pad_maximum_fusion.8), channel_id=1, source_target_pairs={{0,8},{2,10},{4,12},{6,14},{8,16},{10,18},{12,20},{14,22},{16,24},... | collective-permute-start | bytes 1081352 | tf_op jit(solution)/shard_map/ppermute | solution.py:80
  32.0 28.9 %collective-permute-start.11 = (bf16[64,2816]{1,0:T(8,128)(2,1)}, bf16[64,2816]{1,0:T(8,128)(2,1)}, u32[]{:S(2)}, u32[]{:S(2)}) collective-permute-start(bf16[64,2816]{1,0:T(8,128)(2,1)} %pad_maximum_fusion.8), channel_id=1, source_target_pairs={{0,16},{2,18},{4,20},{6,22},{8,24},{10,26},{12,28},{14,30},{16,0},... | collective-permute-start | bytes 1081352 | tf_op jit(solution)/shard_map/ppermute | solution.py:80
  33.7 28.2 %collective-permute-start.12 = (bf16[64,2816]{1,0:T(8,128)(2,1)}, bf16[64,2816]{1,0:T(8,128)(2,1)}, u32[]{:S(2)}, u32[]{:S(2)}) collective-permute-start(bf16[64,2816]{1,0:T(8,128)(2,1)} %pad_maximum_fusion.8), channel_id=1, source_target_pairs={{0,24},{2,26},{4,28},{6,30},{8,0},{10,2},{12,4},{14,6},{16,8},{18,... | collective-permute-start | bytes 1081352 | tf_op jit(solution)/shard_map/ppermute | solution.py:80
  35.4 35.0 %collective-permute-start.8 = (bf16[4,64,768]{2,1,0:T(8,128)(2,1)}, bf16[4,64,768]{2,1,0:T(8,128)(2,1)}, u32[]{:S(2)}, u32[]{:S(2)}) collective-permute-start(bf16[4,64,768]{2,1,0:T(8,128)(2,1)} %get-tuple-element.71), channel_id=1, source_target_pairs={{0,4},{2,6},{4,0},{6,2},{8,12},{10,14},{12,8},{14,10},{16,20},{18,... | collective-permute-start | bytes 1179656 | tf_op jit(solution)/shard_map/ppermute | solution.py:80
  38.0 413.7 %reduce-scatter.2.cloned.1.call-start = ((), (), s32[]{:S(2)}) async-start(), calls=%async_computation.2 | async-start | bytes 4456448 | tf_op jit(solution)/shard_map/reduce_scatter | solution.py:371
  42.8 29.2 %collective-permute-start.6 = (bf16[4,64,768]{2,1,0:T(8,128)(2,1)S(1)}, bf16[4,64,768]{2,1,0:T(8,128)(2,1)S(1)}, u32[]{:S(2)}, u32[]{:S(2)}) collective-permute-start(bf16[4,64,768]{2,1,0:T(8,128)(2,1)S(1)} %copy-done.38), channel_id=1, source_target_pairs={{0,2},{2,0},{4,6},{6,4},{8,10},{10,8},{12,14},{14,12},{16,18},{18,... | collective-permute-start | bytes 1179656 | tf_op jit(solution)/shard_map/ppermute | solution.py:80
  65.2 22.8 %collective-permute-start.15 = (bf16[4,64,1408]{2,1,0:T(8,128)(2,1)S(1)}, bf16[4,64,1408]{2,1,0:T(8,128)(2,1)S(1)}, u32[]{:S(2)}, u32[]{:S(2)}) collective-permute-start(bf16[4,64,1408]{2,1,0:T(8,128)(2,1)S(1)} %get-tuple-element.63), channel_id=1, source_target_pairs={{0,4},{2,6},{4,0},{6,2},{8,12},{10,14},{12,8},{14,10},{16,20},{18,... | collective-permute-start | bytes 2162696 | tf_op jit(solution)/shard_map/ppermute | solution.py:80
  68.9 26.5 %collective-permute-start.13 = (bf16[4,64,1408]{2,1,0:T(8,128)(2,1)S(1)}, bf16[4,64,1408]{2,1,0:T(8,128)(2,1)S(1)}, u32[]{:S(2)}, u32[]{:S(2)}) collective-permute-start(bf16[4,64,1408]{2,1,0:T(8,128)(2,1)S(1)} %get-tuple-element.62), channel_id=1, source_target_pairs={{0,2},{2,0},{4,6},{6,4},{8,10},{10,8},{12,14},{14,12},{16,18},{18,... | collective-permute-start | bytes 2162696 | tf_op jit(solution)/shard_map/ppermute | solution.py:80
  71.4 51.5 %collective-permute-start.9 = (bf16[4,2,64,768]{3,2,1,0:T(8,128)(2,1)S(1)}, bf16[4,2,64,768]{3,2,1,0:T(8,128)(2,1)S(1)}, u32[]{:S(2)}, u32[]{:S(2)}) collective-permute-start(bf16[4,2,64,768]{3,2,1,0:T(8,128)(2,1)S(1)} %bitcast_dynamic-update-slice_fusion.19), channel_id=1, source_target_pairs={{0,2},{2,0},{4,6},{6,4},{8,10},{10,8},{12,14},{14,12},{16,18},{18,... | collective-permute-start | bytes 2359304 | tf_op jit(solution)/shard_map/ppermute | solution.py:80
  72.0 51.0 %collective-permute-start.7 = (bf16[4,2,64,768]{3,2,1,0:T(8,128)(2,1)S(1)}, bf16[4,2,64,768]{3,2,1,0:T(8,128)(2,1)S(1)}, u32[]{:S(2)}, u32[]{:S(2)}) collective-permute-start(bf16[4,2,64,768]{3,2,1,0:T(8,128)(2,1)S(1)} %bitcast_dynamic-update-slice_fusion.16), channel_id=1, source_target_pairs={{0,4},{2,6},{4,0},{6,2},{8,12},{10,14},{12,8},{14,10},{16,20},{18,... | collective-permute-start | bytes 2359304 | tf_op jit(solution)/shard_map/ppermute | solution.py:80
  88.9 67.8 %collective-permute-start.16 = (bf16[4,2,64,1408]{3,2,1,0:T(8,128)(2,1)}, bf16[4,2,64,1408]{3,2,1,0:T(8,128)(2,1)S(1)}, u32[]{:S(2)}, u32[]{:S(2)}) collective-permute-start(bf16[4,2,64,1408]{3,2,1,0:T(8,128)(2,1)} %bitcast_dynamic-update-slice_fusion.11), channel_id=1, source_target_pairs={{0,2},{2,0},{4,6},{6,4},{8,10},{10,8},{12,14},{14,12},{16,18},{18,... | collective-permute-start | bytes 4325384 | tf_op jit(solution)/shard_map/ppermute | solution.py:80
  96.3 61.6 %collective-permute-start.14 = (bf16[4,2,64,1408]{3,2,1,0:T(8,128)(2,1)}, bf16[4,2,64,1408]{3,2,1,0:T(8,128)(2,1)}, u32[]{:S(2)}, u32[]{:S(2)}) collective-permute-start(bf16[4,2,64,1408]{3,2,1,0:T(8,128)(2,1)} %bitcast_dynamic-update-slice_fusion.9), channel_id=1, source_target_pairs={{0,4},{2,6},{4,0},{6,2},{8,12},{10,14},{12,8},{14,10},{16,20},{18,... | collective-permute-start | bytes 4325384 | tf_op jit(solution)/shard_map/ppermute | solution.py:80
  162.1 2.7 collective-permute-start.17
  164.0 6.5 %collective-permute-start.20 = (bf16[512,1024]{1,0:T(8,128)(2,1)}, bf16[512,1024]{1,0:T(8,128)(2,1)}, u32[]{:S(2)}, u32[]{:S(2)}) collective-permute-start(bf16[512,1024]{1,0:T(8,128)(2,1)} %fusion.28), channel_id=1, source_target_pairs={{0,1},{1,0},{2,3},{3,2},{4,5},{5,4},{6,7},{7,6},{8,9},{9,8},{10,11... | collective-permute-start | bytes 3145736 | tf_op jit(solution)/shard_map/ppermute | solution.py:145
  170.4 3.3 collective-permute-start.18
  222.5 6.8 %collective-permute-start.21 = (bf16[512,1024]{1,0:T(8,128)(2,1)}, bf16[512,1024]{1,0:T(8,128)(2,1)}, u32[]{:S(2)}, u32[]{:S(2)}) collective-permute-start(bf16[512,1024]{1,0:T(8,128)(2,1)} %fusion.68), channel_id=1, source_target_pairs={{0,1},{1,0},{2,3},{3,2},{4,5},{5,4},{6,7},{7,6},{8,9},{9,8},{10,11... | collective-permute-start | bytes 3145736 | tf_op jit(solution)/shard_map/ppermute | solution.py:145
  222.9 30.4 %collective-permute-start.31 = (bf16[4,2,64,1024]{3,2,0,1:T(8,128)(2,1)}, bf16[4,2,64,1024]{3,2,0,1:T(8,128)(2,1)}, u32[]{:S(2)}, u32[]{:S(2)}) collective-permute-start(bf16[4,2,64,1024]{3,2,0,1:T(8,128)(2,1)} %get-tuple-element.32), channel_id=1, source_target_pairs={{0,4},{2,6},{4,0},{6,2},{8,12},{10,14},{12,8},{14,10},{16,20},{18,... | collective-permute-start | bytes 3145736 | tf_op jit(solution)/shard_map/ppermute | solution.py:80
  227.7 46.8 %collective-permute-start.33 = (bf16[4,2,64,1024]{3,2,0,1:T(8,128)(2,1)}, bf16[4,2,64,1024]{3,2,0,1:T(8,128)(2,1)S(1)}, u32[]{:S(2)}, u32[]{:S(2)}) collective-permute-start(bf16[4,2,64,1024]{3,2,0,1:T(8,128)(2,1)} %get-tuple-element.34), channel_id=1, source_target_pairs={{0,2},{2,0},{4,6},{6,4},{8,10},{10,8},{12,14},{14,12},{16,18},{18,... | collective-permute-start | bytes 3145736 | tf_op jit(solution)/shard_map/ppermute | solution.py:80
  242.1 78.1 %collective-permute-start.22 = (bf16[512,1024]{1,0:T(8,128)(2,1)}, bf16[512,1024]{1,0:T(8,128)(2,1)}, u32[]{:S(2)}, u32[]{:S(2)}) collective-permute-start(bf16[512,1024]{1,0:T(8,128)(2,1)} %get-tuple-element.95), channel_id=1, source_target_pairs={{0,1},{1,0},{2,3},{3,2},{4,5},{5,4},{6,7},{7,6},{8,9},{9,8},{10,11... | collective-permute-start | bytes 3145736 | tf_op jit(solution)/shard_map/ppermute | solution.py:145
  255.9 42.0 %collective-permute-start.32 = (bf16[4,64,1024]{2,1,0:T(8,128)(2,1)}, bf16[4,64,1024]{2,1,0:T(8,128)(2,1)}, u32[]{:S(2)}, u32[]{:S(2)}) collective-permute-start(bf16[4,64,1024]{2,1,0:T(8,128)(2,1)} %dynamic-slice_bitcast_fusion.1), channel_id=1, source_target_pairs={{0,2},{2,0},{4,6},{6,4},{8,10},{10,8},{12,14},{14,12},{16,18},{18,... | collective-permute-start | bytes 1572872 | tf_op jit(solution)/shard_map/ppermute | solution.py:80
  276.1 23.2 %collective-permute-start.34 = (bf16[4,64,1024]{2,1,0:T(8,128)(2,1)}, bf16[4,64,1024]{2,1,0:T(8,128)(2,1)}, u32[]{:S(2)}, u32[]{:S(2)}) collective-permute-start(bf16[4,64,1024]{2,1,0:T(8,128)(2,1)} %dynamic-slice_bitcast_fusion), channel_id=1, source_target_pairs={{0,4},{2,6},{4,0},{6,2},{8,12},{10,14},{12,8},{14,10},{16,20},{18,... | collective-permute-start | bytes 1572872 | tf_op jit(solution)/shard_map/ppermute | solution.py:80
  302.0 61.8 %collective-permute-start.37 = (bf16[64,2048]{1,0:T(8,128)(2,1)}, bf16[64,2048]{1,0:T(8,128)(2,1)}, u32[]{:S(2)}, u32[]{:S(2)}) collective-permute-start(bf16[64,2048]{1,0:T(8,128)(2,1)} %get-tuple-element.66), channel_id=1, source_target_pairs={{0,24},{2,26},{4,28},{6,30},{8,0},{10,2},{12,4},{14,6},{16,8},{18,... | collective-permute-start | bytes 786440 | tf_op jit(solution)/shard_map/ppermute | solution.py:80
  319.5 44.4 %collective-permute-start.36 = (bf16[64,2048]{1,0:T(8,128)(2,1)}, bf16[64,2048]{1,0:T(8,128)(2,1)}, u32[]{:S(2)}, u32[]{:S(2)}) collective-permute-start(bf16[64,2048]{1,0:T(8,128)(2,1)} %get-tuple-element.65), channel_id=1, source_target_pairs={{0,16},{2,18},{4,20},{6,22},{8,24},{10,26},{12,28},{14,30},{16,0},... | collective-permute-start | bytes 786440 | tf_op jit(solution)/shard_map/ppermute | solution.py:80
  319.5 44.9 %collective-permute-start.35 = (bf16[64,2048]{1,0:T(8,128)(2,1)}, bf16[64,2048]{1,0:T(8,128)(2,1)}, u32[]{:S(2)}, u32[]{:S(2)}) collective-permute-start(bf16[64,2048]{1,0:T(8,128)(2,1)} %get-tuple-element.64), channel_id=1, source_target_pairs={{0,8},{2,10},{4,12},{6,14},{8,16},{10,18},{12,20},{14,22},{16,24},... | collective-permute-start | bytes 786440 | tf_op jit(solution)/shard_map/ppermute | solution.py:80
  355.7 22.0 %collective-permute-start.24 = (bf16[4,2,64,1024]{3,2,0,1:T(8,128)(2,1)S(1)}, bf16[4,2,64,1024]{3,2,0,1:T(8,128)(2,1)S(1)}, u32[]{:S(2)}, u32[]{:S(2)}) collective-permute-start(bf16[4,2,64,1024]{3,2,0,1:T(8,128)(2,1)S(1)} %bitcast.363), channel_id=1, source_target_pairs={{0,4},{2,6},{4,0},{6,2},{8,12},{10,14},{12,8},{14,10},{16,20},{18,... | collective-permute-start | bytes 3145736 | tf_op jit(solution)/shard_map/ppermute | solution.py:80
  359.4 21.3 %collective-permute-start.26 = (bf16[4,2,64,1024]{3,2,0,1:T(8,128)(2,1)S(1)}, bf16[4,2,64,1024]{3,2,0,1:T(8,128)(2,1)S(1)}, u32[]{:S(2)}, u32[]{:S(2)}) collective-permute-start(bf16[4,2,64,1024]{3,2,0,1:T(8,128)(2,1)S(1)} %bitcast.362), channel_id=1, source_target_pairs={{0,2},{2,0},{4,6},{6,4},{8,10},{10,8},{12,14},{14,12},{16,18},{18,... | collective-permute-start | bytes 3145736 | tf_op jit(solution)/shard_map/ppermute | solution.py:80
  363.8 22.7 %collective-permute-start.19 = (bf16[512,1024]{1,0:T(8,128)(2,1)S(1)}, bf16[512,1024]{1,0:T(8,128)(2,1)}, u32[]{:S(2)}, u32[]{:S(2)}) collective-permute-start(bf16[512,1024]{1,0:T(8,128)(2,1)S(1)} %copy-done.45), channel_id=1, source_target_pairs={{0,1},{1,0},{2,3},{3,2},{4,5},{5,4},{6,7},{7,6},{8,9},{9,8},{10,11... | collective-permute-start | bytes 3145736 | tf_op jit(solution)/shard_map/ppermute | solution.py:145
  363.9 19.6 %collective-permute-start.23 = (bf16[512,1024]{1,0:T(8,128)(2,1)S(1)}, bf16[512,1024]{1,0:T(8,128)(2,1)S(1)}, u32[]{:S(2)}, u32[]{:S(2)}) collective-permute-start(bf16[512,1024]{1,0:T(8,128)(2,1)S(1)} %fusion.62), channel_id=1, source_target_pairs={{0,1},{1,0},{2,3},{3,2},{4,5},{5,4},{6,7},{7,6},{8,9},{9,8},{10,11... | collective-permute-start | bytes 3145736 | tf_op jit(solution)/shard_map/ppermute | solution.py:145
  379.0 42.9 %collective-permute-start.25 = (bf16[4,64,1024]{2,1,0:T(8,128)(2,1)}, bf16[4,64,1024]{2,1,0:T(8,128)(2,1)S(1)}, u32[]{:S(2)}, u32[]{:S(2)}) collective-permute-start(bf16[4,64,1024]{2,1,0:T(8,128)(2,1)} %dynamic-slice_bitcast_fusion.3), channel_id=1, source_target_pairs={{0,2},{2,0},{4,6},{6,4},{8,10},{10,8},{12,14},{14,12},{16,18},{18,... | collective-permute-start | bytes 1572872 | tf_op jit(solution)/shard_map/ppermute | solution.py:80
  381.9 40.2 %collective-permute-start.27 = (bf16[4,64,1024]{2,1,0:T(8,128)(2,1)}, bf16[4,64,1024]{2,1,0:T(8,128)(2,1)}, u32[]{:S(2)}, u32[]{:S(2)}) collective-permute-start(bf16[4,64,1024]{2,1,0:T(8,128)(2,1)} %dynamic-slice_bitcast_fusion.2), channel_id=1, source_target_pairs={{0,4},{2,6},{4,0},{6,2},{8,12},{10,14},{12,8},{14,10},{16,20},{18,... | collective-permute-start | bytes 1572872 | tf_op jit(solution)/shard_map/ppermute | solution.py:80
  397.9 1.3 collective-permute-start.38
  399.2 9.2 %collective-permute-start.39 = (bf16[16,3072]{1,0:T(8,128)(2,1)S(1)}, bf16[16,3072]{1,0:T(8,128)(2,1)S(1)}, u32[]{:S(2)}, u32[]{:S(2)}) collective-permute-start(bf16[16,3072]{1,0:T(8,128)(2,1)S(1)} %constant_dynamic-update-slice_fusion), channel_id=1, source_target_pairs={{0,8},{2,10},{4,12},{6,14},{8,16},{10,18},{12,20},{14,22},{16,24},... | collective-permute-start | bytes 294920 | tf_op jit(solution)/shard_map/ppermute | solution.py:80
  404.4 8.0 %collective-permute-start.40 = (bf16[16,3072]{1,0:T(8,128)(2,1)S(1)}, bf16[16,3072]{1,0:T(8,128)(2,1)S(1)}, u32[]{:S(2)}, u32[]{:S(2)}) collective-permute-start(bf16[16,3072]{1,0:T(8,128)(2,1)S(1)} %constant_dynamic-update-slice_fusion), channel_id=1, source_target_pairs={{0,16},{2,18},{4,20},{6,22},{8,24},{10,26},{12,28},{14,30},{16,0},... | collective-permute-start | bytes 294920 | tf_op jit(solution)/shard_map/ppermute | solution.py:80
  405.5 6.9 %collective-permute-start.41 = (bf16[16,3072]{1,0:T(8,128)(2,1)S(1)}, bf16[16,3072]{1,0:T(8,128)(2,1)S(1)}, u32[]{:S(2)}, u32[]{:S(2)}) collective-permute-start(bf16[16,3072]{1,0:T(8,128)(2,1)S(1)} %constant_dynamic-update-slice_fusion), channel_id=1, source_target_pairs={{0,24},{2,26},{4,28},{6,30},{8,0},{10,2},{12,4},{14,6},{16,8},{18,... | collective-permute-start | bytes 294920 | tf_op jit(solution)/shard_map/ppermute | solution.py:80
  412.5 7.1 %collective-permute-start.44 = (bf16[4,16,1536]{2,1,0:T(8,128)(2,1)S(1)}, bf16[4,16,1536]{2,1,0:T(8,128)(2,1)S(1)}, u32[]{:S(2)}, u32[]{:S(2)}) collective-permute-start(bf16[4,16,1536]{2,1,0:T(8,128)(2,1)S(1)} %get-tuple-element.73), channel_id=1, source_target_pairs={{0,4},{2,6},{4,0},{6,2},{8,12},{10,14},{12,8},{14,10},{16,20},{18,... | collective-permute-start | bytes 589832 | tf_op jit(solution)/shard_map/ppermute | solution.py:80
  414.6 6.8 %collective-permute-start.42 = (bf16[4,16,1536]{2,1,0:T(8,128)(2,1)S(1)}, bf16[4,16,1536]{2,1,0:T(8,128)(2,1)S(1)}, u32[]{:S(2)}, u32[]{:S(2)}) collective-permute-start(bf16[4,16,1536]{2,1,0:T(8,128)(2,1)S(1)} %get-tuple-element.72), channel_id=1, source_target_pairs={{0,2},{2,0},{4,6},{6,4},{8,10},{10,8},{12,14},{14,12},{16,18},{18,... | collective-permute-start | bytes 589832 | tf_op jit(solution)/shard_map/ppermute | solution.py:80
  419.6 10.4 %collective-permute-start.45 = (bf16[4,2,16,1536]{3,2,1,0:T(8,128)(2,1)S(1)}, bf16[4,2,16,1536]{3,2,1,0:T(8,128)(2,1)S(1)}, u32[]{:S(2)}, u32[]{:S(2)}) collective-permute-start(bf16[4,2,16,1536]{3,2,1,0:T(8,128)(2,1)S(1)} %bitcast_dynamic-update-slice_fusion.27), channel_id=1, source_target_pairs={{0,2},{2,0},{4,6},{6,4},{8,10},{10,8},{12,14},{14,12},{16,18},{18,... | collective-permute-start | bytes 1179656 | tf_op jit(solution)/shard_map/ppermute | solution.py:80
  421.4 9.9 %collective-permute-start.43 = (bf16[4,2,16,1536]{3,2,1,0:T(8,128)(2,1)S(1)}, bf16[4,2,16,1536]{3,2,1,0:T(8,128)(2,1)S(1)}, u32[]{:S(2)}, u32[]{:S(2)}) collective-permute-start(bf16[4,2,16,1536]{3,2,1,0:T(8,128)(2,1)S(1)} %bitcast_dynamic-update-slice_fusion.25), channel_id=1, source_target_pairs={{0,4},{2,6},{4,0},{6,2},{8,12},{10,14},{12,8},{14,10},{16,20},{18,... | collective-permute-start | bytes 1179656 | tf_op jit(solution)/shard_map/ppermute | solution.py:80
  423.5 15.6 %collective-permute-start.30 = (bf16[64,2048]{1,0:T(8,128)(2,1)S(1)}, bf16[64,2048]{1,0:T(8,128)(2,1)S(1)}, u32[]{:S(2)}, u32[]{:S(2)}) collective-permute-start(bf16[64,2048]{1,0:T(8,128)(2,1)S(1)} %get-tuple-element.69), channel_id=1, source_target_pairs={{0,24},{2,26},{4,28},{6,30},{8,0},{10,2},{12,4},{14,6},{16,8},{18,... | collective-permute-start | bytes 786440 | tf_op jit(solution)/shard_map/ppermute | solution.py:80
  427.5 22.0 %collective-permute-start.29 = (bf16[64,2048]{1,0:T(8,128)(2,1)S(1)}, bf16[64,2048]{1,0:T(8,128)(2,1)S(1)}, u32[]{:S(2)}, u32[]{:S(2)}) collective-permute-start(bf16[64,2048]{1,0:T(8,128)(2,1)S(1)} %get-tuple-element.68), channel_id=1, source_target_pairs={{0,16},{2,18},{4,20},{6,22},{8,24},{10,26},{12,28},{14,30},{16,0},... | collective-permute-start | bytes 786440 | tf_op jit(solution)/shard_map/ppermute | solution.py:80
  427.6 21.9 %collective-permute-start.28 = (bf16[64,2048]{1,0:T(8,128)(2,1)S(1)}, bf16[64,2048]{1,0:T(8,128)(2,1)S(1)}, u32[]{:S(2)}, u32[]{:S(2)}) collective-permute-start(bf16[64,2048]{1,0:T(8,128)(2,1)S(1)} %get-tuple-element.67), channel_id=1, source_target_pairs={{0,8},{2,10},{4,12},{6,14},{8,16},{10,18},{12,20},{14,22},{16,24},... | collective-permute-start | bytes 786440 | tf_op jit(solution)/shard_map/ppermute | solution.py:80
  (47 other events, 391.2 us)
Sparse Core Ops, SparseCore 0:
  38.1 104.7 all-gather.1
  227.8 129.6 reduce-scatter.1

commit v2 on v1

--- a/solution.py
+++ b/solution.py
@@ -194,7 +194,8 @@
         out_ref[start:stop, :] = jnp.concatenate(parts, axis=0).T.astype(bf16)
 
 
-def backward_kernel(qkv_ref, seen_ref, frame_ref, log_ref, grad_ref, out_ref, key_sum, value_sum):
+def backward_kernel(qkv_ref, seen_ref, frame_ref, log_ref, grad_ref, *rest):
+    out_ref, key_sum, value_sum = rest[-3:]
     length = qkv_ref.shape[0]
     queries = qkv_ref[:, 0:PAIR] * jnp.asarray(HEAD**-0.5, bf16)
     keys = qkv_ref[:, PAIR : 2 * PAIR]
@@ -260,30 +261,34 @@
     )(qkv, seen, frames)
 
 
-def attend_back(qkv, seen, frames, logs, grads):
+def attend_back(qkv, seen, frames, logs, grads, first, pairs, into=None):
     length, cols = qkv.shape
-    pairs = cols // (3 * PAIR)
     whole = pl.BlockSpec((length, PAIR), lambda p: (0, 0))
+    operands = [qkv, seen, frames, logs, grads]
+    specs = [
+        pl.BlockSpec((length, 3 * PAIR), lambda p: (0, p + first)),
+        whole,
+        whole,
+        pl.BlockSpec((1, 2, length), lambda p: (p + first, 0, 0)),
+        pl.BlockSpec((length, PAIR), lambda p: (0, p + first)),
+    ]
+    if into is not None:
+        operands.append(into)
+        specs.append(pl.BlockSpec(memory_space=pl.ANY))
     return pl.pallas_call(
         backward_kernel,
         grid=(pairs,),
-        in_specs=[
-            pl.BlockSpec((length, 3 * PAIR), lambda p: (0, p)),
-            whole,
-            whole,
-            pl.BlockSpec((1, 2, length), lambda p: (p, 0, 0)),
-            pl.BlockSpec((length, PAIR), lambda p: (0, p)),
-        ],
-        out_specs=pl.BlockSpec((length, 3 * PAIR), lambda p: (0, p)),
-        out_shape=jax.ShapeDtypeStruct((length, pairs * 3 * PAIR), bf16),
+        in_specs=specs,
+        out_specs=pl.BlockSpec((length, 3 * PAIR), lambda p: (0, p + first)),
+        out_shape=jax.ShapeDtypeStruct((length, cols), bf16),
         scratch_shapes=[pltpu.VMEM((length, PAIR), f32), pltpu.VMEM((length, PAIR), f32)],
+        input_output_aliases={} if into is None else {5: 0},
         cost_estimate=pl.CostEstimate(
             flops=20 * pairs * length * length * HEAD,
             bytes_accessed=14 * pairs * length * PAIR,
             transcendentals=2 * pairs * length * length,
         ),
-        name="attend_back",
-    )(qkv, seen, frames, logs, grads)
+    )(*operands)
 
 
 def frame_lanes(per_frame):
@@ -301,16 +306,16 @@
     share = w_qkv.shape[0]
     head_cols = w_qkv.shape[2]
     pairs = head_cols // PAIR
+    hidden_cols = w_up.shape[1]
 
     qkv_share = (
         w_qkv.reshape(share, 3, pairs, PAIR).transpose(0, 2, 1, 3).reshape(share, 3 * head_cols)
     )
+    qkv_share = jnp.concatenate([qkv_share, w_out.T], axis=1)
     levels = in_order(noise_levels[0], swapped(noise_levels[0]), side)
     condition = noise_features(levels).astype(bf16)
     condition_cols = condition.size // share
-    rest_share = jnp.concatenate(
-        [w_out.T, condition.reshape(share, condition_cols), w_up], axis=1
-    )
+    rest_share = jnp.concatenate([w_up, condition.reshape(share, condition_cols)], axis=1)
     down_share = w_down.T
     qkv_deep = gather_deep(qkv_share, grid, at)
     rest_share, down_share, qkv_deep = lax.optimization_barrier(
@@ -319,9 +324,10 @@
     qkv_whole = gather_rest(qkv_deep, grid, at)
     down_whole = lax.all_gather(down_share, "rows", axis=0, tiled=True)
     rest_whole = gather_rest(gather_deep(rest_share, grid, at), grid, at)
-    out_whole = rest_whole[:, :head_cols]
-    up_whole = rest_whole[:, head_cols + condition_cols :]
-    condition_all = rest_whole[:, head_cols : head_cols + condition_cols].reshape(-1, width)
+    out_whole = qkv_whole[:, 3 * head_cols :]
+    qkv_whole = qkv_whole[:, : 3 * head_cols]
+    up_whole = rest_whole[:, :hidden_cols]
+    condition_all = rest_whole[:, hidden_cols:].reshape(-1, width)
 
     mod_cols = jnp.dot(condition, w_mod, preferred_element_type=f32) + b_mod.astype(f32)
     own_cols = half_of(mod_cols, side)
@@ -386,7 +392,9 @@
     branch_full = in_order(grad_branch, swapped(grad_branch), side)
     grad_out = tn(branch_full, attended).astype(bf16)
     grad_attended = jnp.dot(branch_full, out_whole, preferred_element_type=f32).astype(bf16)
-    grad_qkv = attend_back(qkv, seen, frames, logs, grad_attended)
+    part = pairs // 2
+    grad_qkv = attend_back(qkv, seen, frames, logs, grad_attended, 0, part)
+    grad_qkv = attend_back(qkv, seen, frames, logs, grad_attended, part, pairs - part, grad_qkv)
     grad_tail = jnp.concatenate([tn(first_full, grad_qkv).astype(bf16), grad_out], axis=1)
     tail_sum = scatter_rows(scatter_cut(grad_tail, grid, at), grid, at)
     qkv_sum, out_sum = tail_sum[:, : 3 * head_cols], tail_sum[:, 3 * head_cols :]

time: 468 us -> 484 us (1.034)
  starting transfers between devices: 70.7 us -> 86.9 us
  waiting for transfers between devices: 154 us -> 147 us
    ppermute x35, starting transfers between devices: 68.5 us -> 84.3 us  [moved(): return lax.ppermute(part, 'rows', shift_pairs(grid, axis, k))]
    ppermute x35, waiting for transfers between devices: 152 us -> 145 us  [moved(): return lax.ppermute(part, 'rows', shift_pairs(grid, axis, k))]
    unnamed x96 -> x124, local copies, waits for them, and re-layouts: 13.4 us -> 10 us
    pallas_call x1 -> x2, Pallas kernels: 20.9 us -> 23.6 us  [attend_back(): pl.pallas_call(backward_kernel, grid=(pairs,), in_specs=specs, out_specs=...]
    dynamic_update_slice x36 -> x35, local copies, waits for them, and re-layouts: 15.5 us -> 16.9 us  [gather_axis(): lax.dynamic_update_index_in_dim(whole, piece, (at[axis] - k) % count, dim)]
  transfers between devices with their start and end apart: 48 -> 48, of which waited for: 21 -> 20; matrix products, arithmetic and copies ran while one was open for 30% -> 31% of each run, Pallas kernels for 9% -> 9%
where the time goes in v2:
time: 484 us; the launch traced here: 477 us
  waiting for transfers between devices  147 us (30%)
  matrix products  92.9 us (19%)
  starting transfers between devices  86.9 us (18%)
  local copies, waits for them, and re-layouts  57.1 us (12%)
  Pallas kernels  42.1 us (9%)
  other arithmetic  35 us (7%)
  between operations  15.7 us (3%)
    ppermute x35, waiting for transfers between devices, moved(): return lax.ppermute(part, 'rows', shift_pairs(grid, axis, k))  145 us
    ppermute x35, starting transfers between devices, moved(): return lax.ppermute(part, 'rows', shift_pairs(grid, axis, k))  84.3 us
    dot_general x8, matrix products, nt(): lax.dot_general(a, b, (((1,), (1,)), ((), ())), preferred_element_type=f32)  33.6 us
    dot_general x5, matrix products, tn(): lax.dot_general(a, b, (((0,), (0,)), ((), ())), preferred_element_type=f32)  28.1 us
    pallas_call x2, Pallas kernels, attend_back(): pl.pallas_call(backward_kernel, grid=(pairs,), in_specs=specs, out_specs=...  23.6 us
    pallas_call x1, Pallas kernels, attend(): pl.pallas_call(forward_kernel, grid=(pairs,), in_specs=[pl.BlockSpec((len...  18.5 us
    dynamic_update_slice x35, local copies, waits for them, and re-layouts, gather_axis(): lax.dynamic_update_index_in_dim(whole, piece, (at[axis] - k) % count, dim)  16.9 us
    unnamed x124, local copies, waits for them, and re-layouts  10 us
  transfers between devices with their start and end apart: 48, of which 20 were waited for; matrix products, arithmetic and copies ran while one was open for 31% of the time, Pallas kernels for 9%

profile of v2, /device:TPU:0, one launch (start us, length us, event | category | flops | bytes accessed | tf_op | source)
XLA Modules:
  0.0 476.6 jit_solution(10502599952158175219)
XLA Ops:
  10.3 3.1 collective-permute-start.3
  13.4 2.6 collective-permute-start.4
  19.1 3.8 convolution_add_fusion
  29.6 3.7 collective-permute-done.4
  33.3 6.1 %collective-permute-start.12 = (bf16[64,2304]{1,0:T(8,128)(2,1)}, bf16[64,2304]{1,0:T(8,128)(2,1)}, u32[]{:S(2)}, u32[]{:S(2)}) collective-permute-start(bf16[64,2304]{1,0:T(8,128)(2,1)} %pad_maximum_fusion.8), channel_id=1, source_target_pairs={{0,8},{2,10},{4,12},{6,14},{8,16},{10,18},{12,20},{14,22},{16,24},... | collective-permute-start | bytes 884744 | tf_op jit(solution)/shard_map/ppermute | solution.py:80
  43.5 5.3 %collective-permute-done.12 = bf16[64,2304]{1,0:T(8,128)(2,1)} collective-permute-done((bf16[64,2304]{1,0:T(8,128)(2,1)}, bf16[64,2304]{1,0:T(8,128)(2,1)}, u32[]{:S(2)}, u32[]{:S(2)}) %collective-permute-start.12) | collective-permute-done | bytes 294944 | tf_op jit(solution)/shard_map/ppermute | solution.py:80
  51.3 12.1 %collective-permute-done.13 = bf16[64,2304]{1,0:T(8,128)(2,1)} collective-permute-done((bf16[64,2304]{1,0:T(8,128)(2,1)}, bf16[64,2304]{1,0:T(8,128)(2,1)}, u32[]{:S(2)}, u32[]{:S(2)}) %collective-permute-start.13) | collective-permute-done | bytes 294944 | tf_op jit(solution)/shard_map/ppermute | solution.py:80
  73.3 5.0 %collective-permute-done.6 = bf16[4,64,1024]{2,1,0:T(8,128)(2,1)S(1)} collective-permute-done((bf16[4,64,1024]{2,1,0:T(8,128)(2,1)S(1)}, bf16[4,64,1024]{2,1,0:T(8,128)(2,1)S(1)}, u32[]{:S(2)}, u32[]{:S(2)}) %collective-permute-start.6) | collective-permute-done | bytes 524320 | tf_op jit(solution)/shard_map/ppermute | solution.py:80
  80.5 7.2 %collective-permute-done.17 = bf16[4,64,1152]{2,1,0:T(8,128)(2,1)S(1)} collective-permute-done((bf16[4,64,1152]{2,1,0:T(8,128)(2,1)S(1)}, bf16[4,64,1152]{2,1,0:T(8,128)(2,1)S(1)}, u32[]{:S(2)}, u32[]{:S(2)}) %collective-permute-start.17) | collective-permute-done | bytes 589856 | tf_op jit(solution)/shard_map/ppermute | solution.py:80
  90.1 8.3 %collective-permute-done.15 = bf16[4,64,1152]{2,1,0:T(8,128)(2,1)S(1)} collective-permute-done((bf16[4,64,1152]{2,1,0:T(8,128)(2,1)S(1)}, bf16[4,64,1152]{2,1,0:T(8,128)(2,1)S(1)}, u32[]{:S(2)}, u32[]{:S(2)}) %collective-permute-start.15) | collective-permute-done | bytes 589856 | tf_op jit(solution)/shard_map/ppermute | solution.py:80
  105.5 28.3 %collective-permute-done.9 = bf16[4,2,64,1024]{3,2,1,0:T(8,128)(2,1)S(1)} collective-permute-done((bf16[4,2,64,1024]{3,2,1,0:T(8,128)(2,1)S(1)}, bf16[4,2,64,1024]{3,2,1,0:T(8,128)(2,1)S(1)}, u32[]{:S(2)}, u32[]{:S(2)}) %collective-permute-start.9) | collective-permute-done | bytes 1048608 | tf_op jit(solution)/shard_map/ppermute | solution.py:80
  134.6 5.4 %convolution_convert_fusion.1.qkv_ref = bf16[1024,1536]{1,0:T(8,128)(2,1)} fusion(bf16[1024,1024]{1,0:T(8,128)(2,1)S(1)} %constant_dynamic-update-slice_fusion.3, bf16[1024,2048]{1,0:T(8,128)(2,1)S(1)} %bitcast.349), kind=kOutput, calls=%fused_computation.18 | convolution fusion | flops 3222798336 | bytes 8388608 | tf_op jit(solution)/shard_map/dot_general | solution.py:357
  141.4 18.5 %attend.1 = (bf16[1024,512]{1,0:T(8,128)(2,1)}, f32[4,2,1024]{2,1,0:T(2,128)}) custom-call(bf16[1024,1536]{1,0:T(8,128)(2,1)} %convolution_convert_fusion.1.qkv_ref, bf16[1024,128]{1,0:T(8,128)(2,1)} %bitcast.359, bf16[1024,128]{1,0:T(8,128)(2,1)} %bitcast.362), custom_call_target="tpu_custom_call" | custom-call | flops 2147483648 | bytes 4194304 | tf_op jit(solution)/shard_map/attend/pallas_call | solution.py:243
  163.9 2.4 bitcast_dynamic-update-slice_fusion.2
  166.3 3.0 pad_maximum_fusion.4
  172.2 3.5 bitcast_add_fusion.2
  178.7 3.0 bitcast_dynamic-update-slice_fusion.1
  183.8 9.9 %fusion.8 = (bf16[1024,2048]{1,0:T(8,128)(2,1)}, bf16[1024,2048]{1,0:T(8,128)(2,1)S(1)}) fusion(bf16[1024,2304]{1,0:T(8,128)(2,1)S(1)} %bitcast.344, bf16[512,1024]{1,0:T(8,128)(2,1)S(1)} %collective-permute-done.11, bf16[512,1024]{1,0:T(8,128)(2,1)S(1)} %fusion.35), kind=kOutput, calls=%fused_computation.10 | convolution fusion | flops 4339007488 | bytes 14680064 | tf_op jit(solution)/shard_map/dot_general | solution.py:365
  195.7 7.9 %convolution_convert_fusion.3 = bf16[1024,2048]{1,0:T(8,128)(2,1)} fusion(bf16[1024,2048]{1,0:T(8,128)(2,1)S(1)} %get-tuple-element.25, bf16[512,1024]{1,0:T(8,128)(2,1)} %collective-permute-done.20, bf16[512,1024]{1,0:T(8,128)(2,1)} %fusion.33), kind=kOutput, calls=%fused_computation.20 | convolution fusion | flops 4301258752 | bytes 10485760 | tf_op jit(solution)/shard_map/dot_general | solution.py:373
  203.6 8.6 %multiply_convert_fusion = bf16[1024,2048]{1,0:T(8,128)(2,1)S(1)} fusion(bf16[1024,2048]{1,0:T(8,128)(2,1)} %get-tuple-element.29, bf16[1024,1024]{1,0:T(8,128)(2,1)} %pad_maximum_fusion.4, bf16[1024,2048]{1,0:T(8,128)(2,1)} %all-gather.2.cloned.1.call-done), kind=kOutput, calls=%fused_computation.11 | convolution fusion | flops 4301258752 | bytes 14680064 | tf_op jit(solution)/shard_map/dot_general | solution.py:379
  212.2 7.1 %fusion.75 = bf16[512,1024]{1,0:T(8,128)(2,1)} fusion(bf16[1024,2304]{1,0:T(8,128)(2,1)} %bitcast.345, bf16[1024,2048]{1,0:T(8,128)(2,1)S(1)} %multiply_convert_fusion), kind=kOutput, calls=%fused_computation.116 | convolution fusion | flops 2148007936 | bytes 7340032 | tf_op jit(solution)/shard_map/dot_general | solution.py:161
  219.3 5.2 %convolution_convert_fusion.2 = bf16[1024,2048]{1,0:T(8,128)(2,1)S(1)} fusion(bf16[1024,2048]{1,0:T(8,128)(2,1)S(1)} %multiply_convert_fusion, bf16[512,1024]{1,0:T(8,128)(2,1)S(1)} %copy-done.59, bf16[512,1024]{1,0:T(8,128)(2,1)S(1)} %copy-done.33), kind=kOutput, calls=%fused_computation.19 | convolution fusion | flops 4301258752 | bytes 10485760 | tf_op jit(solution)/shard_map/dot_general | solution.py:373
  236.0 2.5 collective-permute-start.33
  238.5 6.8 %bitcast_multiply_fusion = (f32[512,1024]{1,0:T(8,128)S(1)}, f32[512,1024]{1,0:T(8,128)}) fusion(f32[8,1024]{1,0:T(8,128)S(1)} %get-tuple-element.76, bf16[512,1024]{1,0:T(8,128)(2,1)} %collective-permute-done.21, bf16[1024,2304]{1,0:T(8,128)(2,1)} %bitcast.347, bf16[1024,2048]{1,0:T(8,128)(2,1)} %copy-done.34), kind=kOutput, calls=%fused_computation.28 | convolution fusion | flops 2149056512 | bytes 11567104 | tf_op jit(solution)/shard_map/dot_general | solution.py:161
  251.0 3.4 collective-permute-done.31
  257.0 4.1 collective-permute-start.32
  261.1 17.9 %collective-permute-done.33 = bf16[4,2,64,1024]{3,2,0,1:T(8,128)(2,1)S(1)} collective-permute-done((bf16[4,2,64,1024]{3,2,0,1:T(8,128)(2,1)}, bf16[4,2,64,1024]{3,2,0,1:T(8,128)(2,1)S(1)}, u32[]{:S(2)}, u32[]{:S(2)}) %collective-permute-start.33) | collective-permute-done | bytes 1048608 | tf_op jit(solution)/shard_map/ppermute | solution.py:80
  281.2 3.4 fusion.72
  285.9 16.7 %collective-permute-done.32 = bf16[4,64,1024]{2,1,0:T(8,128)(2,1)} collective-permute-done((bf16[4,64,1024]{2,1,0:T(8,128)(2,1)}, bf16[4,64,1024]{2,1,0:T(8,128)(2,1)}, u32[]{:S(2)}, u32[]{:S(2)}) %collective-permute-start.32) | collective-permute-done | bytes 524320 | tf_op jit(solution)/shard_map/ppermute | solution.py:80
  306.8 27.3 %collective-permute-start.37 = (bf16[64,2048]{1,0:T(8,128)(2,1)}, bf16[64,2048]{1,0:T(8,128)(2,1)S(1)}, u32[]{:S(2)}, u32[]{:S(2)}) collective-permute-start(bf16[64,2048]{1,0:T(8,128)(2,1)} %get-tuple-element.66), channel_id=1, source_target_pairs={{0,24},{2,26},{4,28},{6,30},{8,0},{10,2},{12,4},{14,6},{16,8},{18,... | collective-permute-start | bytes 786440 | tf_op jit(solution)/shard_map/ppermute | solution.py:80
  336.0 3.5 convolution_convert_fusion.5.grad_ref
  339.6 2.2 convolution_convert_fusion.4
  341.8 11.9 %shard_map.161.rest_0_ = bf16[1024,1536]{1,0:T(8,128)(2,1)} custom-call(bf16[1024,1536]{1,0:T(8,128)(2,1)} %convolution_convert_fusion.1.qkv_ref, bf16[1024,128]{1,0:T(8,128)(2,1)} %bitcast.360, bf16[1024,128]{1,0:T(8,128)(2,1)} %bitcast.363, f32[4,2,1024]{2,1,0:T(2,128)} %get-tuple-element.27.log_ref, bf16[1024,512]{1,0:T(8,128)(2,1)} %convolution_convert_fusion.5.grad_ref), custom_call_target="tpu_custom_call" | custom-call | flops 2684354560 | bytes 3670016 | tf_op jit(solution)/shard_map/pallas_call | solution.py:278
  353.7 11.6 %shard_map.162 = bf16[1024,1536]{1,0:T(8,128)(2,1)} custom-call(bf16[1024,1536]{1,0:T(8,128)(2,1)} %convolution_convert_fusion.1.qkv_ref, bf16[1024,128]{1,0:T(8,128)(2,1)} %bitcast.361, bf16[1024,128]{1,0:T(8,128)(2,1)} %bitcast.364, f32[4,2,1024]{2,1,0:T(2,128)} %get-tuple-element.27.log_ref, ...), custom_call_target="tpu_custom_call", output_to_operand_aliasing={{}: (5, {})} | custom-call | flops 2684354560 | bytes 3670016 | tf_op jit(solution)/shard_map/pallas_call | solution.py:278
  365.4 6.1 %convolution_convert_fusion = bf16[1024,1536]{1,0:T(8,128)(2,1)S(1)} fusion(bf16[1024,1024]{1,0:T(8,128)(2,1)} %copy-done.29, bf16[1024,1536]{1,0:T(8,128)(2,1)} %shard_map.162), kind=kOutput, calls=%fused_computation.17 | convolution fusion | flops 3222798336 | bytes 8388608 | tf_op jit(solution)/shard_map/dot_general | solution.py:373
  373.1 2.5 collective-permute-start.24
  382.2 12.0 %collective-permute-done.24 = bf16[4,2,64,1024]{3,2,0,1:T(8,128)(2,1)S(1)} collective-permute-done((bf16[4,2,64,1024]{3,2,0,1:T(8,128)(2,1)S(1)}, bf16[4,2,64,1024]{3,2,0,1:T(8,128)(2,1)S(1)}, u32[]{:S(2)}, u32[]{:S(2)}) %collective-permute-start.24) | collective-permute-done | bytes 1048608 | tf_op jit(solution)/shard_map/ppermute | solution.py:80
  395.4 2.7 collective-permute-start.25
  405.3 7.1 %fusion.22 = (bf16[1,512,1024]{2,1,0:T(8,128)(2,1)}, bf16[1,512,1024]{2,1,0:T(8,128)(2,1)}, f32[512,1024]{1,0:T(8,128)S(1)}) fusion(bf16[1,512,1024]{2,1,0:T(8,128)(2,1)S(1)} %copy-done, f32[512,1024]{1,0:T(8,128)S(1)} %get-tuple-element.96, f32[512,1024]{1,0:T(8,128)S(1)} %copy-done.5, f32[1,512,1024]{2,1,0:T(8,128)S(1)} %get-tuple-element.90, ...), kind=kOutput, calls=%fused_computation.49 | convolution fusion | flops 2159017984 | bytes 19972096 | tf_op jit(solution)/shard_map/dot_general | solution.py:161
  412.5 3.1 bitcast_reduce_fusion.1
  416.9 2.3 collective-permute-start.39
  421.7 2.7 collective-permute-done.39
  424.5 3.4 collective-permute-done.40
  430.7 4.1 collective-permute-done.44
  434.8 2.5 collective-permute-start.45
  439.5 2.7 collective-permute-start.30
  447.6 6.6 %fusion.132 = f32[1024,3072]{1,0:T(8,128)} fusion(bf16[256,1024]{1,0:T(8,128)(2,1)S(1)} %copy-done.26, bf16[256,3072]{1,0:T(8,128)(2,1)S(1)} %bitcast.356), kind=kOutput, calls=%fused_computation.292 | convolution fusion | flops 1610612736 | bytes 14680064 | tf_op jit(solution)/shard_map/dot_general | solution.py:373
  455.1 10.5 %collective-permute-done.29 = bf16[64,2048]{1,0:T(8,128)(2,1)S(1)} collective-permute-done((bf16[64,2048]{1,0:T(8,128)(2,1)S(1)}, bf16[64,2048]{1,0:T(8,128)(2,1)S(1)}, u32[]{:S(2)}, u32[]{:S(2)}) %collective-permute-start.29) | collective-permute-done | bytes 262176 | tf_op jit(solution)/shard_map/ppermute | solution.py:80
  (350 shorter events, 121.1 us)
Async XLA Ops:
  7.2 196.4 %all-gather.2.cloned.1.call-start = ((), (), s32[]{:S(2)}) async-start(), calls=%async_computation.1 | async-start | bytes 4456448 | tf_op jit(solution)/shard_map/all_gather | solution.py:325
  10.3 19.2 %collective-permute-start.3 = (bf16[64,2048]{1,0:T(8,128)(2,1)}, bf16[64,2048]{1,0:T(8,128)(2,1)S(1)}, u32[]{:S(2)}, u32[]{:S(2)}) collective-permute-start(bf16[64,2048]{1,0:T(8,128)(2,1)} %pad_maximum_fusion.9), channel_id=1, source_target_pairs={{0,8},{2,10},{4,12},{6,14},{8,16},{10,18},{12,20},{14,22},{16,24},... | collective-permute-start | bytes 786440 | tf_op jit(solution)/shard_map/ppermute | solution.py:80
  13.4 19.9 %collective-permute-start.4 = (bf16[64,2048]{1,0:T(8,128)(2,1)}, bf16[64,2048]{1,0:T(8,128)(2,1)S(1)}, u32[]{:S(2)}, u32[]{:S(2)}) collective-permute-start(bf16[64,2048]{1,0:T(8,128)(2,1)} %pad_maximum_fusion.9), channel_id=1, source_target_pairs={{0,16},{2,18},{4,20},{6,22},{8,24},{10,26},{12,28},{14,30},{16,0},... | collective-permute-start | bytes 786440 | tf_op jit(solution)/shard_map/ppermute | solution.py:80
  15.9 17.3 %collective-permute-start.5 = (bf16[64,2048]{1,0:T(8,128)(2,1)}, bf16[64,2048]{1,0:T(8,128)(2,1)S(1)}, u32[]{:S(2)}, u32[]{:S(2)}) collective-permute-start(bf16[64,2048]{1,0:T(8,128)(2,1)} %pad_maximum_fusion.9), channel_id=1, source_target_pairs={{0,24},{2,26},{4,28},{6,30},{8,0},{10,2},{12,4},{14,6},{16,8},{18,... | collective-permute-start | bytes 786440 | tf_op jit(solution)/shard_map/ppermute | solution.py:80
  17.3 1.3 collective-permute-start
  23.5 1.7 collective-permute-start.1
  27.5 75.1 %collective-permute-start.2 = (bf16[512,1024]{1,0:T(8,128)(2,1)}, bf16[512,1024]{1,0:T(8,128)(2,1)}, u32[]{:S(2)}, u32[]{:S(2)}) collective-permute-start(bf16[512,1024]{1,0:T(8,128)(2,1)} %get-tuple-element.89), channel_id=1, source_target_pairs={{0,1},{1,0},{2,3},{3,2},{4,5},{5,4},{6,7},{7,6},{8,9},{9,8},{10,11... | collective-permute-start | bytes 3145736 | tf_op jit(solution)/shard_map/ppermute | solution.py:145
  29.2 137.1 %collective-permute-start.20 = (bf16[512,1024]{1,0:T(8,128)(2,1)}, bf16[512,1024]{1,0:T(8,128)(2,1)}, u32[]{:S(2)}, u32[]{:S(2)}) collective-permute-start(bf16[512,1024]{1,0:T(8,128)(2,1)} %fusion.33), channel_id=1, source_target_pairs={{0,1},{1,0},{2,3},{3,2},{4,5},{5,4},{6,7},{7,6},{8,9},{9,8},{10,11... | collective-permute-start | bytes 3145736 | tf_op jit(solution)/shard_map/ppermute | solution.py:145
  33.3 15.5 %collective-permute-start.12 = (bf16[64,2304]{1,0:T(8,128)(2,1)}, bf16[64,2304]{1,0:T(8,128)(2,1)}, u32[]{:S(2)}, u32[]{:S(2)}) collective-permute-start(bf16[64,2304]{1,0:T(8,128)(2,1)} %pad_maximum_fusion.8), channel_id=1, source_target_pairs={{0,8},{2,10},{4,12},{6,14},{8,16},{10,18},{12,20},{14,22},{16,24},... | collective-permute-start | bytes 884744 | tf_op jit(solution)/shard_map/ppermute | solution.py:80
  39.4 24.0 %collective-permute-start.13 = (bf16[64,2304]{1,0:T(8,128)(2,1)}, bf16[64,2304]{1,0:T(8,128)(2,1)}, u32[]{:S(2)}, u32[]{:S(2)}) collective-permute-start(bf16[64,2304]{1,0:T(8,128)(2,1)} %pad_maximum_fusion.8), channel_id=1, source_target_pairs={{0,16},{2,18},{4,20},{6,22},{8,24},{10,26},{12,28},{14,30},{16,0},... | collective-permute-start | bytes 884744 | tf_op jit(solution)/shard_map/ppermute | solution.py:80
  41.1 24.8 %collective-permute-start.14 = (bf16[64,2304]{1,0:T(8,128)(2,1)}, bf16[64,2304]{1,0:T(8,128)(2,1)}, u32[]{:S(2)}, u32[]{:S(2)}) collective-permute-start(bf16[64,2304]{1,0:T(8,128)(2,1)} %pad_maximum_fusion.8), channel_id=1, source_target_pairs={{0,24},{2,26},{4,28},{6,30},{8,0},{10,2},{12,4},{14,6},{16,8},{18,... | collective-permute-start | bytes 884744 | tf_op jit(solution)/shard_map/ppermute | solution.py:80
  43.0 424.7 %reduce-scatter.2.cloned.1.call-start = ((), (), s32[]{:S(2)}) async-start(), calls=%async_computation.2 | async-start | bytes 4456448 | tf_op jit(solution)/shard_map/reduce_scatter | solution.py:377
  48.8 23.8 %collective-permute-start.8 = (bf16[4,64,1024]{2,1,0:T(8,128)(2,1)S(1)}, bf16[4,64,1024]{2,1,0:T(8,128)(2,1)S(1)}, u32[]{:S(2)}, u32[]{:S(2)}) collective-permute-start(bf16[4,64,1024]{2,1,0:T(8,128)(2,1)S(1)} %get-tuple-element.71), channel_id=1, source_target_pairs={{0,4},{2,6},{4,0},{6,2},{8,12},{10,14},{12,8},{14,10},{16,20},{18,... | collective-permute-start | bytes 1572872 | tf_op jit(solution)/shard_map/ppermute | solution.py:80
  63.5 14.8 %collective-permute-start.6 = (bf16[4,64,1024]{2,1,0:T(8,128)(2,1)S(1)}, bf16[4,64,1024]{2,1,0:T(8,128)(2,1)S(1)}, u32[]{:S(2)}, u32[]{:S(2)}) collective-permute-start(bf16[4,64,1024]{2,1,0:T(8,128)(2,1)S(1)} %get-tuple-element.70), channel_id=1, source_target_pairs={{0,2},{2,0},{4,6},{6,4},{8,10},{10,8},{12,14},{14,12},{16,18},{18,... | collective-permute-start | bytes 1572872 | tf_op jit(solution)/shard_map/ppermute | solution.py:80
  69.1 18.6 %collective-permute-start.17 = (bf16[4,64,1152]{2,1,0:T(8,128)(2,1)S(1)}, bf16[4,64,1152]{2,1,0:T(8,128)(2,1)S(1)}, u32[]{:S(2)}, u32[]{:S(2)}) collective-permute-start(bf16[4,64,1152]{2,1,0:T(8,128)(2,1)S(1)} %get-tuple-element.63), channel_id=1, source_target_pairs={{0,4},{2,6},{4,0},{6,2},{8,12},{10,14},{12,8},{14,10},{16,20},{18,... | collective-permute-start | bytes 1769480 | tf_op jit(solution)/shard_map/ppermute | solution.py:80
  72.6 25.7 %collective-permute-start.15 = (bf16[4,64,1152]{2,1,0:T(8,128)(2,1)S(1)}, bf16[4,64,1152]{2,1,0:T(8,128)(2,1)S(1)}, u32[]{:S(2)}, u32[]{:S(2)}) collective-permute-start(bf16[4,64,1152]{2,1,0:T(8,128)(2,1)S(1)} %get-tuple-element.62), channel_id=1, source_target_pairs={{0,2},{2,0},{4,6},{6,4},{8,10},{10,8},{12,14},{14,12},{16,18},{18,... | collective-permute-start | bytes 1769480 | tf_op jit(solution)/shard_map/ppermute | solution.py:80
  78.3 55.6 %collective-permute-start.9 = (bf16[4,2,64,1024]{3,2,1,0:T(8,128)(2,1)S(1)}, bf16[4,2,64,1024]{3,2,1,0:T(8,128)(2,1)S(1)}, u32[]{:S(2)}, u32[]{:S(2)}) collective-permute-start(bf16[4,2,64,1024]{3,2,1,0:T(8,128)(2,1)S(1)} %bitcast_dynamic-update-slice_fusion.15), channel_id=1, source_target_pairs={{0,2},{2,0},{4,6},{6,4},{8,10},{10,8},{12,14},{14,12},{16,18},{18,... | collective-permute-start | bytes 3145736 | tf_op jit(solution)/shard_map/ppermute | solution.py:80
  87.7 46.2 %collective-permute-start.7 = (bf16[4,2,64,1024]{3,2,1,0:T(8,128)(2,1)S(1)}, bf16[4,2,64,1024]{3,2,1,0:T(8,128)(2,1)S(1)}, u32[]{:S(2)}, u32[]{:S(2)}) collective-permute-start(bf16[4,2,64,1024]{3,2,1,0:T(8,128)(2,1)S(1)} %bitcast_dynamic-update-slice_fusion.13), channel_id=1, source_target_pairs={{0,4},{2,6},{4,0},{6,2},{8,12},{10,14},{12,8},{14,10},{16,20},{18,... | collective-permute-start | bytes 3145736 | tf_op jit(solution)/shard_map/ppermute | solution.py:80
  98.4 70.9 %collective-permute-start.18 = (bf16[4,2,64,1152]{3,2,1,0:T(8,128)(2,1)}, bf16[4,2,64,1152]{3,2,1,0:T(8,128)(2,1)}, u32[]{:S(2)}, u32[]{:S(2)}) collective-permute-start(bf16[4,2,64,1152]{3,2,1,0:T(8,128)(2,1)} %bitcast_dynamic-update-slice_fusion.11), channel_id=1, source_target_pairs={{0,2},{2,0},{4,6},{6,4},{8,10},{10,8},{12,14},{14,12},{16,18},{18,... | collective-permute-start | bytes 3538952 | tf_op jit(solution)/shard_map/ppermute | solution.py:80
  102.6 76.1 %collective-permute-start.16 = (bf16[4,2,64,1152]{3,2,1,0:T(8,128)(2,1)}, bf16[4,2,64,1152]{3,2,1,0:T(8,128)(2,1)}, u32[]{:S(2)}, u32[]{:S(2)}) collective-permute-start(bf16[4,2,64,1152]{3,2,1,0:T(8,128)(2,1)} %bitcast_dynamic-update-slice_fusion.9), channel_id=1, source_target_pairs={{0,4},{2,6},{4,0},{6,2},{8,12},{10,14},{12,8},{14,10},{16,20},{18,... | collective-permute-start | bytes 3538952 | tf_op jit(solution)/shard_map/ppermute | solution.py:80
  162.1 8.7 %collective-permute-start.10 = (bf16[512,1024]{1,0:T(8,128)(2,1)S(1)}, bf16[512,1024]{1,0:T(8,128)(2,1)S(1)}, u32[]{:S(2)}, u32[]{:S(2)}) collective-permute-start(bf16[512,1024]{1,0:T(8,128)(2,1)S(1)} %convolution_convert_fusion.6), channel_id=1, source_target_pairs={{0,1},{1,0},{2,3},{3,2},{4,5},{5,4},{6,7},{7,6},{8,9},{9,8},{10,11... | collective-permute-start | bytes 3145736 | tf_op jit(solution)/shard_map/ppermute | solution.py:145
  178.1 5.6 %collective-permute-start.11 = (bf16[512,1024]{1,0:T(8,128)(2,1)S(1)}, bf16[512,1024]{1,0:T(8,128)(2,1)S(1)}, u32[]{:S(2)}, u32[]{:S(2)}) collective-permute-start(bf16[512,1024]{1,0:T(8,128)(2,1)S(1)} %fusion.35), channel_id=1, source_target_pairs={{0,1},{1,0},{2,3},{3,2},{4,5},{5,4},{6,7},{7,6},{8,9},{9,8},{10,11... | collective-permute-start | bytes 3145736 | tf_op jit(solution)/shard_map/ppermute | solution.py:145
  228.5 9.9 %collective-permute-start.21 = (bf16[512,1024]{1,0:T(8,128)(2,1)}, bf16[512,1024]{1,0:T(8,128)(2,1)}, u32[]{:S(2)}, u32[]{:S(2)}) collective-permute-start(bf16[512,1024]{1,0:T(8,128)(2,1)} %fusion.75), channel_id=1, source_target_pairs={{0,1},{1,0},{2,3},{3,2},{4,5},{5,4},{6,7},{7,6},{8,9},{9,8},{10,11... | collective-permute-start | bytes 3145736 | tf_op jit(solution)/shard_map/ppermute | solution.py:145
  228.5 25.9 %collective-permute-start.31 = (bf16[4,2,64,1024]{3,2,0,1:T(8,128)(2,1)}, bf16[4,2,64,1024]{3,2,0,1:T(8,128)(2,1)}, u32[]{:S(2)}, u32[]{:S(2)}) collective-permute-start(bf16[4,2,64,1024]{3,2,0,1:T(8,128)(2,1)} %get-tuple-element.32), channel_id=1, source_target_pairs={{0,4},{2,6},{4,0},{6,2},{8,12},{10,14},{12,8},{14,10},{16,20},{18,... | collective-permute-start | bytes 3145736 | tf_op jit(solution)/shard_map/ppermute | solution.py:80
  236.0 42.9 %collective-permute-start.33 = (bf16[4,2,64,1024]{3,2,0,1:T(8,128)(2,1)}, bf16[4,2,64,1024]{3,2,0,1:T(8,128)(2,1)S(1)}, u32[]{:S(2)}, u32[]{:S(2)}) collective-permute-start(bf16[4,2,64,1024]{3,2,0,1:T(8,128)(2,1)} %get-tuple-element.34), channel_id=1, source_target_pairs={{0,2},{2,0},{4,6},{6,4},{8,10},{10,8},{12,14},{14,12},{16,18},{18,... | collective-permute-start | bytes 3145736 | tf_op jit(solution)/shard_map/ppermute | solution.py:80
  251.0 83.7 %collective-permute-start.22 = (bf16[512,1024]{1,0:T(8,128)(2,1)}, bf16[512,1024]{1,0:T(8,128)(2,1)}, u32[]{:S(2)}, u32[]{:S(2)}) collective-permute-start(bf16[512,1024]{1,0:T(8,128)(2,1)} %get-tuple-element.95), channel_id=1, source_target_pairs={{0,1},{1,0},{2,3},{3,2},{4,5},{5,4},{6,7},{7,6},{8,9},{9,8},{10,11... | collective-permute-start | bytes 3145736 | tf_op jit(solution)/shard_map/ppermute | solution.py:145
  257.0 45.7 %collective-permute-start.32 = (bf16[4,64,1024]{2,1,0:T(8,128)(2,1)}, bf16[4,64,1024]{2,1,0:T(8,128)(2,1)}, u32[]{:S(2)}, u32[]{:S(2)}) collective-permute-start(bf16[4,64,1024]{2,1,0:T(8,128)(2,1)} %dynamic-slice_bitcast_fusion.1), channel_id=1, source_target_pairs={{0,2},{2,0},{4,6},{6,4},{8,10},{10,8},{12,14},{14,12},{16,18},{18,... | collective-permute-start | bytes 1572872 | tf_op jit(solution)/shard_map/ppermute | solution.py:80
  280.6 23.5 %collective-permute-start.34 = (bf16[4,64,1024]{2,1,0:T(8,128)(2,1)}, bf16[4,64,1024]{2,1,0:T(8,128)(2,1)}, u32[]{:S(2)}, u32[]{:S(2)}) collective-permute-start(bf16[4,64,1024]{2,1,0:T(8,128)(2,1)} %dynamic-slice_bitcast_fusion), channel_id=1, source_target_pairs={{0,4},{2,6},{4,0},{6,2},{8,12},{10,14},{12,8},{14,10},{16,20},{18,... | collective-permute-start | bytes 1572872 | tf_op jit(solution)/shard_map/ppermute | solution.py:80
  306.8 72.9 %collective-permute-start.37 = (bf16[64,2048]{1,0:T(8,128)(2,1)}, bf16[64,2048]{1,0:T(8,128)(2,1)S(1)}, u32[]{:S(2)}, u32[]{:S(2)}) collective-permute-start(bf16[64,2048]{1,0:T(8,128)(2,1)} %get-tuple-element.66), channel_id=1, source_target_pairs={{0,24},{2,26},{4,28},{6,30},{8,0},{10,2},{12,4},{14,6},{16,8},{18,... | collective-permute-start | bytes 786440 | tf_op jit(solution)/shard_map/ppermute | solution.py:80
  334.1 45.6 %collective-permute-start.36 = (bf16[64,2048]{1,0:T(8,128)(2,1)}, bf16[64,2048]{1,0:T(8,128)(2,1)}, u32[]{:S(2)}, u32[]{:S(2)}) collective-permute-start(bf16[64,2048]{1,0:T(8,128)(2,1)} %get-tuple-element.65), channel_id=1, source_target_pairs={{0,16},{2,18},{4,20},{6,22},{8,24},{10,26},{12,28},{14,30},{16,0},... | collective-permute-start | bytes 786440 | tf_op jit(solution)/shard_map/ppermute | solution.py:80
  334.5 45.8 %collective-permute-start.35 = (bf16[64,2048]{1,0:T(8,128)(2,1)}, bf16[64,2048]{1,0:T(8,128)(2,1)}, u32[]{:S(2)}, u32[]{:S(2)}) collective-permute-start(bf16[64,2048]{1,0:T(8,128)(2,1)} %get-tuple-element.64), channel_id=1, source_target_pairs={{0,8},{2,10},{4,12},{6,14},{8,16},{10,18},{12,20},{14,22},{16,24},... | collective-permute-start | bytes 786440 | tf_op jit(solution)/shard_map/ppermute | solution.py:80
  373.1 21.1 %collective-permute-start.24 = (bf16[4,2,64,1024]{3,2,0,1:T(8,128)(2,1)S(1)}, bf16[4,2,64,1024]{3,2,0,1:T(8,128)(2,1)S(1)}, u32[]{:S(2)}, u32[]{:S(2)}) collective-permute-start(bf16[4,2,64,1024]{3,2,0,1:T(8,128)(2,1)S(1)} %bitcast.367), channel_id=1, source_target_pairs={{0,4},{2,6},{4,0},{6,2},{8,12},{10,14},{12,8},{14,10},{16,20},{18,... | collective-permute-start | bytes 3145736 | tf_op jit(solution)/shard_map/ppermute | solution.py:80
  375.9 23.2 %collective-permute-start.26 = (bf16[4,2,64,1024]{3,2,0,1:T(8,128)(2,1)S(1)}, bf16[4,2,64,1024]{3,2,0,1:T(8,128)(2,1)S(1)}, u32[]{:S(2)}, u32[]{:S(2)}) collective-permute-start(bf16[4,2,64,1024]{3,2,0,1:T(8,128)(2,1)S(1)} %bitcast.366), channel_id=1, source_target_pairs={{0,2},{2,0},{4,6},{6,4},{8,10},{10,8},{12,14},{14,12},{16,18},{18,... | collective-permute-start | bytes 3145736 | tf_op jit(solution)/shard_map/ppermute | solution.py:80
  379.7 24.6 %collective-permute-start.19 = (bf16[512,1024]{1,0:T(8,128)(2,1)S(1)}, bf16[512,1024]{1,0:T(8,128)(2,1)}, u32[]{:S(2)}, u32[]{:S(2)}) collective-permute-start(bf16[512,1024]{1,0:T(8,128)(2,1)S(1)} %copy-done.57), channel_id=1, source_target_pairs={{0,1},{1,0},{2,3},{3,2},{4,5},{5,4},{6,7},{7,6},{8,9},{9,8},{10,11... | collective-permute-start | bytes 3145736 | tf_op jit(solution)/shard_map/ppermute | solution.py:145
  379.8 21.2 %collective-permute-start.23 = (bf16[512,1024]{1,0:T(8,128)(2,1)S(1)}, bf16[512,1024]{1,0:T(8,128)(2,1)S(1)}, u32[]{:S(2)}, u32[]{:S(2)}) collective-permute-start(bf16[512,1024]{1,0:T(8,128)(2,1)S(1)} %fusion.67), channel_id=1, source_target_pairs={{0,1},{1,0},{2,3},{3,2},{4,5},{5,4},{6,7},{7,6},{8,9},{9,8},{10,11... | collective-permute-start | bytes 3145736 | tf_op jit(solution)/shard_map/ppermute | solution.py:145
  395.4 42.5 %collective-permute-start.25 = (bf16[4,64,1024]{2,1,0:T(8,128)(2,1)}, bf16[4,64,1024]{2,1,0:T(8,128)(2,1)S(1)}, u32[]{:S(2)}, u32[]{:S(2)}) collective-permute-start(bf16[4,64,1024]{2,1,0:T(8,128)(2,1)} %dynamic-slice_bitcast_fusion.3), channel_id=1, source_target_pairs={{0,2},{2,0},{4,6},{6,4},{8,10},{10,8},{12,14},{14,12},{16,18},{18,... | collective-permute-start | bytes 1572872 | tf_op jit(solution)/shard_map/ppermute | solution.py:80
  400.4 37.8 %collective-permute-start.27 = (bf16[4,64,1024]{2,1,0:T(8,128)(2,1)}, bf16[4,64,1024]{2,1,0:T(8,128)(2,1)}, u32[]{:S(2)}, u32[]{:S(2)}) collective-permute-start(bf16[4,64,1024]{2,1,0:T(8,128)(2,1)} %dynamic-slice_bitcast_fusion.2), channel_id=1, source_target_pairs={{0,4},{2,6},{4,0},{6,2},{8,12},{10,14},{12,8},{14,10},{16,20},{18,... | collective-permute-start | bytes 1572872 | tf_op jit(solution)/shard_map/ppermute | solution.py:80
  415.6 1.3 collective-permute-start.38
  416.9 7.6 %collective-permute-start.39 = (bf16[16,3072]{1,0:T(8,128)(2,1)S(1)}, bf16[16,3072]{1,0:T(8,128)(2,1)S(1)}, u32[]{:S(2)}, u32[]{:S(2)}) collective-permute-start(bf16[16,3072]{1,0:T(8,128)(2,1)S(1)} %constant_dynamic-update-slice_fusion), channel_id=1, source_target_pairs={{0,8},{2,10},{4,12},{6,14},{8,16},{10,18},{12,20},{14,22},{16,24},... | collective-permute-start | bytes 294920 | tf_op jit(solution)/shard_map/ppermute | solution.py:80
  419.2 8.7 %collective-permute-start.40 = (bf16[16,3072]{1,0:T(8,128)(2,1)S(1)}, bf16[16,3072]{1,0:T(8,128)(2,1)S(1)}, u32[]{:S(2)}, u32[]{:S(2)}) collective-permute-start(bf16[16,3072]{1,0:T(8,128)(2,1)S(1)} %constant_dynamic-update-slice_fusion), channel_id=1, source_target_pairs={{0,16},{2,18},{4,20},{6,22},{8,24},{10,26},{12,28},{14,30},{16,0},... | collective-permute-start | bytes 294920 | tf_op jit(solution)/shard_map/ppermute | solution.py:80
  420.9 7.0 %collective-permute-start.41 = (bf16[16,3072]{1,0:T(8,128)(2,1)S(1)}, bf16[16,3072]{1,0:T(8,128)(2,1)S(1)}, u32[]{:S(2)}, u32[]{:S(2)}) collective-permute-start(bf16[16,3072]{1,0:T(8,128)(2,1)S(1)} %constant_dynamic-update-slice_fusion), channel_id=1, source_target_pairs={{0,24},{2,26},{4,28},{6,30},{8,0},{10,2},{12,4},{14,6},{16,8},{18,... | collective-permute-start | bytes 294920 | tf_op jit(solution)/shard_map/ppermute | solution.py:80
  428.0 6.8 %collective-permute-start.44 = (bf16[4,16,1536]{2,1,0:T(8,128)(2,1)S(1)}, bf16[4,16,1536]{2,1,0:T(8,128)(2,1)S(1)}, u32[]{:S(2)}, u32[]{:S(2)}) collective-permute-start(bf16[4,16,1536]{2,1,0:T(8,128)(2,1)S(1)} %get-tuple-element.73), channel_id=1, source_target_pairs={{0,4},{2,6},{4,0},{6,2},{8,12},{10,14},{12,8},{14,10},{16,20},{18,... | collective-permute-start | bytes 589832 | tf_op jit(solution)/shard_map/ppermute | solution.py:80
  429.5 7.9 %collective-permute-start.42 = (bf16[4,16,1536]{2,1,0:T(8,128)(2,1)S(1)}, bf16[4,16,1536]{2,1,0:T(8,128)(2,1)S(1)}, u32[]{:S(2)}, u32[]{:S(2)}) collective-permute-start(bf16[4,16,1536]{2,1,0:T(8,128)(2,1)S(1)} %get-tuple-element.72), channel_id=1, source_target_pairs={{0,2},{2,0},{4,6},{6,4},{8,10},{10,8},{12,14},{14,12},{16,18},{18,... | collective-permute-start | bytes 589832 | tf_op jit(solution)/shard_map/ppermute | solution.py:80
  434.8 10.9 %collective-permute-start.45 = (bf16[4,2,16,1536]{3,2,1,0:T(8,128)(2,1)S(1)}, bf16[4,2,16,1536]{3,2,1,0:T(8,128)(2,1)S(1)}, u32[]{:S(2)}, u32[]{:S(2)}) collective-permute-start(bf16[4,2,16,1536]{3,2,1,0:T(8,128)(2,1)S(1)} %bitcast_dynamic-update-slice_fusion.31), channel_id=1, source_target_pairs={{0,2},{2,0},{4,6},{6,4},{8,10},{10,8},{12,14},{14,12},{16,18},{18,... | collective-permute-start | bytes 1179656 | tf_op jit(solution)/shard_map/ppermute | solution.py:80
  437.5 9.9 %collective-permute-start.43 = (bf16[4,2,16,1536]{3,2,1,0:T(8,128)(2,1)S(1)}, bf16[4,2,16,1536]{3,2,1,0:T(8,128)(2,1)S(1)}, u32[]{:S(2)}, u32[]{:S(2)}) collective-permute-start(bf16[4,2,16,1536]{3,2,1,0:T(8,128)(2,1)S(1)} %bitcast_dynamic-update-slice_fusion.29), channel_id=1, source_target_pairs={{0,4},{2,6},{4,0},{6,2},{8,12},{10,14},{12,8},{14,10},{16,20},{18,... | collective-permute-start | bytes 1179656 | tf_op jit(solution)/shard_map/ppermute | solution.py:80
  439.5 15.6 %collective-permute-start.30 = (bf16[64,2048]{1,0:T(8,128)(2,1)S(1)}, bf16[64,2048]{1,0:T(8,128)(2,1)S(1)}, u32[]{:S(2)}, u32[]{:S(2)}) collective-permute-start(bf16[64,2048]{1,0:T(8,128)(2,1)S(1)} %get-tuple-element.69), channel_id=1, source_target_pairs={{0,24},{2,26},{4,28},{6,30},{8,0},{10,2},{12,4},{14,6},{16,8},{18,... | collective-permute-start | bytes 786440 | tf_op jit(solution)/shard_map/ppermute | solution.py:80
  442.2 23.4 %collective-permute-start.29 = (bf16[64,2048]{1,0:T(8,128)(2,1)S(1)}, bf16[64,2048]{1,0:T(8,128)(2,1)S(1)}, u32[]{:S(2)}, u32[]{:S(2)}) collective-permute-start(bf16[64,2048]{1,0:T(8,128)(2,1)S(1)} %get-tuple-element.68), channel_id=1, source_target_pairs={{0,16},{2,18},{4,20},{6,22},{8,24},{10,26},{12,28},{14,30},{16,0},... | collective-permute-start | bytes 786440 | tf_op jit(solution)/shard_map/ppermute | solution.py:80
  443.7 21.9 %collective-permute-start.28 = (bf16[64,2048]{1,0:T(8,128)(2,1)S(1)}, bf16[64,2048]{1,0:T(8,128)(2,1)S(1)}, u32[]{:S(2)}, u32[]{:S(2)}) collective-permute-start(bf16[64,2048]{1,0:T(8,128)(2,1)S(1)} %get-tuple-element.67), channel_id=1, source_target_pairs={{0,8},{2,10},{4,12},{6,14},{8,16},{10,18},{12,20},{14,22},{16,24},... | collective-permute-start | bytes 786440 | tf_op jit(solution)/shard_map/ppermute | solution.py:80
  (61 other events, 462.2 us)
Sparse Core Ops, SparseCore 0:
  43.1 105.9 all-gather.1
  236.1 135.5 reduce-scatter.1

commit v3 on v2

--- a/solution.py
+++ b/solution.py
@@ -110,16 +110,16 @@
     ]
 
 
-def sum_pieces(pieces, grid, axis):
+def sum_pieces(pieces, grid, axis, kept=bf16):
     come = [moved(pieces[k], grid, axis, k) for k in range(1, grid[axis])]
     total = pieces[0].astype(f32)
     for piece in come:
         total = total + piece.astype(f32)
-    return total
-
-
-def scatter_axis(whole, grid, axis, at, dim):
-    return sum_pieces(pieces_of(whole, grid, axis, at, dim), grid, axis)
+    return total.astype(kept)
+
+
+def scatter_axis(whole, grid, axis, at, dim, kept=bf16):
+    return sum_pieces(pieces_of(whole, grid, axis, at, dim), grid, axis, kept)
 
 
 def scatter_cut(whole, grid, at):
@@ -133,12 +133,12 @@
 
 
 def scatter_rows(cuts, grid, at):
-    first = sum_pieces(cuts[0], grid, 1).astype(bf16)
-    second = sum_pieces(cuts[1], grid, 2).astype(bf16)
-    first = scatter_axis(first, grid, 2, at, 1).astype(bf16)
-    second = scatter_axis(second, grid, 1, at, 1).astype(bf16)
+    first = sum_pieces(cuts[0], grid, 1)
+    second = sum_pieces(cuts[1], grid, 2)
+    first = scatter_axis(first, grid, 2, at, 1)
+    second = scatter_axis(second, grid, 1, at, 1)
     both = jnp.concatenate([first, second], axis=-1)
-    return scatter_axis(both, grid, 0, at, 0)
+    return scatter_axis(both, grid, 0, at, 0, f32)
 
 
 def swapped(part):
@@ -170,7 +170,8 @@
     return (lanes // HEAD) == head
 
 
-def forward_kernel(qkv_ref, seen_ref, frame_ref, out_ref, log_ref):
+def forward_kernel(qkv_ref, seen_ref, frame_ref, *rest):
+    out_ref, log_ref = rest[-2:]
     length = qkv_ref.shape[0]
     queries = qkv_ref[:, 0:PAIR] * jnp.asarray(HEAD**-0.5, bf16)
     keys = qkv_ref[:, PAIR : 2 * PAIR]
@@ -236,29 +237,30 @@
     out_ref[:, 2 * PAIR : 3 * PAIR] = value_sum[...].astype(bf16)
 
 
-def attend(qkv, seen, frames):
+def attend(qkv, seen, frames, first, pairs, into=()):
     length, cols = qkv.shape
-    pairs = cols // (3 * PAIR)
+    every = cols // (3 * PAIR)
     whole = pl.BlockSpec((length, PAIR), lambda p: (0, 0))
     return pl.pallas_call(
         forward_kernel,
         grid=(pairs,),
-        in_specs=[pl.BlockSpec((length, 3 * PAIR), lambda p: (0, p)), whole, whole],
+        in_specs=[pl.BlockSpec((length, 3 * PAIR), lambda p: (0, p + first)), whole, whole]
+        + [pl.BlockSpec(memory_space=pl.ANY) for _ in into],
         out_specs=[
-            pl.BlockSpec((length, PAIR), lambda p: (0, p)),
-            pl.BlockSpec((1, 2, length), lambda p: (p, 0, 0)),
+            pl.BlockSpec((length, PAIR), lambda p: (0, p + first)),
+            pl.BlockSpec((1, 2, length), lambda p: (p + first, 0, 0)),
         ],
         out_shape=[
-            jax.ShapeDtypeStruct((length, pairs * PAIR), bf16),
-            jax.ShapeDtypeStruct((pairs, 2, length), f32),
+            jax.ShapeDtypeStruct((length, every * PAIR), bf16),
+            jax.ShapeDtypeStruct((every, 2, length), f32),
         ],
+        input_output_aliases={3 + k: k for k in range(len(into))},
         cost_estimate=pl.CostEstimate(
             flops=8 * pairs * length * length * HEAD,
             bytes_accessed=8 * pairs * length * PAIR,
             transcendentals=2 * pairs * length * length,
         ),
-        name="attend",
-    )(qkv, seen, frames)
+    )(qkv, seen, frames, *into)
 
 
 def attend_back(qkv, seen, frames, logs, grads, first, pairs, into=None):
@@ -318,9 +320,7 @@
     rest_share = jnp.concatenate([w_up, condition.reshape(share, condition_cols)], axis=1)
     down_share = w_down.T
     qkv_deep = gather_deep(qkv_share, grid, at)
-    rest_share, down_share, qkv_deep = lax.optimization_barrier(
-        (rest_share, down_share, qkv_deep)
-    )
+    rest_share, qkv_deep = lax.optimization_barrier((rest_share, qkv_deep))
     qkv_whole = gather_rest(qkv_deep, grid, at)
     down_whole = lax.all_gather(down_share, "rows", axis=0, tiled=True)
     rest_whole = gather_rest(gather_deep(rest_share, grid, at), grid, at)
@@ -355,7 +355,9 @@
     frames = frame_lanes(jnp.eye(clip.shape[0]))
 
     qkv = jnp.dot(first_full, qkv_whole, preferred_element_type=f32).astype(bf16)
-    attended, logs = attend(qkv, seen, frames)
+    part = pairs // 2
+    into = attend(qkv, seen, frames, 0, part)
+    attended, logs = attend(qkv, seen, frames, part, pairs - part, into)
     branch_other = swapped(nt(half_of(attended, 1 - side), out_whole).astype(bf16))
     branch = nt(half_of(attended, side), out_whole) + branch_other.astype(f32)
     branch = branch.reshape(framed.shape)
@@ -392,7 +394,6 @@
     branch_full = in_order(grad_branch, swapped(grad_branch), side)
     grad_out = tn(branch_full, attended).astype(bf16)
     grad_attended = jnp.dot(branch_full, out_whole, preferred_element_type=f32).astype(bf16)
-    part = pairs // 2
     grad_qkv = attend_back(qkv, seen, frames, logs, grad_attended, 0, part)
     grad_qkv = attend_back(qkv, seen, frames, logs, grad_attended, part, pairs - part, grad_qkv)
     grad_tail = jnp.concatenate([tn(first_full, grad_qkv).astype(bf16), grad_out], axis=1)

time: 484 us -> 489 us (1.010)
  waiting for transfers between devices: 147 us -> 160 us
  starting transfers between devices: 86.9 us -> 82 us
    ppermute x35, waiting for transfers between devices: 145 us -> 158 us  [moved(): return lax.ppermute(part, 'rows', shift_pairs(grid, axis, k))]
    ppermute x35, starting transfers between devices: 84.3 us -> 79.3 us  [moved(): return lax.ppermute(part, 'rows', shift_pairs(grid, axis, k))]
    pallas_call x1 -> x2, Pallas kernels: 18.5 us -> 20.5 us  [attend(): pl.pallas_call(forward_kernel, grid=(pairs,), in_specs=[pl.BlockSpec((len...]
    unnamed x124 -> x120, local copies, waits for them, and re-layouts: 10 us -> 10.4 us
  transfers between devices with their start and end apart: 48 -> 48, of which waited for: 20 -> 19; matrix products, arithmetic and copies ran while one was open for 31% -> 29% of each run, Pallas kernels for 9% -> 9%
where the time goes in v3:
time: 489 us; the launch traced here: 482 us
  waiting for transfers between devices  160 us (33%)
  matrix products  92.9 us (19%)
  starting transfers between devices  82 us (17%)
  local copies, waits for them, and re-layouts  54 us (11%)
  Pallas kernels  43.7 us (9%)
  other arithmetic  33.2 us (7%)
  between operations  16 us (3%)
    ppermute x35, waiting for transfers between devices, moved(): return lax.ppermute(part, 'rows', shift_pairs(grid, axis, k))  158 us
    ppermute x35, starting transfers between devices, moved(): return lax.ppermute(part, 'rows', shift_pairs(grid, axis, k))  79.3 us
    dot_general x8, matrix products, nt(): lax.dot_general(a, b, (((1,), (1,)), ((), ())), preferred_element_type=f32)  33.6 us
    dot_general x5, matrix products, tn(): lax.dot_general(a, b, (((0,), (0,)), ((), ())), preferred_element_type=f32)  28 us
    pallas_call x2, Pallas kernels, attend_back(): pl.pallas_call(backward_kernel, grid=(pairs,), in_specs=specs, out_specs=...  23.2 us
    pallas_call x2, Pallas kernels, attend(): pl.pallas_call(forward_kernel, grid=(pairs,), in_specs=[pl.BlockSpec((len...  20.5 us
    dynamic_update_slice x35, local copies, waits for them, and re-layouts, gather_axis(): lax.dynamic_update_index_in_dim(whole, piece, (at[axis] - k) % count, dim)  13.7 us
    unnamed x120, local copies, waits for them, and re-layouts  10.4 us
  transfers between devices with their start and end apart: 48, of which 19 were waited for; matrix products, arithmetic and copies ran while one was open for 29% of the time, Pallas kernels for 9%

profile of v3, /device:TPU:0, one launch (start us, length us, event | category | flops | bytes accessed | tf_op | source)
XLA Modules:
  0.0 482.0 jit_solution(10232783822277252489)
XLA Ops:
  10.3 3.1 collective-permute-start.3
  13.4 2.6 collective-permute-start.4
  19.4 3.8 convolution_add_fusion
  31.1 5.9 %collective-permute-done.4 = bf16[64,2048]{1,0:T(8,128)(2,1)S(1)} collective-permute-done((bf16[64,2048]{1,0:T(8,128)(2,1)}, bf16[64,2048]{1,0:T(8,128)(2,1)S(1)}, u32[]{:S(2)}, u32[]{:S(2)}) %collective-permute-start.4) | collective-permute-done | bytes 262176 | tf_op jit(solution)/shard_map/ppermute | solution.py:80
  37.1 8.0 %collective-permute-start.12 = (bf16[64,2304]{1,0:T(8,128)(2,1)S(1)}, bf16[64,2304]{1,0:T(8,128)(2,1)S(1)}, u32[]{:S(2)}, u32[]{:S(2)}) collective-permute-start(bf16[64,2304]{1,0:T(8,128)(2,1)S(1)} %pad_maximum_fusion.8), channel_id=1, source_target_pairs={{0,8},{2,10},{4,12},{6,14},{8,16},{10,18},{12,20},{14,22},{16,24},... | collective-permute-start | bytes 884744 | tf_op jit(solution)/shard_map/ppermute | solution.py:80
  48.1 8.3 %collective-permute-done.12 = bf16[64,2304]{1,0:T(8,128)(2,1)S(1)} collective-permute-done((bf16[64,2304]{1,0:T(8,128)(2,1)S(1)}, bf16[64,2304]{1,0:T(8,128)(2,1)S(1)}, u32[]{:S(2)}, u32[]{:S(2)}) %collective-permute-start.12) | collective-permute-done | bytes 294944 | tf_op jit(solution)/shard_map/ppermute | solution.py:80
  57.7 18.5 %collective-permute-done.13 = bf16[64,2304]{1,0:T(8,128)(2,1)S(1)} collective-permute-done((bf16[64,2304]{1,0:T(8,128)(2,1)S(1)}, bf16[64,2304]{1,0:T(8,128)(2,1)S(1)}, u32[]{:S(2)}, u32[]{:S(2)}) %collective-permute-start.13) | collective-permute-done | bytes 294944 | tf_op jit(solution)/shard_map/ppermute | solution.py:80
  84.1 10.2 %collective-permute-done.6 = bf16[4,64,1024]{2,1,0:T(8,128)(2,1)S(1)} collective-permute-done((bf16[4,64,1024]{2,1,0:T(8,128)(2,1)S(1)}, bf16[4,64,1024]{2,1,0:T(8,128)(2,1)S(1)}, u32[]{:S(2)}, u32[]{:S(2)}) %collective-permute-start.6) | collective-permute-done | bytes 524320 | tf_op jit(solution)/shard_map/ppermute | solution.py:80
  94.3 2.5 collective-permute-start.9
  97.5 6.1 %collective-permute-done.17 = bf16[4,64,1152]{2,1,0:T(8,128)(2,1)S(1)} collective-permute-done((bf16[4,64,1152]{2,1,0:T(8,128)(2,1)S(1)}, bf16[4,64,1152]{2,1,0:T(8,128)(2,1)S(1)}, u32[]{:S(2)}, u32[]{:S(2)}) %collective-permute-start.17) | collective-permute-done | bytes 589856 | tf_op jit(solution)/shard_map/ppermute | solution.py:80
  103.6 2.5 collective-permute-start.7
  107.0 11.6 %collective-permute-done.15 = bf16[4,64,1152]{2,1,0:T(8,128)(2,1)S(1)} collective-permute-done((bf16[4,64,1152]{2,1,0:T(8,128)(2,1)S(1)}, bf16[4,64,1152]{2,1,0:T(8,128)(2,1)S(1)}, u32[]{:S(2)}, u32[]{:S(2)}) %collective-permute-start.15) | collective-permute-done | bytes 589856 | tf_op jit(solution)/shard_map/ppermute | solution.py:80
  124.4 16.6 %collective-permute-done.9 = bf16[4,2,64,1024]{3,2,1,0:T(8,128)(2,1)S(1)} collective-permute-done((bf16[4,2,64,1024]{3,2,1,0:T(8,128)(2,1)S(1)}, bf16[4,2,64,1024]{3,2,1,0:T(8,128)(2,1)S(1)}, u32[]{:S(2)}, u32[]{:S(2)}) %collective-permute-start.9) | collective-permute-done | bytes 1048608 | tf_op jit(solution)/shard_map/ppermute | solution.py:80
  141.7 5.4 %convolution_convert_fusion.1.qkv_ref = bf16[1024,1536]{1,0:T(8,128)(2,1)} fusion(bf16[1024,1024]{1,0:T(8,128)(2,1)S(1)} %constant_dynamic-update-slice_fusion.3, bf16[1024,2048]{1,0:T(8,128)(2,1)S(1)} %bitcast.349), kind=kOutput, calls=%fused_computation.18 | convolution fusion | flops 3222798336 | bytes 8388608 | tf_op jit(solution)/shard_map/dot_general | solution.py:357
  148.6 10.2 %shard_map.161 = (bf16[1024,512]{1,0:T(8,128)(2,1)}, f32[4,2,1024]{2,1,0:T(2,128)}) custom-call(bf16[1024,1536]{1,0:T(8,128)(2,1)} %convolution_convert_fusion.1.qkv_ref, bf16[1024,128]{1,0:T(8,128)(2,1)} %bitcast.359, bf16[1024,128]{1,0:T(8,128)(2,1)} %bitcast.363), custom_call_target="tpu_custom_call" | custom-call | flops 1073741824 | bytes 2097152 | tf_op jit(solution)/shard_map/pallas_call | solution.py:244
  158.8 10.3 %shard_map.162 = (bf16[1024,512]{1,0:T(8,128)(2,1)}, f32[4,2,1024]{2,1,0:T(2,128)}) custom-call(bf16[1024,1536]{1,0:T(8,128)(2,1)} %convolution_convert_fusion.1.qkv_ref, bf16[1024,128]{1,0:T(8,128)(2,1)} %bitcast.360, bf16[1024,128]{1,0:T(8,128)(2,1)} %bitcast.364, ...), custom_call_target="tpu_custom_call", output_to_operand_aliasing={{0}: (3, {}), {1}: (4, {})} | custom-call | flops 1073741824 | bytes 2097152 | tf_op jit(solution)/shard_map/pallas_call | solution.py:244
  173.0 2.4 bitcast_dynamic-update-slice_fusion.2
  175.4 3.0 pad_maximum_fusion.4
  181.4 3.5 bitcast_add_fusion.2
  187.9 3.0 bitcast_dynamic-update-slice_fusion.1
  193.0 10.1 %fusion.8 = (bf16[1024,2048]{1,0:T(8,128)(2,1)}, bf16[1024,2048]{1,0:T(8,128)(2,1)S(1)}) fusion(bf16[1024,2304]{1,0:T(8,128)(2,1)S(1)} %bitcast.344, bf16[512,1024]{1,0:T(8,128)(2,1)S(1)} %collective-permute-done.11, bf16[512,1024]{1,0:T(8,128)(2,1)S(1)} %fusion.35), kind=kOutput, calls=%fused_computation.10 | convolution fusion | flops 4339007488 | bytes 14680064 | tf_op jit(solution)/shard_map/dot_general | solution.py:367
  205.0 7.8 %convolution_convert_fusion.3 = bf16[1024,2048]{1,0:T(8,128)(2,1)} fusion(bf16[1024,2048]{1,0:T(8,128)(2,1)S(1)} %get-tuple-element.28, bf16[512,1024]{1,0:T(8,128)(2,1)} %collective-permute-done.20, bf16[512,1024]{1,0:T(8,128)(2,1)} %fusion.33), kind=kOutput, calls=%fused_computation.20 | convolution fusion | flops 4301258752 | bytes 10485760 | tf_op jit(solution)/shard_map/dot_general | solution.py:375
  212.8 8.6 %multiply_convert_fusion = bf16[1024,2048]{1,0:T(8,128)(2,1)S(1)} fusion(bf16[1024,2048]{1,0:T(8,128)(2,1)} %get-tuple-element.31, bf16[1024,1024]{1,0:T(8,128)(2,1)} %pad_maximum_fusion.4, bf16[1024,2048]{1,0:T(8,128)(2,1)} %all-gather.2.cloned.1.call-done), kind=kOutput, calls=%fused_computation.11 | convolution fusion | flops 4301258752 | bytes 14680064 | tf_op jit(solution)/shard_map/dot_general | solution.py:381
  221.4 7.1 %fusion.75 = bf16[512,1024]{1,0:T(8,128)(2,1)} fusion(bf16[1024,2304]{1,0:T(8,128)(2,1)} %bitcast.345, bf16[1024,2048]{1,0:T(8,128)(2,1)S(1)} %multiply_convert_fusion), kind=kOutput, calls=%fused_computation.116 | convolution fusion | flops 2148007936 | bytes 7340032 | tf_op jit(solution)/shard_map/dot_general | solution.py:161
  228.5 5.2 %convolution_convert_fusion.2 = bf16[1024,2048]{1,0:T(8,128)(2,1)S(1)} fusion(bf16[1024,2048]{1,0:T(8,128)(2,1)S(1)} %multiply_convert_fusion, bf16[512,1024]{1,0:T(8,128)(2,1)S(1)} %copy-done.57, bf16[512,1024]{1,0:T(8,128)(2,1)S(1)} %copy-done.31), kind=kOutput, calls=%fused_computation.19 | convolution fusion | flops 4301258752 | bytes 10485760 | tf_op jit(solution)/shard_map/dot_general | solution.py:375
  242.4 2.2 reshape.380
  246.9 6.8 %bitcast_multiply_fusion = (f32[512,1024]{1,0:T(8,128)S(1)}, f32[512,1024]{1,0:T(8,128)}) fusion(f32[8,1024]{1,0:T(8,128)S(1)} %get-tuple-element.78, bf16[512,1024]{1,0:T(8,128)(2,1)} %collective-permute-done.21, bf16[1024,2304]{1,0:T(8,128)(2,1)} %bitcast.347, bf16[1024,2048]{1,0:T(8,128)(2,1)} %copy-done.32), kind=kOutput, calls=%fused_computation.28 | convolution fusion | flops 2149056512 | bytes 11567104 | tf_op jit(solution)/shard_map/dot_general | solution.py:161
  259.5 7.6 %collective-permute-done.31 = bf16[4,2,64,1024]{3,2,0,1:T(8,128)(2,1)} collective-permute-done((bf16[4,2,64,1024]{3,2,0,1:T(8,128)(2,1)}, bf16[4,2,64,1024]{3,2,0,1:T(8,128)(2,1)}, u32[]{:S(2)}, u32[]{:S(2)}) %collective-permute-start.31) | collective-permute-done | bytes 1048608 | tf_op jit(solution)/shard_map/ppermute | solution.py:80
  270.3 20.3 %collective-permute-done.33 = bf16[4,2,64,1024]{3,2,0,1:T(8,128)(2,1)S(1)} collective-permute-done((bf16[4,2,64,1024]{3,2,0,1:T(8,128)(2,1)}, bf16[4,2,64,1024]{3,2,0,1:T(8,128)(2,1)S(1)}, u32[]{:S(2)}, u32[]{:S(2)}) %collective-permute-start.33) | collective-permute-done | bytes 1048608 | tf_op jit(solution)/shard_map/ppermute | solution.py:80
  292.8 3.4 fusion.72
  297.5 16.4 %collective-permute-done.32 = bf16[4,64,1024]{2,1,0:T(8,128)(2,1)} collective-permute-done((bf16[4,64,1024]{2,1,0:T(8,128)(2,1)}, bf16[4,64,1024]{2,1,0:T(8,128)(2,1)}, u32[]{:S(2)}, u32[]{:S(2)}) %collective-permute-start.32) | collective-permute-done | bytes 524320 | tf_op jit(solution)/shard_map/ppermute | solution.py:80
  318.0 21.5 %collective-permute-start.37 = (bf16[64,2048]{1,0:T(8,128)(2,1)}, bf16[64,2048]{1,0:T(8,128)(2,1)S(1)}, u32[]{:S(2)}, u32[]{:S(2)}) collective-permute-start(bf16[64,2048]{1,0:T(8,128)(2,1)} %get-tuple-element.68), channel_id=1, source_target_pairs={{0,24},{2,26},{4,28},{6,30},{8,0},{10,2},{12,4},{14,6},{16,8},{18,... | collective-permute-start | bytes 786440 | tf_op jit(solution)/shard_map/ppermute | solution.py:80
  341.8 3.5 convolution_convert_fusion.5.grad_ref
  345.4 2.3 convolution_convert_fusion.4
  347.6 11.5 %shard_map.163.rest_0_ = bf16[1024,1536]{1,0:T(8,128)(2,1)} custom-call(bf16[1024,1536]{1,0:T(8,128)(2,1)} %convolution_convert_fusion.1.qkv_ref, bf16[1024,128]{1,0:T(8,128)(2,1)} %bitcast.361, bf16[1024,128]{1,0:T(8,128)(2,1)} %bitcast.365, f32[4,2,1024]{2,1,0:T(2,128)} %get-tuple-element.29.log_ref, bf16[1024,512]{1,0:T(8,128)(2,1)} %convolution_convert_fusion.5.grad_ref), custom_call_target="tpu_custom_call" | custom-call | flops 2684354560 | bytes 3670016 | tf_op jit(solution)/shard_map/pallas_call | solution.py:280
  359.1 11.7 %shard_map.164 = bf16[1024,1536]{1,0:T(8,128)(2,1)} custom-call(bf16[1024,1536]{1,0:T(8,128)(2,1)} %convolution_convert_fusion.1.qkv_ref, bf16[1024,128]{1,0:T(8,128)(2,1)} %bitcast.362, bf16[1024,128]{1,0:T(8,128)(2,1)} %bitcast.366, f32[4,2,1024]{2,1,0:T(2,128)} %get-tuple-element.29.log_ref, ...), custom_call_target="tpu_custom_call", output_to_operand_aliasing={{}: (5, {})} | custom-call | flops 2684354560 | bytes 3670016 | tf_op jit(solution)/shard_map/pallas_call | solution.py:280
  370.8 6.1 %convolution_convert_fusion = bf16[1024,1536]{1,0:T(8,128)(2,1)S(1)} fusion(bf16[1024,1024]{1,0:T(8,128)(2,1)} %copy-done.27, bf16[1024,1536]{1,0:T(8,128)(2,1)} %shard_map.164), kind=kOutput, calls=%fused_computation.17 | convolution fusion | flops 3222798336 | bytes 8388608 | tf_op jit(solution)/shard_map/dot_general | solution.py:375
  378.5 2.5 collective-permute-start.24
  387.7 11.9 %collective-permute-done.24 = bf16[4,2,64,1024]{3,2,0,1:T(8,128)(2,1)S(1)} collective-permute-done((bf16[4,2,64,1024]{3,2,0,1:T(8,128)(2,1)S(1)}, bf16[4,2,64,1024]{3,2,0,1:T(8,128)(2,1)S(1)}, u32[]{:S(2)}, u32[]{:S(2)}) %collective-permute-start.24) | collective-permute-done | bytes 1048608 | tf_op jit(solution)/shard_map/ppermute | solution.py:80
  400.9 3.1 collective-permute-start.25
  411.3 7.1 %fusion.22 = (bf16[1,512,1024]{2,1,0:T(8,128)(2,1)}, bf16[1,512,1024]{2,1,0:T(8,128)(2,1)}, f32[512,1024]{1,0:T(8,128)S(1)}) fusion(bf16[1,512,1024]{2,1,0:T(8,128)(2,1)S(1)} %copy-done, f32[512,1024]{1,0:T(8,128)S(1)} %get-tuple-element.98, f32[512,1024]{1,0:T(8,128)S(1)} %copy-done.5, f32[1,512,1024]{2,1,0:T(8,128)S(1)} %get-tuple-element.92, ...), kind=kOutput, calls=%fused_computation.49 | convolution fusion | flops 2159017984 | bytes 19972096 | tf_op jit(solution)/shard_map/dot_general | solution.py:161
  418.5 3.1 bitcast_reduce_fusion.1
  422.9 2.9 collective-permute-start.39
  430.3 3.6 collective-permute-done.40
  436.1 4.6 collective-permute-done.44
  444.9 3.4 collective-permute-start.30
  453.0 6.6 %fusion.132 = f32[1024,3072]{1,0:T(8,128)} fusion(bf16[256,1024]{1,0:T(8,128)(2,1)S(1)} %copy-done.26, bf16[256,3072]{1,0:T(8,128)(2,1)S(1)} %bitcast.356), kind=kOutput, calls=%fused_computation.292 | convolution fusion | flops 1610612736 | bytes 14680064 | tf_op jit(solution)/shard_map/dot_general | solution.py:375
  460.5 10.5 %collective-permute-done.29 = bf16[64,2048]{1,0:T(8,128)(2,1)S(1)} collective-permute-done((bf16[64,2048]{1,0:T(8,128)(2,1)S(1)}, bf16[64,2048]{1,0:T(8,128)(2,1)S(1)}, u32[]{:S(2)}, u32[]{:S(2)}) %collective-permute-start.29) | collective-permute-done | bytes 262176 | tf_op jit(solution)/shard_map/ppermute | solution.py:80
  (347 shorter events, 117.5 us)
Async XLA Ops:
  7.2 205.6 %all-gather.2.cloned.1.call-start = ((), (), s32[]{:S(2)}) async-start(), calls=%async_computation.1 | async-start | bytes 4456448 | tf_op jit(solution)/shard_map/all_gather | solution.py:325
  10.3 19.9 %collective-permute-start.3 = (bf16[64,2048]{1,0:T(8,128)(2,1)}, bf16[64,2048]{1,0:T(8,128)(2,1)}, u32[]{:S(2)}, u32[]{:S(2)}) collective-permute-start(bf16[64,2048]{1,0:T(8,128)(2,1)} %pad_maximum_fusion.9), channel_id=1, source_target_pairs={{0,8},{2,10},{4,12},{6,14},{8,16},{10,18},{12,20},{14,22},{16,24},... | collective-permute-start | bytes 786440 | tf_op jit(solution)/shard_map/ppermute | solution.py:80
  13.4 23.7 %collective-permute-start.4 = (bf16[64,2048]{1,0:T(8,128)(2,1)}, bf16[64,2048]{1,0:T(8,128)(2,1)S(1)}, u32[]{:S(2)}, u32[]{:S(2)}) collective-permute-start(bf16[64,2048]{1,0:T(8,128)(2,1)} %pad_maximum_fusion.9), channel_id=1, source_target_pairs={{0,16},{2,18},{4,20},{6,22},{8,24},{10,26},{12,28},{14,30},{16,0},... | collective-permute-start | bytes 786440 | tf_op jit(solution)/shard_map/ppermute | solution.py:80
  15.9 21.1 %collective-permute-start.5 = (bf16[64,2048]{1,0:T(8,128)(2,1)}, bf16[64,2048]{1,0:T(8,128)(2,1)S(1)}, u32[]{:S(2)}, u32[]{:S(2)}) collective-permute-start(bf16[64,2048]{1,0:T(8,128)(2,1)} %pad_maximum_fusion.9), channel_id=1, source_target_pairs={{0,24},{2,26},{4,28},{6,30},{8,0},{10,2},{12,4},{14,6},{16,8},{18,... | collective-permute-start | bytes 786440 | tf_op jit(solution)/shard_map/ppermute | solution.py:80
  17.3 1.6 collective-permute-start
  17.3 455.8 %reduce-scatter.2.cloned.1.call-start = ((), (), s32[]{:S(2)}) async-start(), calls=%async_computation.2 | async-start | bytes 4456448 | tf_op jit(solution)/shard_map/reduce_scatter | solution.py:379
  23.8 1.8 collective-permute-start.1
  27.9 94.8 %collective-permute-start.2 = (bf16[512,1024]{1,0:T(8,128)(2,1)S(1)}, bf16[512,1024]{1,0:T(8,128)(2,1)S(1)}, u32[]{:S(2)}, u32[]{:S(2)}) collective-permute-start(bf16[512,1024]{1,0:T(8,128)(2,1)S(1)} %get-tuple-element.91), channel_id=1, source_target_pairs={{0,1},{1,0},{2,3},{3,2},{4,5},{5,4},{6,7},{7,6},{8,9},{9,8},{10,11... | collective-permute-start | bytes 3145736 | tf_op jit(solution)/shard_map/ppermute | solution.py:145
  29.8 145.6 %collective-permute-start.20 = (bf16[512,1024]{1,0:T(8,128)(2,1)}, bf16[512,1024]{1,0:T(8,128)(2,1)}, u32[]{:S(2)}, u32[]{:S(2)}) collective-permute-start(bf16[512,1024]{1,0:T(8,128)(2,1)} %fusion.33), channel_id=1, source_target_pairs={{0,1},{1,0},{2,3},{3,2},{4,5},{5,4},{6,7},{7,6},{8,9},{9,8},{10,11... | collective-permute-start | bytes 3145736 | tf_op jit(solution)/shard_map/ppermute | solution.py:145
  37.1 19.3 %collective-permute-start.12 = (bf16[64,2304]{1,0:T(8,128)(2,1)S(1)}, bf16[64,2304]{1,0:T(8,128)(2,1)S(1)}, u32[]{:S(2)}, u32[]{:S(2)}) collective-permute-start(bf16[64,2304]{1,0:T(8,128)(2,1)S(1)} %pad_maximum_fusion.8), channel_id=1, source_target_pairs={{0,8},{2,10},{4,12},{6,14},{8,16},{10,18},{12,20},{14,22},{16,24},... | collective-permute-start | bytes 884744 | tf_op jit(solution)/shard_map/ppermute | solution.py:80
  45.0 31.2 %collective-permute-start.13 = (bf16[64,2304]{1,0:T(8,128)(2,1)S(1)}, bf16[64,2304]{1,0:T(8,128)(2,1)S(1)}, u32[]{:S(2)}, u32[]{:S(2)}) collective-permute-start(bf16[64,2304]{1,0:T(8,128)(2,1)S(1)} %pad_maximum_fusion.8), channel_id=1, source_target_pairs={{0,16},{2,18},{4,20},{6,22},{8,24},{10,26},{12,28},{14,30},{16,0},... | collective-permute-start | bytes 884744 | tf_op jit(solution)/shard_map/ppermute | solution.py:80
  46.7 31.1 %collective-permute-start.14 = (bf16[64,2304]{1,0:T(8,128)(2,1)S(1)}, bf16[64,2304]{1,0:T(8,128)(2,1)S(1)}, u32[]{:S(2)}, u32[]{:S(2)}) collective-permute-start(bf16[64,2304]{1,0:T(8,128)(2,1)S(1)} %pad_maximum_fusion.8), channel_id=1, source_target_pairs={{0,24},{2,26},{4,28},{6,30},{8,0},{10,2},{12,4},{14,6},{16,8},{18,... | collective-permute-start | bytes 884744 | tf_op jit(solution)/shard_map/ppermute | solution.py:80
  56.4 27.1 %collective-permute-start.8 = (bf16[4,64,1024]{2,1,0:T(8,128)(2,1)S(1)}, bf16[4,64,1024]{2,1,0:T(8,128)(2,1)S(1)}, u32[]{:S(2)}, u32[]{:S(2)}) collective-permute-start(bf16[4,64,1024]{2,1,0:T(8,128)(2,1)S(1)} %get-tuple-element.73), channel_id=1, source_target_pairs={{0,4},{2,6},{4,0},{6,2},{8,12},{10,14},{12,8},{14,10},{16,20},{18,... | collective-permute-start | bytes 1572872 | tf_op jit(solution)/shard_map/ppermute | solution.py:80
  76.2 18.1 %collective-permute-start.6 = (bf16[4,64,1024]{2,1,0:T(8,128)(2,1)S(1)}, bf16[4,64,1024]{2,1,0:T(8,128)(2,1)S(1)}, u32[]{:S(2)}, u32[]{:S(2)}) collective-permute-start(bf16[4,64,1024]{2,1,0:T(8,128)(2,1)S(1)} %get-tuple-element.72), channel_id=1, source_target_pairs={{0,2},{2,0},{4,6},{6,4},{8,10},{10,8},{12,14},{14,12},{16,18},{18,... | collective-permute-start | bytes 1572872 | tf_op jit(solution)/shard_map/ppermute | solution.py:80
  79.9 23.7 %collective-permute-start.17 = (bf16[4,64,1152]{2,1,0:T(8,128)(2,1)S(1)}, bf16[4,64,1152]{2,1,0:T(8,128)(2,1)S(1)}, u32[]{:S(2)}, u32[]{:S(2)}) collective-permute-start(bf16[4,64,1152]{2,1,0:T(8,128)(2,1)S(1)} %get-tuple-element.65), channel_id=1, source_target_pairs={{0,4},{2,6},{4,0},{6,2},{8,12},{10,14},{12,8},{14,10},{16,20},{18,... | collective-permute-start | bytes 1769480 | tf_op jit(solution)/shard_map/ppermute | solution.py:80
  83.5 35.1 %collective-permute-start.15 = (bf16[4,64,1152]{2,1,0:T(8,128)(2,1)S(1)}, bf16[4,64,1152]{2,1,0:T(8,128)(2,1)S(1)}, u32[]{:S(2)}, u32[]{:S(2)}) collective-permute-start(bf16[4,64,1152]{2,1,0:T(8,128)(2,1)S(1)} %get-tuple-element.64), channel_id=1, source_target_pairs={{0,2},{2,0},{4,6},{6,4},{8,10},{10,8},{12,14},{14,12},{16,18},{18,... | collective-permute-start | bytes 1769480 | tf_op jit(solution)/shard_map/ppermute | solution.py:80
  94.3 46.8 %collective-permute-start.9 = (bf16[4,2,64,1024]{3,2,1,0:T(8,128)(2,1)S(1)}, bf16[4,2,64,1024]{3,2,1,0:T(8,128)(2,1)S(1)}, u32[]{:S(2)}, u32[]{:S(2)}) collective-permute-start(bf16[4,2,64,1024]{3,2,1,0:T(8,128)(2,1)S(1)} %bitcast_dynamic-update-slice_fusion.15), channel_id=1, source_target_pairs={{0,2},{2,0},{4,6},{6,4},{8,10},{10,8},{12,14},{14,12},{16,18},{18,... | collective-permute-start | bytes 3145736 | tf_op jit(solution)/shard_map/ppermute | solution.py:80
  103.6 37.5 %collective-permute-start.7 = (bf16[4,2,64,1024]{3,2,1,0:T(8,128)(2,1)S(1)}, bf16[4,2,64,1024]{3,2,1,0:T(8,128)(2,1)S(1)}, u32[]{:S(2)}, u32[]{:S(2)}) collective-permute-start(bf16[4,2,64,1024]{3,2,1,0:T(8,128)(2,1)S(1)} %bitcast_dynamic-update-slice_fusion.13), channel_id=1, source_target_pairs={{0,4},{2,6},{4,0},{6,2},{8,12},{10,14},{12,8},{14,10},{16,20},{18,... | collective-permute-start | bytes 3145736 | tf_op jit(solution)/shard_map/ppermute | solution.py:80
  118.6 59.9 %collective-permute-start.18 = (bf16[4,2,64,1152]{3,2,1,0:T(8,128)(2,1)}, bf16[4,2,64,1152]{3,2,1,0:T(8,128)(2,1)}, u32[]{:S(2)}, u32[]{:S(2)}) collective-permute-start(bf16[4,2,64,1152]{3,2,1,0:T(8,128)(2,1)} %bitcast_dynamic-update-slice_fusion.11), channel_id=1, source_target_pairs={{0,2},{2,0},{4,6},{6,4},{8,10},{10,8},{12,14},{14,12},{16,18},{18,... | collective-permute-start | bytes 3538952 | tf_op jit(solution)/shard_map/ppermute | solution.py:80
  122.7 65.2 %collective-permute-start.16 = (bf16[4,2,64,1152]{3,2,1,0:T(8,128)(2,1)}, bf16[4,2,64,1152]{3,2,1,0:T(8,128)(2,1)}, u32[]{:S(2)}, u32[]{:S(2)}) collective-permute-start(bf16[4,2,64,1152]{3,2,1,0:T(8,128)(2,1)} %bitcast_dynamic-update-slice_fusion.9), channel_id=1, source_target_pairs={{0,4},{2,6},{4,0},{6,2},{8,12},{10,14},{12,8},{14,10},{16,20},{18,... | collective-permute-start | bytes 3538952 | tf_op jit(solution)/shard_map/ppermute | solution.py:80
  171.2 8.8 %collective-permute-start.10 = (bf16[512,1024]{1,0:T(8,128)(2,1)S(1)}, bf16[512,1024]{1,0:T(8,128)(2,1)S(1)}, u32[]{:S(2)}, u32[]{:S(2)}) collective-permute-start(bf16[512,1024]{1,0:T(8,128)(2,1)S(1)} %convolution_convert_fusion.6), channel_id=1, source_target_pairs={{0,1},{1,0},{2,3},{3,2},{4,5},{5,4},{6,7},{7,6},{8,9},{9,8},{10,11... | collective-permute-start | bytes 3145736 | tf_op jit(solution)/shard_map/ppermute | solution.py:145
  187.3 5.6 %collective-permute-start.11 = (bf16[512,1024]{1,0:T(8,128)(2,1)S(1)}, bf16[512,1024]{1,0:T(8,128)(2,1)S(1)}, u32[]{:S(2)}, u32[]{:S(2)}) collective-permute-start(bf16[512,1024]{1,0:T(8,128)(2,1)S(1)} %fusion.35), channel_id=1, source_target_pairs={{0,1},{1,0},{2,3},{3,2},{4,5},{5,4},{6,7},{7,6},{8,9},{9,8},{10,11... | collective-permute-start | bytes 3145736 | tf_op jit(solution)/shard_map/ppermute | solution.py:145
  237.7 9.2 %collective-permute-start.21 = (bf16[512,1024]{1,0:T(8,128)(2,1)}, bf16[512,1024]{1,0:T(8,128)(2,1)}, u32[]{:S(2)}, u32[]{:S(2)}) collective-permute-start(bf16[512,1024]{1,0:T(8,128)(2,1)} %fusion.75), channel_id=1, source_target_pairs={{0,1},{1,0},{2,3},{3,2},{4,5},{5,4},{6,7},{7,6},{8,9},{9,8},{10,11... | collective-permute-start | bytes 3145736 | tf_op jit(solution)/shard_map/ppermute | solution.py:145
  237.7 29.4 %collective-permute-start.31 = (bf16[4,2,64,1024]{3,2,0,1:T(8,128)(2,1)}, bf16[4,2,64,1024]{3,2,0,1:T(8,128)(2,1)}, u32[]{:S(2)}, u32[]{:S(2)}) collective-permute-start(bf16[4,2,64,1024]{3,2,0,1:T(8,128)(2,1)} %get-tuple-element.34), channel_id=1, source_target_pairs={{0,4},{2,6},{4,0},{6,2},{8,12},{10,14},{12,8},{14,10},{16,20},{18,... | collective-permute-start | bytes 3145736 | tf_op jit(solution)/shard_map/ppermute | solution.py:80
  245.4 45.2 %collective-permute-start.33 = (bf16[4,2,64,1024]{3,2,0,1:T(8,128)(2,1)}, bf16[4,2,64,1024]{3,2,0,1:T(8,128)(2,1)S(1)}, u32[]{:S(2)}, u32[]{:S(2)}) collective-permute-start(bf16[4,2,64,1024]{3,2,0,1:T(8,128)(2,1)} %get-tuple-element.36), channel_id=1, source_target_pairs={{0,2},{2,0},{4,6},{6,4},{8,10},{10,8},{12,14},{14,12},{16,18},{18,... | collective-permute-start | bytes 3145736 | tf_op jit(solution)/shard_map/ppermute | solution.py:80
  259.5 81.0 %collective-permute-start.22 = (bf16[512,1024]{1,0:T(8,128)(2,1)}, bf16[512,1024]{1,0:T(8,128)(2,1)}, u32[]{:S(2)}, u32[]{:S(2)}) collective-permute-start(bf16[512,1024]{1,0:T(8,128)(2,1)} %get-tuple-element.97), channel_id=1, source_target_pairs={{0,1},{1,0},{2,3},{3,2},{4,5},{5,4},{6,7},{7,6},{8,9},{9,8},{10,11... | collective-permute-start | bytes 3145736 | tf_op jit(solution)/shard_map/ppermute | solution.py:145
  269.7 44.2 %collective-permute-start.32 = (bf16[4,64,1024]{2,1,0:T(8,128)(2,1)}, bf16[4,64,1024]{2,1,0:T(8,128)(2,1)}, u32[]{:S(2)}, u32[]{:S(2)}) collective-permute-start(bf16[4,64,1024]{2,1,0:T(8,128)(2,1)} %dynamic-slice_bitcast_fusion.1), channel_id=1, source_target_pairs={{0,2},{2,0},{4,6},{6,4},{8,10},{10,8},{12,14},{14,12},{16,18},{18,... | collective-permute-start | bytes 1572872 | tf_op jit(solution)/shard_map/ppermute | solution.py:80
  292.1 23.2 %collective-permute-start.34 = (bf16[4,64,1024]{2,1,0:T(8,128)(2,1)}, bf16[4,64,1024]{2,1,0:T(8,128)(2,1)}, u32[]{:S(2)}, u32[]{:S(2)}) collective-permute-start(bf16[4,64,1024]{2,1,0:T(8,128)(2,1)} %dynamic-slice_bitcast_fusion), channel_id=1, source_target_pairs={{0,4},{2,6},{4,0},{6,2},{8,12},{10,14},{12,8},{14,10},{16,20},{18,... | collective-permute-start | bytes 1572872 | tf_op jit(solution)/shard_map/ppermute | solution.py:80
  318.0 67.1 %collective-permute-start.37 = (bf16[64,2048]{1,0:T(8,128)(2,1)}, bf16[64,2048]{1,0:T(8,128)(2,1)S(1)}, u32[]{:S(2)}, u32[]{:S(2)}) collective-permute-start(bf16[64,2048]{1,0:T(8,128)(2,1)} %get-tuple-element.68), channel_id=1, source_target_pairs={{0,24},{2,26},{4,28},{6,30},{8,0},{10,2},{12,4},{14,6},{16,8},{18,... | collective-permute-start | bytes 786440 | tf_op jit(solution)/shard_map/ppermute | solution.py:80
  339.5 45.7 %collective-permute-start.36 = (bf16[64,2048]{1,0:T(8,128)(2,1)}, bf16[64,2048]{1,0:T(8,128)(2,1)}, u32[]{:S(2)}, u32[]{:S(2)}) collective-permute-start(bf16[64,2048]{1,0:T(8,128)(2,1)} %get-tuple-element.67), channel_id=1, source_target_pairs={{0,16},{2,18},{4,20},{6,22},{8,24},{10,26},{12,28},{14,30},{16,0},... | collective-permute-start | bytes 786440 | tf_op jit(solution)/shard_map/ppermute | solution.py:80
  339.6 46.1 %collective-permute-start.35 = (bf16[64,2048]{1,0:T(8,128)(2,1)}, bf16[64,2048]{1,0:T(8,128)(2,1)}, u32[]{:S(2)}, u32[]{:S(2)}) collective-permute-start(bf16[64,2048]{1,0:T(8,128)(2,1)} %get-tuple-element.66), channel_id=1, source_target_pairs={{0,8},{2,10},{4,12},{6,14},{8,16},{10,18},{12,20},{14,22},{16,24},... | collective-permute-start | bytes 786440 | tf_op jit(solution)/shard_map/ppermute | solution.py:80
  378.5 21.1 %collective-permute-start.24 = (bf16[4,2,64,1024]{3,2,0,1:T(8,128)(2,1)S(1)}, bf16[4,2,64,1024]{3,2,0,1:T(8,128)(2,1)S(1)}, u32[]{:S(2)}, u32[]{:S(2)}) collective-permute-start(bf16[4,2,64,1024]{3,2,0,1:T(8,128)(2,1)S(1)} %bitcast.369), channel_id=1, source_target_pairs={{0,4},{2,6},{4,0},{6,2},{8,12},{10,14},{12,8},{14,10},{16,20},{18,... | collective-permute-start | bytes 3145736 | tf_op jit(solution)/shard_map/ppermute | solution.py:80
  381.4 22.6 %collective-permute-start.26 = (bf16[4,2,64,1024]{3,2,0,1:T(8,128)(2,1)S(1)}, bf16[4,2,64,1024]{3,2,0,1:T(8,128)(2,1)S(1)}, u32[]{:S(2)}, u32[]{:S(2)}) collective-permute-start(bf16[4,2,64,1024]{3,2,0,1:T(8,128)(2,1)S(1)} %bitcast.368), channel_id=1, source_target_pairs={{0,2},{2,0},{4,6},{6,4},{8,10},{10,8},{12,14},{14,12},{16,18},{18,... | collective-permute-start | bytes 3145736 | tf_op jit(solution)/shard_map/ppermute | solution.py:80
  385.1 25.1 %collective-permute-start.19 = (bf16[512,1024]{1,0:T(8,128)(2,1)S(1)}, bf16[512,1024]{1,0:T(8,128)(2,1)}, u32[]{:S(2)}, u32[]{:S(2)}) collective-permute-start(bf16[512,1024]{1,0:T(8,128)(2,1)S(1)} %copy-done.55), channel_id=1, source_target_pairs={{0,1},{1,0},{2,3},{3,2},{4,5},{5,4},{6,7},{7,6},{8,9},{9,8},{10,11... | collective-permute-start | bytes 3145736 | tf_op jit(solution)/shard_map/ppermute | solution.py:145
  385.2 21.8 %collective-permute-start.23 = (bf16[512,1024]{1,0:T(8,128)(2,1)S(1)}, bf16[512,1024]{1,0:T(8,128)(2,1)S(1)}, u32[]{:S(2)}, u32[]{:S(2)}) collective-permute-start(bf16[512,1024]{1,0:T(8,128)(2,1)S(1)} %fusion.67), channel_id=1, source_target_pairs={{0,1},{1,0},{2,3},{3,2},{4,5},{5,4},{6,7},{7,6},{8,9},{9,8},{10,11... | collective-permute-start | bytes 3145736 | tf_op jit(solution)/shard_map/ppermute | solution.py:145
  400.9 42.5 %collective-permute-start.25 = (bf16[4,64,1024]{2,1,0:T(8,128)(2,1)}, bf16[4,64,1024]{2,1,0:T(8,128)(2,1)S(1)}, u32[]{:S(2)}, u32[]{:S(2)}) collective-permute-start(bf16[4,64,1024]{2,1,0:T(8,128)(2,1)} %dynamic-slice_bitcast_fusion.3), channel_id=1, source_target_pairs={{0,2},{2,0},{4,6},{6,4},{8,10},{10,8},{12,14},{14,12},{16,18},{18,... | collective-permute-start | bytes 1572872 | tf_op jit(solution)/shard_map/ppermute | solution.py:80
  405.2 38.4 %collective-permute-start.27 = (bf16[4,64,1024]{2,1,0:T(8,128)(2,1)}, bf16[4,64,1024]{2,1,0:T(8,128)(2,1)}, u32[]{:S(2)}, u32[]{:S(2)}) collective-permute-start(bf16[4,64,1024]{2,1,0:T(8,128)(2,1)} %dynamic-slice_bitcast_fusion.2), channel_id=1, source_target_pairs={{0,4},{2,6},{4,0},{6,2},{8,12},{10,14},{12,8},{14,10},{16,20},{18,... | collective-permute-start | bytes 1572872 | tf_op jit(solution)/shard_map/ppermute | solution.py:80
  421.6 1.3 collective-permute-start.38
  422.9 7.4 %collective-permute-start.39 = (bf16[16,3072]{1,0:T(8,128)(2,1)S(1)}, bf16[16,3072]{1,0:T(8,128)(2,1)S(1)}, u32[]{:S(2)}, u32[]{:S(2)}) collective-permute-start(bf16[16,3072]{1,0:T(8,128)(2,1)S(1)} %constant_dynamic-update-slice_fusion), channel_id=1, source_target_pairs={{0,8},{2,10},{4,12},{6,14},{8,16},{10,18},{12,20},{14,22},{16,24},... | collective-permute-start | bytes 294920 | tf_op jit(solution)/shard_map/ppermute | solution.py:80
  425.8 8.1 %collective-permute-start.40 = (bf16[16,3072]{1,0:T(8,128)(2,1)S(1)}, bf16[16,3072]{1,0:T(8,128)(2,1)S(1)}, u32[]{:S(2)}, u32[]{:S(2)}) collective-permute-start(bf16[16,3072]{1,0:T(8,128)(2,1)S(1)} %constant_dynamic-update-slice_fusion), channel_id=1, source_target_pairs={{0,16},{2,18},{4,20},{6,22},{8,24},{10,26},{12,28},{14,30},{16,0},... | collective-permute-start | bytes 294920 | tf_op jit(solution)/shard_map/ppermute | solution.py:80
  426.8 7.1 %collective-permute-start.41 = (bf16[16,3072]{1,0:T(8,128)(2,1)S(1)}, bf16[16,3072]{1,0:T(8,128)(2,1)S(1)}, u32[]{:S(2)}, u32[]{:S(2)}) collective-permute-start(bf16[16,3072]{1,0:T(8,128)(2,1)S(1)} %constant_dynamic-update-slice_fusion), channel_id=1, source_target_pairs={{0,24},{2,26},{4,28},{6,30},{8,0},{10,2},{12,4},{14,6},{16,8},{18,... | collective-permute-start | bytes 294920 | tf_op jit(solution)/shard_map/ppermute | solution.py:80
  434.0 6.8 %collective-permute-start.44 = (bf16[4,16,1536]{2,1,0:T(8,128)(2,1)S(1)}, bf16[4,16,1536]{2,1,0:T(8,128)(2,1)S(1)}, u32[]{:S(2)}, u32[]{:S(2)}) collective-permute-start(bf16[4,16,1536]{2,1,0:T(8,128)(2,1)S(1)} %get-tuple-element.75), channel_id=1, source_target_pairs={{0,4},{2,6},{4,0},{6,2},{8,12},{10,14},{12,8},{14,10},{16,20},{18,... | collective-permute-start | bytes 589832 | tf_op jit(solution)/shard_map/ppermute | solution.py:80
  434.4 8.4 %collective-permute-start.42 = (bf16[4,16,1536]{2,1,0:T(8,128)(2,1)S(1)}, bf16[4,16,1536]{2,1,0:T(8,128)(2,1)S(1)}, u32[]{:S(2)}, u32[]{:S(2)}) collective-permute-start(bf16[4,16,1536]{2,1,0:T(8,128)(2,1)S(1)} %get-tuple-element.74), channel_id=1, source_target_pairs={{0,2},{2,0},{4,6},{6,4},{8,10},{10,8},{12,14},{14,12},{16,18},{18,... | collective-permute-start | bytes 589832 | tf_op jit(solution)/shard_map/ppermute | solution.py:80
  440.8 10.3 %collective-permute-start.45 = (bf16[4,2,16,1536]{3,2,1,0:T(8,128)(2,1)S(1)}, bf16[4,2,16,1536]{3,2,1,0:T(8,128)(2,1)S(1)}, u32[]{:S(2)}, u32[]{:S(2)}) collective-permute-start(bf16[4,2,16,1536]{3,2,1,0:T(8,128)(2,1)S(1)} %bitcast_dynamic-update-slice_fusion.31), channel_id=1, source_target_pairs={{0,2},{2,0},{4,6},{6,4},{8,10},{10,8},{12,14},{14,12},{16,18},{18,... | collective-permute-start | bytes 1179656 | tf_op jit(solution)/shard_map/ppermute | solution.py:80
  442.9 9.9 %collective-permute-start.43 = (bf16[4,2,16,1536]{3,2,1,0:T(8,128)(2,1)S(1)}, bf16[4,2,16,1536]{3,2,1,0:T(8,128)(2,1)S(1)}, u32[]{:S(2)}, u32[]{:S(2)}) collective-permute-start(bf16[4,2,16,1536]{3,2,1,0:T(8,128)(2,1)S(1)} %bitcast_dynamic-update-slice_fusion.29), channel_id=1, source_target_pairs={{0,4},{2,6},{4,0},{6,2},{8,12},{10,14},{12,8},{14,10},{16,20},{18,... | collective-permute-start | bytes 1179656 | tf_op jit(solution)/shard_map/ppermute | solution.py:80
  444.9 15.6 %collective-permute-start.30 = (bf16[64,2048]{1,0:T(8,128)(2,1)S(1)}, bf16[64,2048]{1,0:T(8,128)(2,1)S(1)}, u32[]{:S(2)}, u32[]{:S(2)}) collective-permute-start(bf16[64,2048]{1,0:T(8,128)(2,1)S(1)} %get-tuple-element.71), channel_id=1, source_target_pairs={{0,24},{2,26},{4,28},{6,30},{8,0},{10,2},{12,4},{14,6},{16,8},{18,... | collective-permute-start | bytes 786440 | tf_op jit(solution)/shard_map/ppermute | solution.py:80
  448.3 22.7 %collective-permute-start.29 = (bf16[64,2048]{1,0:T(8,128)(2,1)S(1)}, bf16[64,2048]{1,0:T(8,128)(2,1)S(1)}, u32[]{:S(2)}, u32[]{:S(2)}) collective-permute-start(bf16[64,2048]{1,0:T(8,128)(2,1)S(1)} %get-tuple-element.70), channel_id=1, source_target_pairs={{0,16},{2,18},{4,20},{6,22},{8,24},{10,26},{12,28},{14,30},{16,0},... | collective-permute-start | bytes 786440 | tf_op jit(solution)/shard_map/ppermute | solution.py:80
  449.1 21.9 %collective-permute-start.28 = (bf16[64,2048]{1,0:T(8,128)(2,1)S(1)}, bf16[64,2048]{1,0:T(8,128)(2,1)S(1)}, u32[]{:S(2)}, u32[]{:S(2)}) collective-permute-start(bf16[64,2048]{1,0:T(8,128)(2,1)S(1)} %get-tuple-element.69), channel_id=1, source_target_pairs={{0,8},{2,10},{4,12},{6,14},{8,16},{10,18},{12,20},{14,22},{16,24},... | collective-permute-start | bytes 786440 | tf_op jit(solution)/shard_map/ppermute | solution.py:80
  (59 other events, 455.2 us)
Sparse Core Ops, SparseCore 0:
  17.4 111.2 all-gather.1
  245.5 131.9 reduce-scatter.1

commit v4 on v3

--- a/solution.py
+++ b/solution.py
@@ -327,7 +327,6 @@
     out_whole = qkv_whole[:, 3 * head_cols :]
     qkv_whole = qkv_whole[:, : 3 * head_cols]
     up_whole = rest_whole[:, :hidden_cols]
-    condition_all = rest_whole[:, hidden_cols:].reshape(-1, width)
 
     mod_cols = jnp.dot(condition, w_mod, preferred_element_type=f32) + b_mod.astype(f32)
     own_cols = half_of(mod_cols, side)
@@ -366,10 +365,6 @@
     second_full = jnp.concatenate([second_own, swapped(second_own)], axis=0)
     hidden_pre = jnp.dot(second_full, up_whole, preferred_element_type=f32)
     hidden, slope = lax.optimization_barrier(gelu_and_slope(hidden_pre))
-    mlp_other = swapped(nt(hidden[local_len:], down_whole).astype(bf16))
-    mlp_out = (nt(hidden[:local_len], down_whole) + mlp_other.astype(f32)).reshape(framed.shape)
-    output = (middle + gate_mlp * mlp_out).astype(bf16).reshape(tokens.shape)
-    grad_gate_mlp = jnp.sum(upstream * mlp_out, axis=1)
 
     def tn(a, b):
         return lax.dot_general(a, b, (((0,), (0,)), ((), ())), preferred_element_type=f32)
@@ -401,6 +396,13 @@
     qkv_sum, out_sum = tail_sum[:, : 3 * head_cols], tail_sum[:, 3 * head_cols :]
     first_other = swapped(nt(half_of(grad_qkv, 1 - side), qkv_whole).astype(bf16))
     grad_first = nt(half_of(grad_qkv, side), qkv_whole) + first_other.astype(f32)
+    hidden_late, grad_qkv = lax.optimization_barrier((hidden, grad_qkv))
+    mlp_other = swapped(nt(hidden_late[local_len:], down_whole).astype(bf16))
+    mlp_out = nt(hidden_late[:local_len], down_whole) + mlp_other.astype(f32)
+    mlp_out = mlp_out.reshape(framed.shape)
+    output = (middle + gate_mlp * mlp_out).astype(bf16).reshape(tokens.shape)
+    grad_gate_mlp = jnp.sum(upstream * mlp_out, axis=1)
+
     first_back = jax.vjp(modulated, framed, shift_attn, scale_attn)[1]
     grad_framed, grad_shift_attn, grad_scale_attn = first_back(grad_first.reshape(framed.shape))
     grad_tokens = (grad_framed + grad_middle).astype(bf16).reshape(tokens.shape)
@@ -410,6 +412,8 @@
     low, high = low.reshape(frames_here, -1), high.reshape(frames_here, -1)
     keep = jnp.where(side == 0, low, high).astype(bf16)
     give = jnp.where(side == 0, high, low).astype(bf16)
+    rest_late, give = lax.optimization_barrier((rest_whole, give))
+    condition_all = rest_late[:, hidden_cols:].reshape(-1, width)
     give = swapped(give)
     mine = in_order(keep, give, side)
     grad_mods = gather_rest(gather_deep(mine, grid, at), grid, at)

time: 489 us -> 512 us (1.047)
  the two profiles are of different devices: /device:TPU:0 before, /device:TPU:10 now
where the time goes in v4:
time: 512 us; the launch traced here: 505 us
  waiting for transfers between devices  207 us (40%)
  matrix products  90.9 us (18%)
  starting transfers between devices  61.4 us (12%)
  local copies, waits for them, and re-layouts  50.7 us (10%)
  Pallas kernels  44.2 us (9%)
  other arithmetic  34.5 us (7%)
  between operations  16.1 us (3%)
    ppermute x35, waiting for transfers between devices, moved(): return lax.ppermute(part, 'rows', shift_pairs(grid, axis, k))  206 us
    ppermute x35, starting transfers between devices, moved(): return lax.ppermute(part, 'rows', shift_pairs(grid, axis, k))  59.5 us
    dot_general x8, matrix products, nt(): lax.dot_general(a, b, (((1,), (1,)), ((), ())), preferred_element_type=f32)  31.8 us
    dot_general x5, matrix products, tn(): lax.dot_general(a, b, (((0,), (0,)), ((), ())), preferred_element_type=f32)  27.9 us
    pallas_call x2, Pallas kernels, attend_back(): pl.pallas_call(backward_kernel, grid=(pairs,), in_specs=specs, out_specs=...  23.7 us
    pallas_call x2, Pallas kernels, attend(): pl.pallas_call(forward_kernel, grid=(pairs,), in_specs=[pl.BlockSpec((len...  20.5 us
    dynamic_update_slice x35, local copies, waits for them, and re-layouts, gather_axis(): lax.dynamic_update_index_in_dim(whole, piece, (at[axis] - k) % count, dim)  12.8 us
    unnamed x116, local copies, waits for them, and re-layouts  10.6 us
  transfers between devices with their start and end apart: 48, of which 19 were waited for; matrix products, arithmetic and copies ran while one was open for 27% of the time, Pallas kernels for 9%

profile of v4, /device:TPU:10, one launch (start us, length us, event | category | flops | bytes accessed | tf_op | source)
XLA Modules:
  0.0 504.6 jit_solution(6620397446877768080)
XLA Ops:
  10.3 2.6 collective-permute-start.4
  17.1 3.8 convolution_add_fusion
  25.5 22.0 %collective-permute-done.3 = bf16[64,2048]{1,0:T(8,128)(2,1)S(1)} collective-permute-done((bf16[64,2048]{1,0:T(8,128)(2,1)}, bf16[64,2048]{1,0:T(8,128)(2,1)S(1)}, u32[]{:S(2)}, u32[]{:S(2)}) %collective-permute-start.3) | collective-permute-done | bytes 262176 | tf_op jit(solution)/shard_map/ppermute | solution.py:80
  47.6 3.8 collective-permute-start.13
  52.0 29.2 %collective-permute-done.12 = bf16[64,2304]{1,0:T(8,128)(2,1)S(1)} collective-permute-done((bf16[64,2304]{1,0:T(8,128)(2,1)S(1)}, bf16[64,2304]{1,0:T(8,128)(2,1)S(1)}, u32[]{:S(2)}, u32[]{:S(2)}) %collective-permute-start.12) | collective-permute-done | bytes 294944 | tf_op jit(solution)/shard_map/ppermute | solution.py:80
  89.2 12.5 %collective-permute-done.8 = bf16[4,64,1024]{2,1,0:T(8,128)(2,1)S(1)} collective-permute-done((bf16[4,64,1024]{2,1,0:T(8,128)(2,1)S(1)}, bf16[4,64,1024]{2,1,0:T(8,128)(2,1)S(1)}, u32[]{:S(2)}, u32[]{:S(2)}) %collective-permute-start.8) | collective-permute-done | bytes 524320 | tf_op jit(solution)/shard_map/ppermute | solution.py:80
  101.6 2.5 collective-permute-start.17
  104.2 2.5 collective-permute-start.9
  107.5 15.6 %collective-permute-done.17 = bf16[4,64,1152]{2,1,0:T(8,128)(2,1)S(1)} collective-permute-done((bf16[4,64,1152]{2,1,0:T(8,128)(2,1)S(1)}, bf16[4,64,1152]{2,1,0:T(8,128)(2,1)S(1)}, u32[]{:S(2)}, u32[]{:S(2)}) %collective-permute-start.17) | collective-permute-done | bytes 589856 | tf_op jit(solution)/shard_map/ppermute | solution.py:80
  130.2 15.9 %collective-permute-done.9 = bf16[4,2,64,1024]{3,2,1,0:T(8,128)(2,1)S(1)} collective-permute-done((bf16[4,2,64,1024]{3,2,1,0:T(8,128)(2,1)S(1)}, bf16[4,2,64,1024]{3,2,1,0:T(8,128)(2,1)S(1)}, u32[]{:S(2)}, u32[]{:S(2)}) %collective-permute-start.9) | collective-permute-done | bytes 1048608 | tf_op jit(solution)/shard_map/ppermute | solution.py:80
  146.2 2.9 collective-permute-done.7
  149.6 5.4 %convolution_convert_fusion.1.qkv_ref = bf16[1024,1536]{1,0:T(8,128)(2,1)} fusion(bf16[1024,1024]{1,0:T(8,128)(2,1)S(1)} %constant_dynamic-update-slice_fusion.3, bf16[1024,2048]{1,0:T(8,128)(2,1)S(1)} %bitcast.353), kind=kOutput, calls=%fused_computation.18 | convolution fusion | flops 3222798336 | bytes 8388608 | tf_op jit(solution)/shard_map/dot_general | solution.py:356
  156.5 10.2 %shard_map.161 = (bf16[1024,512]{1,0:T(8,128)(2,1)}, f32[4,2,1024]{2,1,0:T(2,128)}) custom-call(bf16[1024,1536]{1,0:T(8,128)(2,1)} %convolution_convert_fusion.1.qkv_ref, bf16[1024,128]{1,0:T(8,128)(2,1)} %bitcast.367, bf16[1024,128]{1,0:T(8,128)(2,1)} %bitcast.363), custom_call_target="tpu_custom_call" | custom-call | flops 1073741824 | bytes 2097152 | tf_op jit(solution)/shard_map/pallas_call | solution.py:244
  166.7 10.3 %shard_map.162 = (bf16[1024,512]{1,0:T(8,128)(2,1)}, f32[4,2,1024]{2,1,0:T(2,128)}) custom-call(bf16[1024,1536]{1,0:T(8,128)(2,1)} %convolution_convert_fusion.1.qkv_ref, bf16[1024,128]{1,0:T(8,128)(2,1)} %bitcast.368, bf16[1024,128]{1,0:T(8,128)(2,1)} %bitcast.364, ...), custom_call_target="tpu_custom_call", output_to_operand_aliasing={{0}: (3, {}), {1}: (4, {})} | custom-call | flops 1073741824 | bytes 2097152 | tf_op jit(solution)/shard_map/pallas_call | solution.py:244
  180.9 2.4 bitcast_dynamic-update-slice_fusion.2
  183.3 3.0 pad_maximum_fusion.4
  189.3 3.5 bitcast_add_fusion.2
  195.8 3.0 bitcast_dynamic-update-slice_fusion.1
  200.9 10.0 %fusion.8 = (bf16[1024,2048]{1,0:T(8,128)(2,1)}, bf16[1024,2048]{1,0:T(8,128)(2,1)S(1)}) fusion(bf16[1024,2304]{1,0:T(8,128)(2,1)S(1)} %bitcast.348, bf16[512,1024]{1,0:T(8,128)(2,1)S(1)} %collective-permute-done.11, bf16[512,1024]{1,0:T(8,128)(2,1)S(1)} %fusion.35), kind=kOutput, calls=%fused_computation.10 | convolution fusion | flops 4339007488 | bytes 14680064 | tf_op jit(solution)/shard_map/dot_general | solution.py:366
  212.9 7.8 %convolution_convert_fusion.3 = bf16[1024,2048]{1,0:T(8,128)(2,1)} fusion(bf16[1024,2048]{1,0:T(8,128)(2,1)S(1)} %get-tuple-element.36, bf16[512,1024]{1,0:T(8,128)(2,1)} %collective-permute-done.19, bf16[512,1024]{1,0:T(8,128)(2,1)} %fusion.33), kind=kOutput, calls=%fused_computation.20 | convolution fusion | flops 4301258752 | bytes 10485760 | tf_op jit(solution)/shard_map/dot_general | solution.py:370
  220.7 8.6 %multiply_convert_fusion = bf16[1024,2048]{1,0:T(8,128)(2,1)S(1)} fusion(bf16[1024,2048]{1,0:T(8,128)(2,1)} %get-tuple-element.34, bf16[1024,1024]{1,0:T(8,128)(2,1)} %pad_maximum_fusion.4, bf16[1024,2048]{1,0:T(8,128)(2,1)} %all-gather.2.cloned.1.call-done), kind=kOutput, calls=%fused_computation.11 | convolution fusion | flops 4301258752 | bytes 14680064 | tf_op jit(solution)/shard_map/dot_general | solution.py:376
  229.3 7.1 %fusion.76 = bf16[512,1024]{1,0:T(8,128)(2,1)} fusion(bf16[1024,2304]{1,0:T(8,128)(2,1)} %bitcast.349, bf16[1024,2048]{1,0:T(8,128)(2,1)S(1)} %multiply_convert_fusion), kind=kOutput, calls=%fused_computation.118 | convolution fusion | flops 2148007936 | bytes 7340032 | tf_op jit(solution)/shard_map/dot_general | solution.py:161
  236.3 5.2 %convolution_convert_fusion.2 = bf16[1024,2048]{1,0:T(8,128)(2,1)S(1)} fusion(bf16[1024,2048]{1,0:T(8,128)(2,1)S(1)} %multiply_convert_fusion, bf16[512,1024]{1,0:T(8,128)(2,1)S(1)} %copy-done.55, bf16[512,1024]{1,0:T(8,128)(2,1)S(1)} %copy-done.28), kind=kOutput, calls=%fused_computation.19 | convolution fusion | flops 4301258752 | bytes 10485760 | tf_op jit(solution)/shard_map/dot_general | solution.py:370
  248.7 22.3 %collective-permute-done.31 = bf16[4,2,64,1024]{3,2,0,1:T(8,128)(2,1)} collective-permute-done((bf16[4,2,64,1024]{3,2,0,1:T(8,128)(2,1)}, bf16[4,2,64,1024]{3,2,0,1:T(8,128)(2,1)}, u32[]{:S(2)}, u32[]{:S(2)}) %collective-permute-start.31) | collective-permute-done | bytes 1048608 | tf_op jit(solution)/shard_map/ppermute | solution.py:80
  274.6 6.2 %bitcast_multiply_fusion = (f32[512,1024]{1,0:T(8,128)S(1)}, f32[512,1024]{1,0:T(8,128)}) fusion(f32[8,1024]{1,0:T(8,128)S(1)} %get-tuple-element.82, bf16[512,1024]{1,0:T(8,128)(2,1)} %collective-permute-done.20, bf16[1024,2304]{1,0:T(8,128)(2,1)} %bitcast.350, bf16[1024,2048]{1,0:T(8,128)(2,1)S(1)} %copy-done.30), kind=kOutput, calls=%fused_computation.28 | convolution fusion | flops 2149056512 | bytes 11567104 | tf_op jit(solution)/shard_map/dot_general | solution.py:161
  289.7 7.4 %collective-permute-done.34 = bf16[4,64,1024]{2,1,0:T(8,128)(2,1)S(1)} collective-permute-done((bf16[4,64,1024]{2,1,0:T(8,128)(2,1)S(1)}, bf16[4,64,1024]{2,1,0:T(8,128)(2,1)S(1)}, u32[]{:S(2)}, u32[]{:S(2)}) %collective-permute-start.34) | collective-permute-done | bytes 524320 | tf_op jit(solution)/shard_map/ppermute | solution.py:80
  298.4 3.7 collective-permute-start.35
  302.1 4.3 collective-permute-start.36
  313.8 5.4 %collective-permute-done.35 = bf16[64,2048]{1,0:T(8,128)(2,1)S(1)} collective-permute-done((bf16[64,2048]{1,0:T(8,128)(2,1)}, bf16[64,2048]{1,0:T(8,128)(2,1)S(1)}, u32[]{:S(2)}, u32[]{:S(2)}) %collective-permute-start.35) | collective-permute-done | bytes 262176 | tf_op jit(solution)/shard_map/ppermute | solution.py:80
  319.2 3.9 collective-permute-done.36
  323.1 3.6 collective-permute-done.37
  330.2 2.2 convolution_convert_fusion.4
  332.4 3.5 convolution_convert_fusion.5.grad_ref
  335.9 12.0 %shard_map.163.rest_0_ = bf16[1024,1536]{1,0:T(8,128)(2,1)} custom-call(bf16[1024,1536]{1,0:T(8,128)(2,1)} %convolution_convert_fusion.1.qkv_ref, bf16[1024,128]{1,0:T(8,128)(2,1)} %bitcast.369, bf16[1024,128]{1,0:T(8,128)(2,1)} %bitcast.365, f32[4,2,1024]{2,1,0:T(2,128)} %get-tuple-element.32.log_ref, bf16[1024,512]{1,0:T(8,128)(2,1)} %convolution_convert_fusion.5.grad_ref), custom_call_target="tpu_custom_call" | custom-call | flops 2684354560 | bytes 3670016 | tf_op jit(solution)/shard_map/pallas_call | solution.py:280
  347.8 11.8 %shard_map.164 = bf16[1024,1536]{1,0:T(8,128)(2,1)} custom-call(bf16[1024,1536]{1,0:T(8,128)(2,1)} %convolution_convert_fusion.1.qkv_ref, bf16[1024,128]{1,0:T(8,128)(2,1)} %bitcast.370, bf16[1024,128]{1,0:T(8,128)(2,1)} %bitcast.366, f32[4,2,1024]{2,1,0:T(2,128)} %get-tuple-element.32.log_ref, ...), custom_call_target="tpu_custom_call", output_to_operand_aliasing={{}: (5, {})} | custom-call | flops 2684354560 | bytes 3670016 | tf_op jit(solution)/shard_map/pallas_call | solution.py:280
  359.6 6.1 %convolution_convert_fusion = bf16[1024,1536]{1,0:T(8,128)(2,1)S(1)} fusion(bf16[1024,1024]{1,0:T(8,128)(2,1)} %copy-done.24, bf16[1024,1536]{1,0:T(8,128)(2,1)} %shard_map.164), kind=kOutput, calls=%fused_computation.17 | convolution fusion | flops 3222798336 | bytes 8388608 | tf_op jit(solution)/shard_map/dot_general | solution.py:370
  367.2 10.4 %collective-permute-start.26 = (bf16[4,2,64,1024]{3,2,0,1:T(8,128)(2,1)S(1)}, bf16[4,2,64,1024]{3,2,0,1:T(8,128)(2,1)S(1)}, u32[]{:S(2)}, u32[]{:S(2)}) collective-permute-start(bf16[4,2,64,1024]{3,2,0,1:T(8,128)(2,1)S(1)} %bitcast.373), channel_id=1, source_target_pairs={{0,2},{2,0},{4,6},{6,4},{8,10},{10,8},{12,14},{14,12},{16,18},{18,... | collective-permute-start | bytes 3145736 | tf_op jit(solution)/shard_map/ppermute | solution.py:80
  382.4 2.4 fusion.73
  384.9 39.7 %collective-permute-done.26 = bf16[4,2,64,1024]{3,2,0,1:T(8,128)(2,1)S(1)} collective-permute-done((bf16[4,2,64,1024]{3,2,0,1:T(8,128)(2,1)S(1)}, bf16[4,2,64,1024]{3,2,0,1:T(8,128)(2,1)S(1)}, u32[]{:S(2)}, u32[]{:S(2)}) %collective-permute-start.26) | collective-permute-done | bytes 1048608 | tf_op jit(solution)/shard_map/ppermute | solution.py:80
  433.8 6.9 %fusion.22 = (bf16[1,512,1024]{2,1,0:T(8,128)(2,1)}, bf16[1,512,1024]{2,1,0:T(8,128)(2,1)}, f32[512,1024]{1,0:T(8,128)S(1)}) fusion(bf16[1,512,1024]{2,1,0:T(8,128)(2,1)S(1)} %copy-done, f32[512,1024]{1,0:T(8,128)S(1)} %get-tuple-element.102, f32[512,1024]{1,0:T(8,128)S(1)} %copy-done.5, f32[1,512,1024]{2,1,0:T(8,128)S(1)} %get-tuple-element.96, ...), kind=kOutput, calls=%fused_computation.49 | convolution fusion | flops 2159017984 | bytes 19972096 | tf_op jit(solution)/shard_map/dot_general | solution.py:161
  440.7 2.9 fusion.41
  445.3 3.3 collective-permute-start.40
  450.7 6.6 %collective-permute-done.39 = bf16[16,3072]{1,0:T(8,128)(2,1)S(1)} collective-permute-done((bf16[16,3072]{1,0:T(8,128)(2,1)S(1)}, bf16[16,3072]{1,0:T(8,128)(2,1)S(1)}, u32[]{:S(2)}, u32[]{:S(2)}) %collective-permute-start.39) | collective-permute-done | bytes 98336 | tf_op jit(solution)/shard_map/ppermute | solution.py:80
  458.2 5.9 %collective-permute-done.42 = bf16[4,16,1536]{2,1,0:T(8,128)(2,1)S(1)} collective-permute-done((bf16[4,16,1536]{2,1,0:T(8,128)(2,1)S(1)}, bf16[4,16,1536]{2,1,0:T(8,128)(2,1)S(1)}, u32[]{:S(2)}, u32[]{:S(2)}) %collective-permute-start.42) | collective-permute-done | bytes 196640 | tf_op jit(solution)/shard_map/ppermute | solution.py:80
  468.8 2.5 collective-permute-start.28
  474.5 6.6 %fusion.133 = f32[1024,3072]{1,0:T(8,128)} fusion(bf16[256,1024]{1,0:T(8,128)(2,1)S(1)} %reshape.388, bf16[256,3072]{1,0:T(8,128)(2,1)S(1)} %bitcast.360), kind=kOutput, calls=%fused_computation.294 | convolution fusion | flops 1610612736 | bytes 14680064 | tf_op jit(solution)/shard_map/dot_general | solution.py:370
  482.0 7.0 %collective-permute-done.28 = bf16[64,2048]{1,0:T(8,128)(2,1)S(1)} collective-permute-done((bf16[64,2048]{1,0:T(8,128)(2,1)S(1)}, bf16[64,2048]{1,0:T(8,128)(2,1)S(1)}, u32[]{:S(2)}, u32[]{:S(2)}) %collective-permute-start.28) | collective-permute-done | bytes 262176 | tf_op jit(solution)/shard_map/ppermute | solution.py:80
  489.0 3.2 collective-permute-done.29
  (343 shorter events, 109.2 us)
Async XLA Ops:
  7.2 213.5 %all-gather.2.cloned.1.call-start = ((), (), s32[]{:S(2)}) async-start(), calls=%async_computation.1 | async-start | bytes 4456448 | tf_op jit(solution)/shard_map/all_gather | solution.py:325
  10.3 37.2 %collective-permute-start.4 = (bf16[64,2048]{1,0:T(8,128)(2,1)}, bf16[64,2048]{1,0:T(8,128)(2,1)S(1)}, u32[]{:S(2)}, u32[]{:S(2)}) collective-permute-start(bf16[64,2048]{1,0:T(8,128)(2,1)} %pad_maximum_fusion.9), channel_id=1, source_target_pairs={{0,16},{2,18},{4,20},{6,22},{8,24},{10,26},{12,28},{14,30},{16,0},... | collective-permute-start | bytes 786440 | tf_op jit(solution)/shard_map/ppermute | solution.py:80
  12.9 34.5 %collective-permute-start.3 = (bf16[64,2048]{1,0:T(8,128)(2,1)}, bf16[64,2048]{1,0:T(8,128)(2,1)S(1)}, u32[]{:S(2)}, u32[]{:S(2)}) collective-permute-start(bf16[64,2048]{1,0:T(8,128)(2,1)} %pad_maximum_fusion.9), channel_id=1, source_target_pairs={{0,8},{2,10},{4,12},{6,14},{8,16},{10,18},{12,20},{14,22},{16,24},... | collective-permute-start | bytes 786440 | tf_op jit(solution)/shard_map/ppermute | solution.py:80
  12.9 34.6 %collective-permute-start.5 = (bf16[64,2048]{1,0:T(8,128)(2,1)}, bf16[64,2048]{1,0:T(8,128)(2,1)S(1)}, u32[]{:S(2)}, u32[]{:S(2)}) collective-permute-start(bf16[64,2048]{1,0:T(8,128)(2,1)} %pad_maximum_fusion.9), channel_id=1, source_target_pairs={{0,24},{2,26},{4,28},{6,30},{8,0},{10,2},{12,4},{14,6},{16,8},{18,... | collective-permute-start | bytes 786440 | tf_op jit(solution)/shard_map/ppermute | solution.py:80
  14.9 480.8 %reduce-scatter.2.cloned.1.call-start = ((), (), s32[]{:S(2)}) async-start(), calls=%async_computation.2 | async-start | bytes 4456448 | tf_op jit(solution)/shard_map/reduce_scatter | solution.py:374
  15.0 1.6 collective-permute-start
  20.9 1.4 collective-permute-start.1
  24.1 159.2 %collective-permute-start.19 = (bf16[512,1024]{1,0:T(8,128)(2,1)}, bf16[512,1024]{1,0:T(8,128)(2,1)}, u32[]{:S(2)}, u32[]{:S(2)}) collective-permute-start(bf16[512,1024]{1,0:T(8,128)(2,1)} %fusion.33), channel_id=1, source_target_pairs={{0,1},{1,0},{2,3},{3,2},{4,5},{5,4},{6,7},{7,6},{8,9},{9,8},{10,11... | collective-permute-start | bytes 3145736 | tf_op jit(solution)/shard_map/ppermute | solution.py:145
  25.1 104.4 %collective-permute-start.2 = (bf16[512,1024]{1,0:T(8,128)(2,1)S(1)}, bf16[512,1024]{1,0:T(8,128)(2,1)S(1)}, u32[]{:S(2)}, u32[]{:S(2)}) collective-permute-start(bf16[512,1024]{1,0:T(8,128)(2,1)S(1)} %get-tuple-element.95), channel_id=1, source_target_pairs={{0,1},{1,0},{2,3},{3,2},{4,5},{5,4},{6,7},{7,6},{8,9},{9,8},{10,11... | collective-permute-start | bytes 3145736 | tf_op jit(solution)/shard_map/ppermute | solution.py:145
  47.5 35.9 %collective-permute-start.14 = (bf16[64,2304]{1,0:T(8,128)(2,1)S(1)}, bf16[64,2304]{1,0:T(8,128)(2,1)S(1)}, u32[]{:S(2)}, u32[]{:S(2)}) collective-permute-start(bf16[64,2304]{1,0:T(8,128)(2,1)S(1)} %pad_maximum_fusion.8), channel_id=1, source_target_pairs={{0,24},{2,26},{4,28},{6,30},{8,0},{10,2},{12,4},{14,6},{16,8},{18,... | collective-permute-start | bytes 884744 | tf_op jit(solution)/shard_map/ppermute | solution.py:80
  47.6 34.2 %collective-permute-start.13 = (bf16[64,2304]{1,0:T(8,128)(2,1)S(1)}, bf16[64,2304]{1,0:T(8,128)(2,1)S(1)}, u32[]{:S(2)}, u32[]{:S(2)}) collective-permute-start(bf16[64,2304]{1,0:T(8,128)(2,1)S(1)} %pad_maximum_fusion.8), channel_id=1, source_target_pairs={{0,16},{2,18},{4,20},{6,22},{8,24},{10,26},{12,28},{14,30},{16,0},... | collective-permute-start | bytes 884744 | tf_op jit(solution)/shard_map/ppermute | solution.py:80
  51.4 29.8 %collective-permute-start.12 = (bf16[64,2304]{1,0:T(8,128)(2,1)S(1)}, bf16[64,2304]{1,0:T(8,128)(2,1)S(1)}, u32[]{:S(2)}, u32[]{:S(2)}) collective-permute-start(bf16[64,2304]{1,0:T(8,128)(2,1)S(1)} %pad_maximum_fusion.8), channel_id=1, source_target_pairs={{0,8},{2,10},{4,12},{6,14},{8,16},{10,18},{12,20},{14,22},{16,24},... | collective-permute-start | bytes 884744 | tf_op jit(solution)/shard_map/ppermute | solution.py:80
  81.2 22.9 %collective-permute-start.6 = (bf16[4,64,1024]{2,1,0:T(8,128)(2,1)S(1)}, bf16[4,64,1024]{2,1,0:T(8,128)(2,1)S(1)}, u32[]{:S(2)}, u32[]{:S(2)}) collective-permute-start(bf16[4,64,1024]{2,1,0:T(8,128)(2,1)S(1)} %get-tuple-element.76), channel_id=1, source_target_pairs={{0,2},{2,0},{4,6},{6,4},{8,10},{10,8},{12,14},{14,12},{16,18},{18,... | collective-permute-start | bytes 1572872 | tf_op jit(solution)/shard_map/ppermute | solution.py:80
  81.8 19.8 %collective-permute-start.8 = (bf16[4,64,1024]{2,1,0:T(8,128)(2,1)S(1)}, bf16[4,64,1024]{2,1,0:T(8,128)(2,1)S(1)}, u32[]{:S(2)}, u32[]{:S(2)}) collective-permute-start(bf16[4,64,1024]{2,1,0:T(8,128)(2,1)S(1)} %get-tuple-element.77), channel_id=1, source_target_pairs={{0,4},{2,6},{4,0},{6,2},{8,12},{10,14},{12,8},{14,10},{16,20},{18,... | collective-permute-start | bytes 1572872 | tf_op jit(solution)/shard_map/ppermute | solution.py:80
  85.6 39.8 %collective-permute-start.15 = (bf16[4,64,1152]{2,1,0:T(8,128)(2,1)S(1)}, bf16[4,64,1152]{2,1,0:T(8,128)(2,1)S(1)}, u32[]{:S(2)}, u32[]{:S(2)}) collective-permute-start(bf16[4,64,1152]{2,1,0:T(8,128)(2,1)S(1)} %get-tuple-element.68), channel_id=1, source_target_pairs={{0,2},{2,0},{4,6},{6,4},{8,10},{10,8},{12,14},{14,12},{16,18},{18,... | collective-permute-start | bytes 1769480 | tf_op jit(solution)/shard_map/ppermute | solution.py:80
  101.6 21.4 %collective-permute-start.17 = (bf16[4,64,1152]{2,1,0:T(8,128)(2,1)S(1)}, bf16[4,64,1152]{2,1,0:T(8,128)(2,1)S(1)}, u32[]{:S(2)}, u32[]{:S(2)}) collective-permute-start(bf16[4,64,1152]{2,1,0:T(8,128)(2,1)S(1)} %get-tuple-element.69), channel_id=1, source_target_pairs={{0,4},{2,6},{4,0},{6,2},{8,12},{10,14},{12,8},{14,10},{16,20},{18,... | collective-permute-start | bytes 1769480 | tf_op jit(solution)/shard_map/ppermute | solution.py:80
  104.2 41.9 %collective-permute-start.9 = (bf16[4,2,64,1024]{3,2,1,0:T(8,128)(2,1)S(1)}, bf16[4,2,64,1024]{3,2,1,0:T(8,128)(2,1)S(1)}, u32[]{:S(2)}, u32[]{:S(2)}) collective-permute-start(bf16[4,2,64,1024]{3,2,1,0:T(8,128)(2,1)S(1)} %bitcast_dynamic-update-slice_fusion.15), channel_id=1, source_target_pairs={{0,2},{2,0},{4,6},{6,4},{8,10},{10,8},{12,14},{14,12},{16,18},{18,... | collective-permute-start | bytes 3145736 | tf_op jit(solution)/shard_map/ppermute | solution.py:80
  123.0 26.0 %collective-permute-start.7 = (bf16[4,2,64,1024]{3,2,1,0:T(8,128)(2,1)S(1)}, bf16[4,2,64,1024]{3,2,1,0:T(8,128)(2,1)S(1)}, u32[]{:S(2)}, u32[]{:S(2)}) collective-permute-start(bf16[4,2,64,1024]{3,2,1,0:T(8,128)(2,1)S(1)} %bitcast_dynamic-update-slice_fusion.13), channel_id=1, source_target_pairs={{0,4},{2,6},{4,0},{6,2},{8,12},{10,14},{12,8},{14,10},{16,20},{18,... | collective-permute-start | bytes 3145736 | tf_op jit(solution)/shard_map/ppermute | solution.py:80
  125.4 60.9 %collective-permute-start.18 = (bf16[4,2,64,1152]{3,2,1,0:T(8,128)(2,1)}, bf16[4,2,64,1152]{3,2,1,0:T(8,128)(2,1)}, u32[]{:S(2)}, u32[]{:S(2)}) collective-permute-start(bf16[4,2,64,1152]{3,2,1,0:T(8,128)(2,1)} %bitcast_dynamic-update-slice_fusion.11), channel_id=1, source_target_pairs={{0,2},{2,0},{4,6},{6,4},{8,10},{10,8},{12,14},{14,12},{16,18},{18,... | collective-permute-start | bytes 3538952 | tf_op jit(solution)/shard_map/ppermute | solution.py:80
  129.5 66.3 %collective-permute-start.16 = (bf16[4,2,64,1152]{3,2,1,0:T(8,128)(2,1)}, bf16[4,2,64,1152]{3,2,1,0:T(8,128)(2,1)}, u32[]{:S(2)}, u32[]{:S(2)}) collective-permute-start(bf16[4,2,64,1152]{3,2,1,0:T(8,128)(2,1)} %bitcast_dynamic-update-slice_fusion.9), channel_id=1, source_target_pairs={{0,4},{2,6},{4,0},{6,2},{8,12},{10,14},{12,8},{14,10},{16,20},{18,... | collective-permute-start | bytes 3538952 | tf_op jit(solution)/shard_map/ppermute | solution.py:80
  179.1 8.8 %collective-permute-start.10 = (bf16[512,1024]{1,0:T(8,128)(2,1)S(1)}, bf16[512,1024]{1,0:T(8,128)(2,1)S(1)}, u32[]{:S(2)}, u32[]{:S(2)}) collective-permute-start(bf16[512,1024]{1,0:T(8,128)(2,1)S(1)} %convolution_convert_fusion.6), channel_id=1, source_target_pairs={{0,1},{1,0},{2,3},{3,2},{4,5},{5,4},{6,7},{7,6},{8,9},{9,8},{10,11... | collective-permute-start | bytes 3145736 | tf_op jit(solution)/shard_map/ppermute | solution.py:145
  195.2 5.6 %collective-permute-start.11 = (bf16[512,1024]{1,0:T(8,128)(2,1)S(1)}, bf16[512,1024]{1,0:T(8,128)(2,1)S(1)}, u32[]{:S(2)}, u32[]{:S(2)}) collective-permute-start(bf16[512,1024]{1,0:T(8,128)(2,1)S(1)} %fusion.35), channel_id=1, source_target_pairs={{0,1},{1,0},{2,3},{3,2},{4,5},{5,4},{6,7},{7,6},{8,9},{9,8},{10,11... | collective-permute-start | bytes 3145736 | tf_op jit(solution)/shard_map/ppermute | solution.py:145
  245.7 25.3 %collective-permute-start.31 = (bf16[4,2,64,1024]{3,2,0,1:T(8,128)(2,1)}, bf16[4,2,64,1024]{3,2,0,1:T(8,128)(2,1)}, u32[]{:S(2)}, u32[]{:S(2)}) collective-permute-start(bf16[4,2,64,1024]{3,2,0,1:T(8,128)(2,1)} %get-tuple-element.38), channel_id=1, source_target_pairs={{0,4},{2,6},{4,0},{6,2},{8,12},{10,14},{12,8},{14,10},{16,20},{18,... | collective-permute-start | bytes 3145736 | tf_op jit(solution)/shard_map/ppermute | solution.py:80
  247.2 27.4 %collective-permute-start.20 = (bf16[512,1024]{1,0:T(8,128)(2,1)}, bf16[512,1024]{1,0:T(8,128)(2,1)}, u32[]{:S(2)}, u32[]{:S(2)}) collective-permute-start(bf16[512,1024]{1,0:T(8,128)(2,1)} %fusion.76), channel_id=1, source_target_pairs={{0,1},{1,0},{2,3},{3,2},{4,5},{5,4},{6,7},{7,6},{8,9},{9,8},{10,11... | collective-permute-start | bytes 3145736 | tf_op jit(solution)/shard_map/ppermute | solution.py:145
  247.2 34.0 %collective-permute-start.33 = (bf16[4,2,64,1024]{3,2,0,1:T(8,128)(2,1)}, bf16[4,2,64,1024]{3,2,0,1:T(8,128)(2,1)}, u32[]{:S(2)}, u32[]{:S(2)}) collective-permute-start(bf16[4,2,64,1024]{3,2,0,1:T(8,128)(2,1)} %get-tuple-element.40), channel_id=1, source_target_pairs={{0,2},{2,0},{4,6},{6,4},{8,10},{10,8},{12,14},{14,12},{16,18},{18,... | collective-permute-start | bytes 3145736 | tf_op jit(solution)/shard_map/ppermute | solution.py:80
  273.0 16.5 %collective-permute-start.32 = (bf16[4,64,1024]{2,1,0:T(8,128)(2,1)S(1)}, bf16[4,64,1024]{2,1,0:T(8,128)(2,1)S(1)}, u32[]{:S(2)}, u32[]{:S(2)}) collective-permute-start(bf16[4,64,1024]{2,1,0:T(8,128)(2,1)S(1)} %dynamic-slice_bitcast_fusion.1), channel_id=1, source_target_pairs={{0,2},{2,0},{4,6},{6,4},{8,10},{10,8},{12,14},{14,12},{16,18},{18,... | collective-permute-start | bytes 1572872 | tf_op jit(solution)/shard_map/ppermute | solution.py:80
  284.4 12.7 %collective-permute-start.34 = (bf16[4,64,1024]{2,1,0:T(8,128)(2,1)S(1)}, bf16[4,64,1024]{2,1,0:T(8,128)(2,1)S(1)}, u32[]{:S(2)}, u32[]{:S(2)}) collective-permute-start(bf16[4,64,1024]{2,1,0:T(8,128)(2,1)S(1)} %dynamic-slice_bitcast_fusion), channel_id=1, source_target_pairs={{0,4},{2,6},{4,0},{6,2},{8,12},{10,14},{12,8},{14,10},{16,20},{18,... | collective-permute-start | bytes 1572872 | tf_op jit(solution)/shard_map/ppermute | solution.py:80
  289.5 39.3 %collective-permute-start.21 = (bf16[512,1024]{1,0:T(8,128)(2,1)}, bf16[512,1024]{1,0:T(8,128)(2,1)}, u32[]{:S(2)}, u32[]{:S(2)}) collective-permute-start(bf16[512,1024]{1,0:T(8,128)(2,1)} %get-tuple-element.101), channel_id=1, source_target_pairs={{0,1},{1,0},{2,3},{3,2},{4,5},{5,4},{6,7},{7,6},{8,9},{9,8},{10,11... | collective-permute-start | bytes 3145736 | tf_op jit(solution)/shard_map/ppermute | solution.py:145
  298.4 20.9 %collective-permute-start.35 = (bf16[64,2048]{1,0:T(8,128)(2,1)}, bf16[64,2048]{1,0:T(8,128)(2,1)S(1)}, u32[]{:S(2)}, u32[]{:S(2)}) collective-permute-start(bf16[64,2048]{1,0:T(8,128)(2,1)} %get-tuple-element.70), channel_id=1, source_target_pairs={{0,8},{2,10},{4,12},{6,14},{8,16},{10,18},{12,20},{14,22},{16,24},... | collective-permute-start | bytes 786440 | tf_op jit(solution)/shard_map/ppermute | solution.py:80
  302.1 21.1 %collective-permute-start.36 = (bf16[64,2048]{1,0:T(8,128)(2,1)}, bf16[64,2048]{1,0:T(8,128)(2,1)}, u32[]{:S(2)}, u32[]{:S(2)}) collective-permute-start(bf16[64,2048]{1,0:T(8,128)(2,1)} %get-tuple-element.71), channel_id=1, source_target_pairs={{0,16},{2,18},{4,20},{6,22},{8,24},{10,26},{12,28},{14,30},{16,0},... | collective-permute-start | bytes 786440 | tf_op jit(solution)/shard_map/ppermute | solution.py:80
  306.3 20.4 %collective-permute-start.37 = (bf16[64,2048]{1,0:T(8,128)(2,1)}, bf16[64,2048]{1,0:T(8,128)(2,1)}, u32[]{:S(2)}, u32[]{:S(2)}) collective-permute-start(bf16[64,2048]{1,0:T(8,128)(2,1)} %get-tuple-element.72), channel_id=1, source_target_pairs={{0,24},{2,26},{4,28},{6,30},{8,0},{10,2},{12,4},{14,6},{16,8},{18,... | collective-permute-start | bytes 786440 | tf_op jit(solution)/shard_map/ppermute | solution.py:80
  367.2 57.4 %collective-permute-start.26 = (bf16[4,2,64,1024]{3,2,0,1:T(8,128)(2,1)S(1)}, bf16[4,2,64,1024]{3,2,0,1:T(8,128)(2,1)S(1)}, u32[]{:S(2)}, u32[]{:S(2)}) collective-permute-start(bf16[4,2,64,1024]{3,2,0,1:T(8,128)(2,1)S(1)} %bitcast.373), channel_id=1, source_target_pairs={{0,2},{2,0},{4,6},{6,4},{8,10},{10,8},{12,14},{14,12},{16,18},{18,... | collective-permute-start | bytes 3145736 | tf_op jit(solution)/shard_map/ppermute | solution.py:80
  378.0 48.6 %collective-permute-start.24 = (bf16[4,2,64,1024]{3,2,0,1:T(8,128)(2,1)S(1)}, bf16[4,2,64,1024]{3,2,0,1:T(8,128)(2,1)S(1)}, u32[]{:S(2)}, u32[]{:S(2)}) collective-permute-start(bf16[4,2,64,1024]{3,2,0,1:T(8,128)(2,1)S(1)} %bitcast.372), channel_id=1, source_target_pairs={{0,4},{2,6},{4,0},{6,2},{8,12},{10,14},{12,8},{14,10},{16,20},{18,... | collective-permute-start | bytes 3145736 | tf_op jit(solution)/shard_map/ppermute | solution.py:80
  381.7 47.8 %collective-permute-start.23 = (bf16[512,1024]{1,0:T(8,128)(2,1)S(1)}, bf16[512,1024]{1,0:T(8,128)(2,1)S(1)}, u32[]{:S(2)}, u32[]{:S(2)}) collective-permute-start(bf16[512,1024]{1,0:T(8,128)(2,1)S(1)} %fusion.68), channel_id=1, source_target_pairs={{0,1},{1,0},{2,3},{3,2},{4,5},{5,4},{6,7},{7,6},{8,9},{9,8},{10,11... | collective-permute-start | bytes 3145736 | tf_op jit(solution)/shard_map/ppermute | solution.py:145
  384.8 47.9 %collective-permute-start.22 = (bf16[512,1024]{1,0:T(8,128)(2,1)S(1)}, bf16[512,1024]{1,0:T(8,128)(2,1)S(1)}, u32[]{:S(2)}, u32[]{:S(2)}) collective-permute-start(bf16[512,1024]{1,0:T(8,128)(2,1)S(1)} %fusion.73), channel_id=1, source_target_pairs={{0,1},{1,0},{2,3},{3,2},{4,5},{5,4},{6,7},{7,6},{8,9},{9,8},{10,11... | collective-permute-start | bytes 3145736 | tf_op jit(solution)/shard_map/ppermute | solution.py:145
  426.0 40.2 %collective-permute-start.27 = (bf16[4,64,1024]{2,1,0:T(8,128)(2,1)}, bf16[4,64,1024]{2,1,0:T(8,128)(2,1)}, u32[]{:S(2)}, u32[]{:S(2)}) collective-permute-start(bf16[4,64,1024]{2,1,0:T(8,128)(2,1)} %dynamic-slice_bitcast_fusion.2), channel_id=1, source_target_pairs={{0,4},{2,6},{4,0},{6,2},{8,12},{10,14},{12,8},{14,10},{16,20},{18,... | collective-permute-start | bytes 1572872 | tf_op jit(solution)/shard_map/ppermute | solution.py:80
  427.9 39.6 %collective-permute-start.25 = (bf16[4,64,1024]{2,1,0:T(8,128)(2,1)}, bf16[4,64,1024]{2,1,0:T(8,128)(2,1)}, u32[]{:S(2)}, u32[]{:S(2)}) collective-permute-start(bf16[4,64,1024]{2,1,0:T(8,128)(2,1)} %dynamic-slice_bitcast_fusion.3), channel_id=1, source_target_pairs={{0,2},{2,0},{4,6},{6,4},{8,10},{10,8},{12,14},{14,12},{16,18},{18,... | collective-permute-start | bytes 1572872 | tf_op jit(solution)/shard_map/ppermute | solution.py:80
  443.7 1.5 collective-permute-start.38
  445.2 12.1 %collective-permute-start.41 = (bf16[16,3072]{1,0:T(8,128)(2,1)S(1)}, bf16[16,3072]{1,0:T(8,128)(2,1)S(1)}, u32[]{:S(2)}, u32[]{:S(2)}) collective-permute-start(bf16[16,3072]{1,0:T(8,128)(2,1)S(1)} %constant_dynamic-update-slice_fusion), channel_id=1, source_target_pairs={{0,24},{2,26},{4,28},{6,30},{8,0},{10,2},{12,4},{14,6},{16,8},{18,... | collective-permute-start | bytes 294920 | tf_op jit(solution)/shard_map/ppermute | solution.py:80
  445.3 12.0 %collective-permute-start.40 = (bf16[16,3072]{1,0:T(8,128)(2,1)S(1)}, bf16[16,3072]{1,0:T(8,128)(2,1)S(1)}, u32[]{:S(2)}, u32[]{:S(2)}) collective-permute-start(bf16[16,3072]{1,0:T(8,128)(2,1)S(1)} %constant_dynamic-update-slice_fusion), channel_id=1, source_target_pairs={{0,16},{2,18},{4,20},{6,22},{8,24},{10,26},{12,28},{14,30},{16,0},... | collective-permute-start | bytes 294920 | tf_op jit(solution)/shard_map/ppermute | solution.py:80
  448.6 8.7 %collective-permute-start.39 = (bf16[16,3072]{1,0:T(8,128)(2,1)S(1)}, bf16[16,3072]{1,0:T(8,128)(2,1)S(1)}, u32[]{:S(2)}, u32[]{:S(2)}) collective-permute-start(bf16[16,3072]{1,0:T(8,128)(2,1)S(1)} %constant_dynamic-update-slice_fusion), channel_id=1, source_target_pairs={{0,8},{2,10},{4,12},{6,14},{8,16},{10,18},{12,20},{14,22},{16,24},... | collective-permute-start | bytes 294920 | tf_op jit(solution)/shard_map/ppermute | solution.py:80
  457.4 6.6 %collective-permute-start.42 = (bf16[4,16,1536]{2,1,0:T(8,128)(2,1)S(1)}, bf16[4,16,1536]{2,1,0:T(8,128)(2,1)S(1)}, u32[]{:S(2)}, u32[]{:S(2)}) collective-permute-start(bf16[4,16,1536]{2,1,0:T(8,128)(2,1)S(1)} %get-tuple-element.78), channel_id=1, source_target_pairs={{0,2},{2,0},{4,6},{6,4},{8,10},{10,8},{12,14},{14,12},{16,18},{18,... | collective-permute-start | bytes 589832 | tf_op jit(solution)/shard_map/ppermute | solution.py:80
  457.7 6.6 %collective-permute-start.44 = (bf16[4,16,1536]{2,1,0:T(8,128)(2,1)S(1)}, bf16[4,16,1536]{2,1,0:T(8,128)(2,1)S(1)}, u32[]{:S(2)}, u32[]{:S(2)}) collective-permute-start(bf16[4,16,1536]{2,1,0:T(8,128)(2,1)S(1)} %get-tuple-element.79), channel_id=1, source_target_pairs={{0,4},{2,6},{4,0},{6,2},{8,12},{10,14},{12,8},{14,10},{16,20},{18,... | collective-permute-start | bytes 589832 | tf_op jit(solution)/shard_map/ppermute | solution.py:80
  464.0 10.2 %collective-permute-start.43 = (bf16[4,2,16,1536]{3,2,1,0:T(8,128)(2,1)S(1)}, bf16[4,2,16,1536]{3,2,1,0:T(8,128)(2,1)S(1)}, u32[]{:S(2)}, u32[]{:S(2)}) collective-permute-start(bf16[4,2,16,1536]{3,2,1,0:T(8,128)(2,1)S(1)} %bitcast_dynamic-update-slice_fusion.29), channel_id=1, source_target_pairs={{0,4},{2,6},{4,0},{6,2},{8,12},{10,14},{12,8},{14,10},{16,20},{18,... | collective-permute-start | bytes 1179656 | tf_op jit(solution)/shard_map/ppermute | solution.py:80
  464.3 9.9 %collective-permute-start.45 = (bf16[4,2,16,1536]{3,2,1,0:T(8,128)(2,1)S(1)}, bf16[4,2,16,1536]{3,2,1,0:T(8,128)(2,1)S(1)}, u32[]{:S(2)}, u32[]{:S(2)}) collective-permute-start(bf16[4,2,16,1536]{3,2,1,0:T(8,128)(2,1)S(1)} %bitcast_dynamic-update-slice_fusion.31), channel_id=1, source_target_pairs={{0,2},{2,0},{4,6},{6,4},{8,10},{10,8},{12,14},{14,12},{16,18},{18,... | collective-permute-start | bytes 1179656 | tf_op jit(solution)/shard_map/ppermute | solution.py:80
  468.8 20.2 %collective-permute-start.28 = (bf16[64,2048]{1,0:T(8,128)(2,1)S(1)}, bf16[64,2048]{1,0:T(8,128)(2,1)S(1)}, u32[]{:S(2)}, u32[]{:S(2)}) collective-permute-start(bf16[64,2048]{1,0:T(8,128)(2,1)S(1)} %get-tuple-element.73), channel_id=1, source_target_pairs={{0,8},{2,10},{4,12},{6,14},{8,16},{10,18},{12,20},{14,22},{16,24},... | collective-permute-start | bytes 786440 | tf_op jit(solution)/shard_map/ppermute | solution.py:80
  471.3 20.9 %collective-permute-start.29 = (bf16[64,2048]{1,0:T(8,128)(2,1)S(1)}, bf16[64,2048]{1,0:T(8,128)(2,1)S(1)}, u32[]{:S(2)}, u32[]{:S(2)}) collective-permute-start(bf16[64,2048]{1,0:T(8,128)(2,1)S(1)} %get-tuple-element.74), channel_id=1, source_target_pairs={{0,16},{2,18},{4,20},{6,22},{8,24},{10,26},{12,28},{14,30},{16,0},... | collective-permute-start | bytes 786440 | tf_op jit(solution)/shard_map/ppermute | solution.py:80
  473.0 20.6 %collective-permute-start.30 = (bf16[64,2048]{1,0:T(8,128)(2,1)S(1)}, bf16[64,2048]{1,0:T(8,128)(2,1)S(1)}, u32[]{:S(2)}, u32[]{:S(2)}) collective-permute-start(bf16[64,2048]{1,0:T(8,128)(2,1)S(1)} %get-tuple-element.75), channel_id=1, source_target_pairs={{0,24},{2,26},{4,28},{6,30},{8,0},{10,2},{12,4},{14,6},{16,8},{18,... | collective-permute-start | bytes 786440 | tf_op jit(solution)/shard_map/ppermute | solution.py:80
  (57 other events, 350.1 us)
Sparse Core Ops, SparseCore 0:
  15.1 115.9 all-gather.1
  309.8 117.6 reduce-scatter.1
